TPU v7x, 512 devices: a whole 4x8x8 slice. The times are simulated.
512 devices in a mesh: bulk: 64 (over x, z, core), span: 8 (over y).
Axes of the slice: x: 4, y: 8, z: 8, core: 2. Of those that a mesh axis runs over, the one named last changes fastest.
Arguments:
- snapshots: float32 [1048576, 128], P(('span', 'bulk'))
- jac_blocks: bfloat16 [8192, 4, 128, 128], P(('span', 'bulk'))
- jac_cols: int32 [8192, 4], P(('span', 'bulk')), may hold values from 0 to 8191, as said below
Outputs:
- modes: float32 [1048576, 128], P(('span', 'bulk'))
- factor: float32 [128, 128], replicated
- jac_modes: bfloat16 [1048576, 128], P(('span', 'bulk'))
- reduced: float32 [128, 128], replicated
Inputs may be any that keep to these rules, and one draw needn't show every extreme that they name: jac_cols[r, 0] = r. Every column block lies in the die region of r (aligned runs of 1024 block rows) and within 16 block rows of the shard of 16 block rows that holds r.
All inputs are finite; a program needn't handle non-finite values.
Results may differ from a plain program's by a relative error of at most 0.0029.
The roundings to bfloat16 on the way count: a program that leaves them out, or rounds other values in their place, can miss the bound.
Values may be sent and summed in bfloat16 or wider, within the bound.
A program may use at most 64 MiB of HBM per device.

v0:
```python
import jax
import jax.numpy as jnp
from jax import lax
from jax.sharding import PartitionSpec as P


def with_halo(array, sides, width):
    for axis, dim in sides:
        size, length = (lax.axis_size(axis), array.shape[dim])
        up = [(i, (i + 1) % size) for i in range(size - 1)]
        down = [(j, i) for i, j in up]
        last = lax.slice_in_dim(array, length - width, length, axis=dim)
        initial = lax.slice_in_dim(array, 0, width, axis=dim)
        before = lax.ppermute(last, axis, up)
        after = lax.ppermute(initial, axis, down)
        array = jnp.concatenate([before, array, after], axis=dim)
    return array


def total_gram(partial_value):
    return lax.psum(partial_value, ("bulk", "span"))


def cholesky_step(data, row_count):
    high = lax.Precision.HIGHEST
    width = data.shape[1]
    partial_value = lax.dot_general(
        data, data, (((0,), (0,)), ((), ())), precision=high, preferred_element_type=jnp.float32
    )
    gram = total_gram(partial_value) / row_count
    lower = jnp.linalg.cholesky(gram)
    inverse = lax.linalg.triangular_solve(
        lower, jnp.eye(width, dtype=jnp.float32), left_side=True, lower=True
    )
    result = jnp.dot(data, inverse.T, precision=high, preferred_element_type=jnp.float32)
    return (result, lower)


def shards(snapshots, jac_blocks, jac_cols):
    high = lax.Precision.HIGHEST
    local_rows, width = snapshots.shape
    block_rows = jac_cols.shape[0]
    blk = jac_blocks.shape[2]
    row_count = local_rows * lax.axis_size(("bulk", "span"))
    first, lower1 = cholesky_step(snapshots, row_count)
    modes, lower2 = cholesky_step(first, row_count)
    factor = jnp.dot(lower2.T, lower1.T, precision=high, preferred_element_type=jnp.float32)
    modes_b = modes.astype(jnp.bfloat16)
    shard_start = (
        lax.axis_index("span") * lax.axis_size("bulk") + lax.axis_index("bulk")
    ) * block_rows
    relative = jac_cols - shard_start
    extended = with_halo(modes_b, (("bulk", 0),), local_rows)
    ext_blocks = extended.reshape(3 * block_rows, blk, width)
    picked = jnp.take(ext_blocks, relative + block_rows, axis=0)
    product = jnp.einsum("rnij,rnjk->rik", jac_blocks, picked, preferred_element_type=jnp.float32)
    jac_modes = product.astype(jnp.bfloat16).reshape(local_rows, width)
    partial_value = lax.dot_general(
        modes,
        jac_modes.astype(jnp.float32),
        (((0,), (0,)), ((), ())),
        precision=high,
        preferred_element_type=jnp.float32,
    )
    reduced = lax.psum(partial_value, ("bulk", "span")) / row_count
    return (modes, factor, jac_modes, reduced)


def solution(mesh):
    return jax.shard_map(
        shards,
        mesh=mesh,
        in_specs=(
            P(("span", "bulk"), None),
            P(("span", "bulk"), None, None, None),
            P(("span", "bulk"), None),
        ),
        out_specs=(P(("span", "bulk"), None), P(), P(("span", "bulk"), None), P()),
        check_vma=False,
    )
```

profile of v0, /device:TPU:1, one launch (start us, length us, event | category | flops | bytes accessed | tf_op | source)
XLA Modules:
  0.0 870.4 jit_solution(4245679873390945482)
XLA Ops:
  7.2 4.1 fusion.29
  11.4 266.6 %all-reduce.4.cloned.1.call-done = f32[128,128]{0,1:T(8,128)} async-done(((f32[128,128]{0,1:T(8,128)}), f32[128,128]{0,1:T(8,128)}) %all-reduce.4.cloned.1.call-update) | async-done | bytes 65552 | tf_op jit(solution)/shard_map/psum | solution.py:21
  278.0 0.8 broadcast_multiply_fusion.2
  279.0 0.9 fusion.17
  279.8 11.7 %cholesky.44 = f32[128,128]{1,0:T(8,128)S(1)} custom-call(f32[128,128]{1,0:T(8,128)S(1)} %fusion.17), custom_call_target="Cholesky" | custom-call | tf_op jit(solution)/shard_map/jit(cholesky)/cholesky | solution.py:31
  291.6 0.6 compare_reduce_fusion.1
  292.2 0.6 select_bitcast_fusion.1
  292.8 9.8 %custom-call.6 = f32[1,128,128]{1,2,0:T(8,128)S(1)} custom-call(f32[1,128,128]{2,1,0:T(8,128)S(1)} %select_bitcast_fusion.1), custom_call_target="InvertDiagBlocksLowerTriangular" | custom-call | tf_op jit(solution)/shard_map/triangular_solve/custom-call.0 | solution.py:32
  302.6 0.3 fusion.12
  302.9 2.2 fusion.30
  305.1 1.6 fusion.31
  307.0 250.7 %all-reduce.6.cloned.1.call-done = f32[128,128]{0,1:T(8,128)} async-done(((f32[128,128]{0,1:T(8,128)}), f32[128,128]{0,1:T(8,128)}) %all-reduce.6.cloned.1.call-update) | async-done | bytes 65552 | tf_op jit(solution)/shard_map/psum | solution.py:21
  557.7 0.8 broadcast_multiply_fusion.1
  558.6 0.9 fusion.15
  559.5 11.7 %cholesky.55 = f32[128,128]{1,0:T(8,128)S(1)} custom-call(f32[128,128]{1,0:T(8,128)S(1)} %fusion.15), custom_call_target="Cholesky" | custom-call | tf_op jit(solution)/shard_map/jit(cholesky)/cholesky | solution.py:31
  571.2 0.7 compare_reduce_fusion
  572.0 0.7 select_bitcast_fusion
  572.7 9.8 %custom-call.7 = f32[1,128,128]{1,2,0:T(8,128)S(1)} custom-call(f32[1,128,128]{2,1,0:T(8,128)S(1)} %select_bitcast_fusion), custom_call_target="InvertDiagBlocksLowerTriangular" | custom-call | tf_op jit(solution)/shard_map/triangular_solve/custom-call.0 | solution.py:32
  582.5 0.3 fusion.10
  582.8 2.9 fusion.28
  585.7 1.9 collective-permute-start.1
  587.6 3.6 collective-permute-start
  591.6 4.8 collective-permute-done.1
  596.4 1.3 collective-permute-done
  597.7 2.3 pad_maximum_fusion
  600.0 3.6 gather_fusion
  603.6 2.5 fusion.6
  606.1 1.4 fusion.32
  607.5 2.2 fusion.19
  609.6 252.7 %all-reduce.8.cloned.1.call-done = f32[128,128]{0,1:T(8,128)} async-done(((f32[128,128]{0,1:T(8,128)}), f32[128,128]{0,1:T(8,128)}) %all-reduce.8.cloned.1.call-update) | async-done | bytes 65552 | tf_op jit(solution)/shard_map/psum | solution.py:65
  862.3 0.8 broadcast_multiply_fusion
  863.2 0.7 copy.22
  (23 shorter events, 0.9 us)
Async XLA Ops:
  7.2 596.4 %copy-start = (bf16[16,4,128,128]{3,2,1,0:T(8,128)(2,1)S(1)}, bf16[16,4,128,128]{3,2,1,0:T(8,128)(2,1)}, u32[]{:S(2)}) copy-start(bf16[16,4,128,128]{3,2,1,0:T(8,128)(2,1)} %param.7) | copy-start | bytes 6291460
  7.2 270.8 %all-reduce.4.cloned.1.call-start = ((), (), s32[]{:S(2)}) async-start(), calls=%async_computation | async-start | bytes 131072 | tf_op jit(solution)/shard_map/psum | solution.py:21
  11.4 546.3 %all-reduce.6.cloned.1.call-start = ((), (), s32[]{:S(2)}) async-start(), calls=%async_computation.1 | async-start | bytes 131072 | tf_op jit(solution)/shard_map/psum | solution.py:21
  306.8 284.5 %copy-start.3 = (s32[16,4]{0,1:T(4,128)S(1)}, s32[16,4]{0,1:T(4,128)}, u32[]{:S(2)}) copy-start(s32[16,4]{0,1:T(4,128)} %param.8) | copy-start | bytes 772
  306.8 555.5 %all-reduce.8.cloned.1.call-start = ((), (), s32[]{:S(2)}) async-start(), calls=%async_computation.2 | async-start | bytes 131072 | tf_op jit(solution)/shard_map/psum | solution.py:65
  585.7 10.7 %collective-permute-start.1 = (bf16[2048,128]{1,0:T(8,128)(2,1)}, bf16[2048,128]{1,0:T(8,128)(2,1)S(1)}, u32[]{:S(2)}, u32[]{:S(2)}) collective-permute-start(bf16[2048,128]{1,0:T(8,128)(2,1)} %get-tuple-element.16), channel_id=1, source_target_pairs={{8,0},{16,8},{24,16},{32,24},{40,32},{48,40},{56,48},{64,56},{72,6... | collective-permute-start | bytes 1572872 | tf_op jit(solution)/shard_map/ppermute | solution.py:15
  587.6 10.1 %collective-permute-start = (bf16[2048,128]{1,0:T(8,128)(2,1)}, bf16[2048,128]{1,0:T(8,128)(2,1)S(1)}, u32[]{:S(2)}, u32[]{:S(2)}) collective-permute-start(bf16[2048,128]{1,0:T(8,128)(2,1)} %get-tuple-element.16), channel_id=1, source_target_pairs={{0,8},{8,16},{16,24},{24,32},{32,40},{40,48},{48,56},{56,64},{64,7... | collective-permute-start | bytes 1572872 | tf_op jit(solution)/shard_map/ppermute | solution.py:14
  603.6 2.5 copy-start.1
  606.0 257.9 %copy-start.2 = (bf16[16,128,128]{1,2,0:T(8,128)(2,1)}, bf16[16,128,128]{1,2,0:T(8,128)(2,1)S(1)}, u32[]{:S(2)}) copy-start(bf16[16,128,128]{1,2,0:T(8,128)(2,1)S(1)} %fusion.6) | copy-start | bytes 1572868
Sparse Core Ops, SparseCore 0:
  13.6 264.4 all-reduce.3
  306.9 250.7 all-reduce.5
  607.6 254.6 all-reduce.7
where the time goes:
time: 871 us; the launch traced here: 870 us
  waiting for transfers between devices  776 us (89%)
  other arithmetic  52.3 us (6%)
  matrix products  17.5 us (2%)
  between operations  13.9 us (2%)
    psum x2, waiting for transfers between devices, total_gram(): return lax.psum(partial_value, ('bulk', 'span'))  517 us
    psum x1, waiting for transfers between devices, shards(): reduced = lax.psum(partial_value, ('bulk', 'span')) / row_count  253 us
    another operation x6, other arithmetic, cholesky_step(): lower = jnp.linalg.cholesky(gram)  24.9 us
    another operation x4, other arithmetic, cholesky_step(): lax.linalg.triangular_solve(lower, jnp.eye(width, dtype=jnp.float32), lef...  20.9 us
  transfers between devices with their start and end apart: 5, of which 5 were waited for; matrix products, arithmetic and copies ran while one was open for 0% of the time, Pallas kernels for 0%

commit v1 on v0

--- a/solution.py
+++ b/solution.py
@@ -1,7 +1,13 @@
+import functools
+
 import jax
 import jax.numpy as jnp
 from jax import lax
+from jax.experimental import pallas as pl
+from jax.experimental.pallas import tpu as pltpu
 from jax.sharding import PartitionSpec as P
+
+MESH = pl.DeviceIdType.MESH
 
 
 def with_halo(array, sides, width):
@@ -17,17 +23,99 @@
     return array
 
 
-def total_gram(partial_value):
-    return lax.psum(partial_value, ("bulk", "span"))
+def _groups(nx, nz, ny):
+    b = lax.axis_index("bulk")
+    s = lax.axis_index("span")
+    core = b % 2
+    z = (b // 2) % nz
+    x = b // (2 * nz)
+    return [
+        (2, core, lambda p: (b - core + p, s)),
+        (nx, x, lambda p: ((p * nz + z) * 2 + core, s)),
+        (nz, z, lambda p: ((x * nz + p) * 2 + core, s)),
+        (ny, s, lambda p: (b, p)),
+    ]
 
 
-def cholesky_step(data, row_count):
+def _allreduce_kernel(dims, x_ref, o_ref, slots, send_sem, recv_sem):
+    groups = _groups(*dims)
+    barrier = pltpu.get_barrier_semaphore()
+    peers = 0
+    for n, pos, dev in groups:
+        for d in range(1, n):
+            pl.semaphore_signal(barrier, inc=1, device_id=dev((pos + d) % n), device_id_type=MESH)
+            peers += 1
+    pl.semaphore_wait(barrier, peers)
+
+    offset = 0
+    src = x_ref
+    for n, pos, dev in groups:
+        own = offset + pos
+        if src is not x_ref:
+            slots[own] = src
+        else:
+            slots[own] = x_ref[...]
+        send_from = x_ref if src is x_ref else slots.at[own]
+        copies = []
+        for d in range(1, n):
+            peer = (pos + d) % n
+            copy = pltpu.make_async_remote_copy(
+                src_ref=send_from,
+                dst_ref=slots.at[own],
+                send_sem=send_sem.at[offset + peer],
+                recv_sem=recv_sem.at[own],
+                device_id=dev(peer),
+                device_id_type=MESH,
+            )
+            copy.start()
+            copies.append(copy)
+        for d in range(1, n):
+            j = offset + (pos + d) % n
+            pltpu.make_async_remote_copy(
+                src_ref=slots.at[j],
+                dst_ref=slots.at[j],
+                send_sem=send_sem.at[j],
+                recv_sem=recv_sem.at[j],
+                device_id=dev(0),
+                device_id_type=MESH,
+            ).wait_recv()
+        for copy in copies:
+            copy.wait_send()
+        acc = slots[offset]
+        for k in range(1, n):
+            acc = acc + slots[offset + k]
+        src = acc
+        offset += n
+    o_ref[...] = src
+
+
+def make_allreduce(dims, cid):
+    total = sum((2,) + tuple(dims))
+
+    def allreduce(partial_value):
+        return pl.pallas_call(
+            functools.partial(_allreduce_kernel, dims),
+            out_shape=jax.ShapeDtypeStruct(partial_value.shape, jnp.float32),
+            in_specs=[pl.BlockSpec(memory_space=pltpu.VMEM)],
+            out_specs=pl.BlockSpec(memory_space=pltpu.VMEM),
+            scratch_shapes=[
+                pltpu.VMEM((total,) + partial_value.shape, jnp.float32),
+                pltpu.SemaphoreType.DMA((total,)),
+                pltpu.SemaphoreType.DMA((total,)),
+            ],
+            compiler_params=pltpu.CompilerParams(collective_id=cid, has_side_effects=True),
+        )(partial_value)
+
+    return allreduce
+
+
+def cholesky_step(data, row_count, allreduce):
     high = lax.Precision.HIGHEST
     width = data.shape[1]
     partial_value = lax.dot_general(
         data, data, (((0,), (0,)), ((), ())), precision=high, preferred_element_type=jnp.float32
     )
-    gram = total_gram(partial_value) / row_count
+    gram = allreduce(partial_value) / row_count
     lower = jnp.linalg.cholesky(gram)
     inverse = lax.linalg.triangular_solve(
         lower, jnp.eye(width, dtype=jnp.float32), left_side=True, lower=True
@@ -36,14 +124,14 @@
     return (result, lower)
 
 
-def shards(snapshots, jac_blocks, jac_cols):
+def shards(dims, snapshots, jac_blocks, jac_cols):
     high = lax.Precision.HIGHEST
     local_rows, width = snapshots.shape
     block_rows = jac_cols.shape[0]
     blk = jac_blocks.shape[2]
     row_count = local_rows * lax.axis_size(("bulk", "span"))
-    first, lower1 = cholesky_step(snapshots, row_count)
-    modes, lower2 = cholesky_step(first, row_count)
+    first, lower1 = cholesky_step(snapshots, row_count, make_allreduce(dims, 0))
+    modes, lower2 = cholesky_step(first, row_count, make_allreduce(dims, 1))
     factor = jnp.dot(lower2.T, lower1.T, precision=high, preferred_element_type=jnp.float32)
     modes_b = modes.astype(jnp.bfloat16)
     shard_start = (
@@ -62,13 +150,20 @@
         precision=high,
         preferred_element_type=jnp.float32,
     )
-    reduced = lax.psum(partial_value, ("bulk", "span")) / row_count
+    reduced = make_allreduce(dims, 2)(partial_value) / row_count
     return (modes, factor, jac_modes, reduced)
 
 
+def _torus_dims(mesh):
+    coords = [d.coords for d in mesh.devices.flat]
+    return tuple(len({c[i] for c in coords}) for i in (0, 2, 1))
+
+
 def solution(mesh):
+    nx, nz, ny = _torus_dims(mesh)
+    assert mesh.shape["bulk"] == 2 * nx * nz and mesh.shape["span"] == ny
     return jax.shard_map(
-        shards,
+        functools.partial(shards, (nx, nz, ny)),
         mesh=mesh,
         in_specs=(
             P(("span", "bulk"), None),

time: 871 us -> 219 us (0.25)
  waiting for transfers between devices: 776 us -> 3.93 us
  Pallas kernels: 0 us -> 128 us
  between operations: 13.9 us -> 0.83 us
    psum x3 -> x0, waiting for transfers between devices: 770 us -> none  [the longest x2 517 us: total_gram(): return lax.psum(partial_value, ('bulk', 'span'))]
    pallas_call x0 -> x3, Pallas kernels: none -> 128 us  [allreduce(): pl.pallas_call(functools.partial(_allreduce_kernel, dims), out_shape=jax....]
  transfers between devices with their start and end apart: 5 -> 2, of which waited for: 5 -> 2; matrix products, arithmetic and copies ran while one was open for 0% -> 1% of each run, Pallas kernels for 0% -> 0%
where the time goes in v1:
time: 219 us; the launch traced here: 218 us
  Pallas kernels  128 us (58%)
  other arithmetic  53.1 us (24%)
  matrix products  17.8 us (8%)
  starting transfers between devices  9.9 us (5%)
  local copies, waits for them, and re-layouts  4.21 us (2%)
  waiting for transfers between devices  3.93 us (2%)
    pallas_call x3, Pallas kernels, allreduce(): pl.pallas_call(functools.partial(_allreduce_kernel, dims), out_shape=jax....  128 us
    another operation x6, other arithmetic, cholesky_step(): lower = jnp.linalg.cholesky(gram)  25 us
    another operation x4, other arithmetic, cholesky_step(): lax.linalg.triangular_solve(lower, jnp.eye(width, dtype=jnp.float32), lef...  20.9 us
    ppermute x1, starting transfers between devices, with_halo(): after = lax.ppermute(initial, axis, down)  6.25 us
    dot_general x2, matrix products, cholesky_step(): lax.dot_general(data, data, (((0,), (0,)), ((), ())), precision=high, pre...  5.75 us
    dot_general x2, matrix products, cholesky_step(): jnp.dot(data, inverse.T, precision=high, preferred_element_type=jnp.float32)  5.18 us
  transfers between devices with their start and end apart: 2, of which 2 were waited for; matrix products, arithmetic and copies ran while one was open for 1% of the time, Pallas kernels for 0%

profile of v1, /device:TPU:1, one launch (start us, length us, event | category | flops | bytes accessed | tf_op | source)
XLA Modules:
  0.0 218.2 jit_solution(9113515897541892509)
XLA Ops:
  0.6 4.1 %fusion.29.x_ref = f32[128,128]{1,0:T(8,128)} fusion(f32[2048,128]{1,0:T(8,128)} %param.6), kind=kOutput, calls=%fused_computation.43 | convolution fusion | flops 402653184 | bytes 1114112 | tf_op jit(solution)/shard_map/dot_general | solution.py:115
  4.8 49.4 %shard_map.66 = f32[128,128]{1,0:T(8,128)} custom-call(f32[128,128]{1,0:T(8,128)} %fusion.29.x_ref), custom_call_target="tpu_custom_call" | custom-call | tf_op jit(solution)/shard_map/pallas_call | solution.py:96
  54.1 0.8 broadcast_multiply_fusion.2
  55.1 0.9 fusion.17
  56.0 11.7 %cholesky.44 = f32[128,128]{1,0:T(8,128)S(1)} custom-call(f32[128,128]{1,0:T(8,128)S(1)} %copy.14), custom_call_target="Cholesky" | custom-call | tf_op jit(solution)/shard_map/jit(cholesky)/cholesky | solution.py:119
  67.8 0.7 compare_reduce_fusion.1
  68.5 0.6 select_bitcast_fusion.1
  69.1 9.8 %custom-call.6 = f32[1,128,128]{1,2,0:T(8,128)S(1)} custom-call(f32[1,128,128]{2,1,0:T(8,128)S(1)} %select_bitcast_fusion.1), custom_call_target="InvertDiagBlocksLowerTriangular" | custom-call | tf_op jit(solution)/shard_map/triangular_solve/custom-call.0 | solution.py:120
  78.9 0.3 fusion.12
  79.2 2.2 %fusion.30 = f32[128,2048]{1,0:T(8,128)S(1)} fusion(f32[128,128]{1,0:T(8,128)S(1)} %fusion.12, f32[2048,128]{1,0:T(8,128)} %param.6), kind=kOutput, calls=%fused_computation.44 | convolution fusion | flops 402653184 | bytes 2162688 | tf_op jit(solution)/shard_map/dot_general | solution.py:123
  81.4 1.6 fusion.31.x_ref
  83.1 38.0 %shard_map.67 = f32[128,128]{1,0:T(8,128)} custom-call(f32[128,128]{1,0:T(8,128)} %fusion.31.x_ref), custom_call_target="tpu_custom_call" | custom-call | tf_op jit(solution)/shard_map/pallas_call | solution.py:96
  121.1 0.8 broadcast_multiply_fusion.1
  122.0 0.9 fusion.15
  123.0 11.9 %cholesky.55 = f32[128,128]{1,0:T(8,128)S(1)} custom-call(f32[128,128]{1,0:T(8,128)S(1)} %copy.16), custom_call_target="Cholesky" | custom-call | tf_op jit(solution)/shard_map/jit(cholesky)/cholesky | solution.py:119
  134.9 0.6 compare_reduce_fusion
  135.5 0.7 select_bitcast_fusion
  136.2 9.8 %custom-call.7 = f32[1,128,128]{1,2,0:T(8,128)S(1)} custom-call(f32[1,128,128]{2,1,0:T(8,128)S(1)} %select_bitcast_fusion), custom_call_target="InvertDiagBlocksLowerTriangular" | custom-call | tf_op jit(solution)/shard_map/triangular_solve/custom-call.0 | solution.py:120
  146.0 0.3 fusion.10
  146.3 2.9 %fusion.28 = (bf16[2048,128]{1,0:T(8,128)(2,1)}, f32[2048,128]{1,0:T(8,128)}) fusion(f32[128,2048]{1,0:T(8,128)S(1)} %fusion.30, f32[128,128]{1,0:T(8,128)S(1)} %fusion.10), kind=kOutput, calls=%fused_computation.42 | convolution fusion | flops 402915328 | bytes 2686976 | tf_op jit(solution)/shard_map/dot_general | solution.py:123
  149.2 6.3 %collective-permute-start.1 = (bf16[2048,128]{1,0:T(8,128)(2,1)}, bf16[2048,128]{1,0:T(8,128)(2,1)S(1)}, u32[]{:S(2)}, u32[]{:S(2)}) collective-permute-start(bf16[2048,128]{1,0:T(8,128)(2,1)} %get-tuple-element.8), channel_id=1, source_target_pairs={{8,0},{16,8},{24,16},{32,24},{40,32},{48,40},{56,48},{64,56},{72,6... | collective-permute-start | bytes 1572872 | tf_op jit(solution)/shard_map/ppermute | solution.py:21
  155.5 3.7 %collective-permute-start = (bf16[2048,128]{1,0:T(8,128)(2,1)}, bf16[2048,128]{1,0:T(8,128)(2,1)S(1)}, u32[]{:S(2)}, u32[]{:S(2)}) collective-permute-start(bf16[2048,128]{1,0:T(8,128)(2,1)} %get-tuple-element.8), channel_id=1, source_target_pairs={{0,8},{8,16},{16,24},{24,32},{32,40},{40,48},{48,56},{56,64},{64,7... | collective-permute-start | bytes 1572872 | tf_op jit(solution)/shard_map/ppermute | solution.py:20
  159.4 0.1 copy.17
  159.5 2.2 fusion.19
  161.7 2.6 %collective-permute-done.1 = bf16[2048,128]{1,0:T(8,128)(2,1)S(1)} collective-permute-done((bf16[2048,128]{1,0:T(8,128)(2,1)}, bf16[2048,128]{1,0:T(8,128)(2,1)S(1)}, u32[]{:S(2)}, u32[]{:S(2)}) %collective-permute-start.1) | collective-permute-done | bytes 524320 | tf_op jit(solution)/shard_map/ppermute | solution.py:21
  164.3 1.3 collective-permute-done
  165.6 2.3 %pad_maximum_fusion = bf16[6144,128]{1,0:T(8,128)(2,1)} fusion(bf16[2048,128]{1,0:T(8,128)(2,1)S(1)} %collective-permute-done.1, bf16[2048,128]{1,0:T(8,128)(2,1)} %get-tuple-element.8, bf16[2048,128]{1,0:T(8,128)(2,1)S(1)} %collective-permute-done), kind=kLoop, calls=%fused_computation.4 | loop fusion | flops 4718592 | bytes 3145728 | tf_op jit(solution)/shard_map/concatenate | solution.py:22
  167.9 3.6 %gather_fusion = bf16[64,128,128]{2,1,0:T(8,128)(2,1)} fusion(bf16[48,128,128]{2,1,0:T(8,128)(2,1)} %bitcast.39, s32[1024]{0:T(1024)S(1)} %pad_clamp_fusion), kind=kCustom, calls=%fused_computation | custom fusion | bytes 4194560 | tf_op jit(solution)/shard_map/jit(_take)/gather | solution.py:143
  171.5 2.5 %fusion.6 = bf16[16,128,128]{1,2,0:T(8,128)(2,1)S(1)} fusion(bf16[16,4,128,128]{3,2,1,0:T(8,128)(2,1)S(1)} %copy-done, bf16[16,4,128,128]{3,2,1,0:T(8,128)(2,1)} %bitcast.40, pred[16,4]{1,0:T(8,128)(4,1)S(1)} %copy.17), kind=kOutput, calls=%fused_computation.6 | convolution fusion | flops 269746176 | bytes 4718656 | tf_op jit(solution)/shard_map/rnij,rnjk->rik/dot_general | solution.py:144
  174.0 1.7 fusion.32.x_ref
  175.6 41.1 %shard_map.68 = f32[128,128]{1,0:T(8,128)} custom-call(f32[128,128]{1,0:T(8,128)} %fusion.32.x_ref), custom_call_target="tpu_custom_call" | custom-call | tf_op jit(solution)/shard_map/pallas_call | solution.py:96
  216.8 1.5 broadcast_multiply_fusion
  (18 shorter events, 0.6 us)
Async XLA Ops:
  0.6 170.8 %copy-start = (bf16[16,4,128,128]{3,2,1,0:T(8,128)(2,1)S(1)}, bf16[16,4,128,128]{3,2,1,0:T(8,128)(2,1)}, u32[]{:S(2)}) copy-start(bf16[16,4,128,128]{3,2,1,0:T(8,128)(2,1)} %param.7) | copy-start | bytes 6291460
  83.1 76.1 %copy-start.3 = (s32[16,4]{0,1:T(4,128)S(1)}, s32[16,4]{0,1:T(4,128)}, u32[]{:S(2)}) copy-start(s32[16,4]{0,1:T(4,128)} %param.8) | copy-start | bytes 772
  149.2 15.1 %collective-permute-start.1 = (bf16[2048,128]{1,0:T(8,128)(2,1)}, bf16[2048,128]{1,0:T(8,128)(2,1)S(1)}, u32[]{:S(2)}, u32[]{:S(2)}) collective-permute-start(bf16[2048,128]{1,0:T(8,128)(2,1)} %get-tuple-element.8), channel_id=1, source_target_pairs={{8,0},{16,8},{24,16},{32,24},{40,32},{48,40},{56,48},{64,56},{72,6... | collective-permute-start | bytes 1572872 | tf_op jit(solution)/shard_map/ppermute | solution.py:21
  155.5 10.1 %collective-permute-start = (bf16[2048,128]{1,0:T(8,128)(2,1)}, bf16[2048,128]{1,0:T(8,128)(2,1)S(1)}, u32[]{:S(2)}, u32[]{:S(2)}) collective-permute-start(bf16[2048,128]{1,0:T(8,128)(2,1)} %get-tuple-element.8), channel_id=1, source_target_pairs={{0,8},{8,16},{16,24},{24,32},{32,40},{40,48},{48,56},{56,64},{64,7... | collective-permute-start | bytes 1572872 | tf_op jit(solution)/shard_map/ppermute | solution.py:20
  171.5 2.5 %copy-start.1 = (f32[2048,128]{1,0:T(8,128)S(1)}, f32[2048,128]{1,0:T(8,128)}, u32[]{:S(2)}) copy-start(f32[2048,128]{1,0:T(8,128)} %get-tuple-element.9) | copy-start | bytes 3145732
  173.9 44.3 %copy-start.2 = (bf16[16,128,128]{1,2,0:T(8,128)(2,1)}, bf16[16,128,128]{1,2,0:T(8,128)(2,1)S(1)}, u32[]{:S(2)}) copy-start(bf16[16,128,128]{1,2,0:T(8,128)(2,1)S(1)} %fusion.6) | copy-start | bytes 1572868

commit v2 on v0

--- a/solution.py
+++ b/solution.py
@@ -1,7 +1,13 @@
+import functools
+
 import jax
 import jax.numpy as jnp
 from jax import lax
+from jax.experimental import pallas as pl
+from jax.experimental.pallas import tpu as pltpu
 from jax.sharding import PartitionSpec as P
+
+MESH = pl.DeviceIdType.MESH
 
 
 def with_halo(array, sides, width):
@@ -17,17 +23,149 @@
     return array
 
 
-def total_gram(partial_value):
-    return lax.psum(partial_value, ("bulk", "span"))
-
-
-def cholesky_step(data, row_count):
+def _coords(nx, nz):
+    b = lax.axis_index("bulk")
+    s = lax.axis_index("span")
+    core = b % 2
+    z = (b // 2) % nz
+    x = b // (2 * nz)
+    return b, s, core, x, z
+
+
+def _remote(src, dst, send_sem, recv_sem, device):
+    return pltpu.make_async_remote_copy(
+        src_ref=src, dst_ref=dst, send_sem=send_sem, recv_sem=recv_sem,
+        device_id=device, device_id_type=MESH,
+    )
+
+
+def _allreduce_kernel(dims, x_ref, o_ref, s_core, s_x, s_z, s_y, res, send_sem, recv_sem):
+    nx, nz, ny = dims
+    b, s, core, x, z = _coords(nx, nz)
+    rows = x_ref.shape[0]
+    half = rows // 2
+    chunk = half // nx
+    partner = (b + 1 - 2 * core, s)
+    x_dev = lambda p: ((p * nz + z) * 2 + core, s)
+    z_dev = lambda p: ((x * nz + p) * 2 + core, s)
+    y_dev = lambda p: (b, p)
+    o_core, o_x, o_z, o_y = 0, 2, 2 + nx, 2 + nx + nz
+    o_gx = o_y + ny
+    o_gc = o_gx + nx
+
+    barrier = pltpu.get_barrier_semaphore()
+    peers = [partner]
+    for n, pos, dev in ((nx, x, x_dev), (nz, z, z_dev), (ny, s, y_dev)):
+        peers += [dev((pos + d) % n) for d in range(1, n)]
+    for peer in peers:
+        pl.semaphore_signal(barrier, inc=1, device_id=peer, device_id_type=MESH)
+    pl.semaphore_wait(barrier, len(peers))
+
+    mine = pl.multiple_of(core * half, half)
+    theirs = pl.multiple_of((1 - core) * half, half)
+    c_copy = _remote(x_ref.at[pl.ds(theirs, half)], s_core.at[core],
+                     send_sem.at[o_core], recv_sem.at[o_core + core], partner)
+    c_copy.start()
+    s_core[core] = x_ref[pl.ds(mine, half), :]
+    _remote(s_core.at[1 - core], s_core.at[1 - core], send_sem.at[o_core],
+            recv_sem.at[o_core + 1 - core], partner).wait_recv()
+    c_copy.wait_send()
+    s_core[core] = s_core[0] + s_core[1]
+
+    copies = []
+    for d in range(1, nx):
+        p = (x + d) % nx
+        cp = _remote(s_core.at[core, pl.ds(pl.multiple_of(p * chunk, chunk), chunk)], s_x.at[x],
+                     send_sem.at[o_x + p], recv_sem.at[o_x + x], x_dev(p))
+        cp.start()
+        copies.append(cp)
+    s_x[x] = s_core[core, pl.ds(pl.multiple_of(x * chunk, chunk), chunk), :]
+    for d in range(1, nx):
+        j = (x + d) % nx
+        _remote(s_x.at[j], s_x.at[j], send_sem.at[o_x + j], recv_sem.at[o_x + j], x_dev(j)).wait_recv()
+    for cp in copies:
+        cp.wait_send()
+    acc = s_x[0]
+    for k in range(1, nx):
+        acc = acc + s_x[k]
+
+    for n, pos, dev, slots, off in ((nz, z, z_dev, s_z, o_z), (ny, s, y_dev, s_y, o_y)):
+        slots[pos] = acc
+        copies = []
+        for d in range(1, n):
+            p = (pos + d) % n
+            cp = _remote(slots.at[pos], slots.at[pos], send_sem.at[off + p], recv_sem.at[off + pos], dev(p))
+            cp.start()
+            copies.append(cp)
+        for d in range(1, n):
+            j = (pos + d) % n
+            _remote(slots.at[j], slots.at[j], send_sem.at[off + j], recv_sem.at[off + j], dev(j)).wait_recv()
+        for cp in copies:
+            cp.wait_send()
+        acc = slots[0]
+        for k in range(1, n):
+            acc = acc + slots[k]
+
+    row = lambda p: pl.multiple_of(core * half + p * chunk, chunk)
+    res[pl.ds(row(x), chunk), :] = acc
+    copies = []
+    for d in range(1, nx):
+        p = (x + d) % nx
+        cp = _remote(res.at[pl.ds(row(x), chunk)], res.at[pl.ds(row(x), chunk)],
+                     send_sem.at[o_gx + p], recv_sem.at[o_gx + x], x_dev(p))
+        cp.start()
+        copies.append(cp)
+    for d in range(1, nx):
+        j = (x + d) % nx
+        _remote(res.at[pl.ds(row(j), chunk)], res.at[pl.ds(row(j), chunk)],
+                send_sem.at[o_gx + j], recv_sem.at[o_gx + j], x_dev(j)).wait_recv()
+    for cp in copies:
+        cp.wait_send()
+
+    cp = _remote(res.at[pl.ds(mine, half)], res.at[pl.ds(mine, half)],
+                 send_sem.at[o_gc], recv_sem.at[o_gc + core], partner)
+    cp.start()
+    _remote(res.at[pl.ds(theirs, half)], res.at[pl.ds(theirs, half)],
+            send_sem.at[o_gc], recv_sem.at[o_gc + 1 - core], partner).wait_recv()
+    cp.wait_send()
+    o_ref[...] = res[...]
+
+
+def make_allreduce(dims, cid):
+    nx, nz, ny = dims
+    total = 2 + nx + nz + ny + nx + 2
+
+    def allreduce(partial_value):
+        rows, cols = partial_value.shape
+        half = rows // 2
+        chunk = half // nx
+        return pl.pallas_call(
+            functools.partial(_allreduce_kernel, dims),
+            out_shape=jax.ShapeDtypeStruct(partial_value.shape, jnp.float32),
+            in_specs=[pl.BlockSpec(memory_space=pltpu.VMEM)],
+            out_specs=pl.BlockSpec(memory_space=pltpu.VMEM),
+            scratch_shapes=[
+                pltpu.VMEM((2, half, cols), jnp.float32),
+                pltpu.VMEM((nx, chunk, cols), jnp.float32),
+                pltpu.VMEM((nz, chunk, cols), jnp.float32),
+                pltpu.VMEM((ny, chunk, cols), jnp.float32),
+                pltpu.VMEM((rows, cols), jnp.float32),
+                pltpu.SemaphoreType.DMA((total,)),
+                pltpu.SemaphoreType.DMA((total,)),
+            ],
+            compiler_params=pltpu.CompilerParams(collective_id=cid, has_side_effects=True),
+        )(partial_value)
+
+    return allreduce
+
+
+def cholesky_step(data, row_count, allreduce):
     high = lax.Precision.HIGHEST
     width = data.shape[1]
     partial_value = lax.dot_general(
         data, data, (((0,), (0,)), ((), ())), precision=high, preferred_element_type=jnp.float32
     )
-    gram = total_gram(partial_value) / row_count
+    gram = allreduce(partial_value) / row_count
     lower = jnp.linalg.cholesky(gram)
     inverse = lax.linalg.triangular_solve(
         lower, jnp.eye(width, dtype=jnp.float32), left_side=True, lower=True
@@ -36,14 +174,14 @@
     return (result, lower)
 
 
-def shards(snapshots, jac_blocks, jac_cols):
+def shards(dims, snapshots, jac_blocks, jac_cols):
     high = lax.Precision.HIGHEST
     local_rows, width = snapshots.shape
     block_rows = jac_cols.shape[0]
     blk = jac_blocks.shape[2]
     row_count = local_rows * lax.axis_size(("bulk", "span"))
-    first, lower1 = cholesky_step(snapshots, row_count)
-    modes, lower2 = cholesky_step(first, row_count)
+    first, lower1 = cholesky_step(snapshots, row_count, make_allreduce(dims, 0))
+    modes, lower2 = cholesky_step(first, row_count, make_allreduce(dims, 1))
     factor = jnp.dot(lower2.T, lower1.T, precision=high, preferred_element_type=jnp.float32)
     modes_b = modes.astype(jnp.bfloat16)
     shard_start = (
@@ -62,13 +200,20 @@
         precision=high,
         preferred_element_type=jnp.float32,
     )
-    reduced = lax.psum(partial_value, ("bulk", "span")) / row_count
+    reduced = make_allreduce(dims, 2)(partial_value) / row_count
     return (modes, factor, jac_modes, reduced)
 
 
+def _torus_dims(mesh):
+    coords = [d.coords for d in mesh.devices.flat]
+    return tuple(len({c[i] for c in coords}) for i in (0, 2, 1))
+
+
 def solution(mesh):
+    nx, nz, ny = _torus_dims(mesh)
+    assert mesh.shape["bulk"] == 2 * nx * nz and mesh.shape["span"] == ny
     return jax.shard_map(
-        shards,
+        functools.partial(shards, (nx, nz, ny)),
         mesh=mesh,
         in_specs=(
             P(("span", "bulk"), None),

time: 871 us -> 176 us (0.20)
  waiting for transfers between devices: 776 us -> 3.93 us
  Pallas kernels: 0 us -> 90.1 us
  between operations: 13.9 us -> 0.83 us
    psum x3 -> x0, waiting for transfers between devices: 770 us -> none  [the longest x2 517 us: total_gram(): return lax.psum(partial_value, ('bulk', 'span'))]
    pallas_call x0 -> x3, Pallas kernels: none -> 90.1 us  [allreduce(): pl.pallas_call(functools.partial(_allreduce_kernel, dims), out_shape=jax....]
  transfers between devices with their start and end apart: 5 -> 2, of which waited for: 5 -> 2; matrix products, arithmetic and copies ran while one was open for 0% -> 1% of each run, Pallas kernels for 0% -> 0%
where the time goes in v2:
time: 176 us
  Pallas kernels  90.1 us (51%)
  other arithmetic  53.1 us (30%)
  matrix products  17.8 us (10%)
  starting transfers between devices  5.55 us (3%)
  local copies, waits for them, and re-layouts  4.21 us (2%)
  waiting for transfers between devices  3.93 us (2%)
    pallas_call x3, Pallas kernels, allreduce(): pl.pallas_call(functools.partial(_allreduce_kernel, dims), out_shape=jax....  90.1 us
    another operation x6, other arithmetic, cholesky_step(): lower = jnp.linalg.cholesky(gram)  25 us
    another operation x4, other arithmetic, cholesky_step(): lax.linalg.triangular_solve(lower, jnp.eye(width, dtype=jnp.float32), lef...  20.9 us
    dot_general x2, matrix products, cholesky_step(): lax.dot_general(data, data, (((0,), (0,)), ((), ())), precision=high, pre...  5.75 us
    dot_general x2, matrix products, cholesky_step(): jnp.dot(data, inverse.T, precision=high, preferred_element_type=jnp.float32)  5.18 us
    gather x1, local copies, waits for them, and re-layouts, shards(): picked = jnp.take(ext_blocks, relative + block_rows, axis=0)  3.57 us
  transfers between devices with their start and end apart: 2, of which 2 were waited for; matrix products, arithmetic and copies ran while one was open for 1% of the time, Pallas kernels for 0%

profile of v2, /device:TPU:1, one launch (start us, length us, event | category | flops | bytes accessed | tf_op | source)
XLA Modules:
  0.0 175.5 jit_solution(14074593822495629171)
XLA Ops:
  0.6 4.1 %fusion.29.x_ref = f32[128,128]{1,0:T(8,128)} fusion(f32[2048,128]{1,0:T(8,128)} %param.6), kind=kOutput, calls=%fused_computation.43 | convolution fusion | flops 402653184 | bytes 1114112 | tf_op jit(solution)/shard_map/dot_general | solution.py:165
  4.8 35.5 %shard_map.66 = f32[128,128]{1,0:T(8,128)} custom-call(f32[128,128]{1,0:T(8,128)} %fusion.29.x_ref), custom_call_target="tpu_custom_call" | custom-call | tf_op jit(solution)/shard_map/pallas_call | solution.py:142
  40.3 0.8 broadcast_multiply_fusion.2
  41.3 0.9 fusion.17
  42.2 11.7 %cholesky.44 = f32[128,128]{1,0:T(8,128)S(1)} custom-call(f32[128,128]{1,0:T(8,128)S(1)} %copy.14), custom_call_target="Cholesky" | custom-call | tf_op jit(solution)/shard_map/jit(cholesky)/cholesky | solution.py:169
  54.0 0.7 compare_reduce_fusion.1
  54.6 0.6 select_bitcast_fusion.1
  55.3 9.8 %custom-call.6 = f32[1,128,128]{1,2,0:T(8,128)S(1)} custom-call(f32[1,128,128]{2,1,0:T(8,128)S(1)} %select_bitcast_fusion.1), custom_call_target="InvertDiagBlocksLowerTriangular" | custom-call | tf_op jit(solution)/shard_map/triangular_solve/custom-call.0 | solution.py:170
  65.1 0.3 fusion.12
  65.4 2.2 %fusion.30 = f32[128,2048]{1,0:T(8,128)S(1)} fusion(f32[128,128]{1,0:T(8,128)S(1)} %fusion.12, f32[2048,128]{1,0:T(8,128)} %param.6), kind=kOutput, calls=%fused_computation.44 | convolution fusion | flops 402653184 | bytes 2162688 | tf_op jit(solution)/shard_map/dot_general | solution.py:173
  67.6 1.6 fusion.31.x_ref
  69.2 24.8 %shard_map.67 = f32[128,128]{1,0:T(8,128)} custom-call(f32[128,128]{1,0:T(8,128)} %fusion.31.x_ref), custom_call_target="tpu_custom_call" | custom-call | tf_op jit(solution)/shard_map/pallas_call | solution.py:142
  94.1 0.8 broadcast_multiply_fusion.1
  95.0 0.9 fusion.15
  96.0 11.9 %cholesky.55 = f32[128,128]{1,0:T(8,128)S(1)} custom-call(f32[128,128]{1,0:T(8,128)S(1)} %copy.16), custom_call_target="Cholesky" | custom-call | tf_op jit(solution)/shard_map/jit(cholesky)/cholesky | solution.py:169
  107.9 0.6 compare_reduce_fusion
  108.5 0.7 select_bitcast_fusion
  109.2 9.8 %custom-call.7 = f32[1,128,128]{1,2,0:T(8,128)S(1)} custom-call(f32[1,128,128]{2,1,0:T(8,128)S(1)} %select_bitcast_fusion), custom_call_target="InvertDiagBlocksLowerTriangular" | custom-call | tf_op jit(solution)/shard_map/triangular_solve/custom-call.0 | solution.py:170
  119.0 0.3 fusion.10
  119.3 2.9 %fusion.28 = (bf16[2048,128]{1,0:T(8,128)(2,1)}, f32[2048,128]{1,0:T(8,128)}) fusion(f32[128,2048]{1,0:T(8,128)S(1)} %fusion.30, f32[128,128]{1,0:T(8,128)S(1)} %fusion.10), kind=kOutput, calls=%fused_computation.42 | convolution fusion | flops 402915328 | bytes 2686976 | tf_op jit(solution)/shard_map/dot_general | solution.py:173
  122.3 2.1 %collective-permute-start.1 = (bf16[2048,128]{1,0:T(8,128)(2,1)}, bf16[2048,128]{1,0:T(8,128)(2,1)S(1)}, u32[]{:S(2)}, u32[]{:S(2)}) collective-permute-start(bf16[2048,128]{1,0:T(8,128)(2,1)} %get-tuple-element.8), channel_id=1, source_target_pairs={{8,0},{16,8},{24,16},{32,24},{40,32},{48,40},{56,48},{64,56},{72,6... | collective-permute-start | bytes 1572872 | tf_op jit(solution)/shard_map/ppermute | solution.py:21
  124.3 3.5 %collective-permute-start = (bf16[2048,128]{1,0:T(8,128)(2,1)}, bf16[2048,128]{1,0:T(8,128)(2,1)S(1)}, u32[]{:S(2)}, u32[]{:S(2)}) collective-permute-start(bf16[2048,128]{1,0:T(8,128)(2,1)} %get-tuple-element.8), channel_id=1, source_target_pairs={{0,8},{8,16},{16,24},{24,32},{32,40},{40,48},{48,56},{56,64},{64,7... | collective-permute-start | bytes 1572872 | tf_op jit(solution)/shard_map/ppermute | solution.py:20
  128.0 0.1 copy.17
  128.1 2.2 %fusion.19 = f32[128,128]{1,0:T(8,128)} fusion(f32[128,128]{1,0:T(8,128)S(1)} %cholesky.44, f32[128,128]{1,0:T(8,128)S(1)} %cholesky.55, pred[]{:T(512)} %compare_reduce_fusion, pred[]{:T(512)} %compare_reduce_fusion.1), kind=kOutput, calls=%fused_computation.26 | convolution fusion | flops 25264128 | bytes 196610 | tf_op jit(solution)/shard_map/dot_general | solution.py:185
  130.3 2.6 %collective-permute-done.1 = bf16[2048,128]{1,0:T(8,128)(2,1)S(1)} collective-permute-done((bf16[2048,128]{1,0:T(8,128)(2,1)}, bf16[2048,128]{1,0:T(8,128)(2,1)S(1)}, u32[]{:S(2)}, u32[]{:S(2)}) %collective-permute-start.1) | collective-permute-done | bytes 524320 | tf_op jit(solution)/shard_map/ppermute | solution.py:21
  133.0 1.3 collective-permute-done
  134.2 2.3 %pad_maximum_fusion = bf16[6144,128]{1,0:T(8,128)(2,1)} fusion(bf16[2048,128]{1,0:T(8,128)(2,1)S(1)} %collective-permute-done.1, bf16[2048,128]{1,0:T(8,128)(2,1)} %get-tuple-element.8, bf16[2048,128]{1,0:T(8,128)(2,1)S(1)} %collective-permute-done), kind=kLoop, calls=%fused_computation.4 | loop fusion | flops 4718592 | bytes 3145728 | tf_op jit(solution)/shard_map/concatenate | solution.py:22
  136.5 3.6 %gather_fusion = bf16[64,128,128]{2,1,0:T(8,128)(2,1)} fusion(bf16[48,128,128]{2,1,0:T(8,128)(2,1)} %bitcast.39, s32[1024]{0:T(1024)S(1)} %pad_clamp_fusion), kind=kCustom, calls=%fused_computation | custom fusion | bytes 4194560 | tf_op jit(solution)/shard_map/jit(_take)/gather | solution.py:193
  140.1 2.5 %fusion.6 = bf16[16,128,128]{1,2,0:T(8,128)(2,1)S(1)} fusion(bf16[16,4,128,128]{3,2,1,0:T(8,128)(2,1)S(1)} %copy-done, bf16[16,4,128,128]{3,2,1,0:T(8,128)(2,1)} %bitcast.40, pred[16,4]{1,0:T(8,128)(4,1)S(1)} %copy.17), kind=kOutput, calls=%fused_computation.6 | convolution fusion | flops 269746176 | bytes 4718656 | tf_op jit(solution)/shard_map/rnij,rnjk->rik/dot_general | solution.py:194
  142.6 1.7 fusion.32.x_ref
  144.3 29.8 %shard_map.68 = f32[128,128]{1,0:T(8,128)} custom-call(f32[128,128]{1,0:T(8,128)} %fusion.32.x_ref), custom_call_target="tpu_custom_call" | custom-call | tf_op jit(solution)/shard_map/pallas_call | solution.py:142
  174.1 1.5 broadcast_multiply_fusion
  (18 shorter events, 0.6 us)
Async XLA Ops:
  0.6 139.5 %copy-start = (bf16[16,4,128,128]{3,2,1,0:T(8,128)(2,1)S(1)}, bf16[16,4,128,128]{3,2,1,0:T(8,128)(2,1)}, u32[]{:S(2)}) copy-start(bf16[16,4,128,128]{3,2,1,0:T(8,128)(2,1)} %param.7) | copy-start | bytes 6291460
  69.2 58.6 %copy-start.3 = (s32[16,4]{0,1:T(4,128)S(1)}, s32[16,4]{0,1:T(4,128)}, u32[]{:S(2)}) copy-start(s32[16,4]{0,1:T(4,128)} %param.8) | copy-start | bytes 772
  122.3 10.7 %collective-permute-start.1 = (bf16[2048,128]{1,0:T(8,128)(2,1)}, bf16[2048,128]{1,0:T(8,128)(2,1)S(1)}, u32[]{:S(2)}, u32[]{:S(2)}) collective-permute-start(bf16[2048,128]{1,0:T(8,128)(2,1)} %get-tuple-element.8), channel_id=1, source_target_pairs={{8,0},{16,8},{24,16},{32,24},{40,32},{48,40},{56,48},{64,56},{72,6... | collective-permute-start | bytes 1572872 | tf_op jit(solution)/shard_map/ppermute | solution.py:21
  124.3 9.9 %collective-permute-start = (bf16[2048,128]{1,0:T(8,128)(2,1)}, bf16[2048,128]{1,0:T(8,128)(2,1)S(1)}, u32[]{:S(2)}, u32[]{:S(2)}) collective-permute-start(bf16[2048,128]{1,0:T(8,128)(2,1)} %get-tuple-element.8), channel_id=1, source_target_pairs={{0,8},{8,16},{16,24},{24,32},{32,40},{40,48},{48,56},{56,64},{64,7... | collective-permute-start | bytes 1572872 | tf_op jit(solution)/shard_map/ppermute | solution.py:20
  140.1 2.5 %copy-start.1 = (f32[2048,128]{1,0:T(8,128)S(1)}, f32[2048,128]{1,0:T(8,128)}, u32[]{:S(2)}) copy-start(f32[2048,128]{1,0:T(8,128)} %get-tuple-element.9) | copy-start | bytes 3145732
  142.6 32.9 %copy-start.2 = (bf16[16,128,128]{1,2,0:T(8,128)(2,1)}, bf16[16,128,128]{1,2,0:T(8,128)(2,1)S(1)}, u32[]{:S(2)}) copy-start(bf16[16,128,128]{1,2,0:T(8,128)(2,1)S(1)} %fusion.6) | copy-start | bytes 1572868

commit v3 on v2

--- a/solution.py
+++ b/solution.py
@@ -159,19 +159,51 @@
     return allreduce
 
 
+def _chol_kernel(g_ref, lt_ref, w_ref, a_ref):
+    n = g_ref.shape[0]
+    a_ref[...] = g_ref[...]
+    sub = lax.broadcasted_iota(jnp.int32, (n, n), 0)
+    lane = lax.broadcasted_iota(jnp.int32, (n, n), 1)
+    w_ref[...] = jnp.where(sub == lane, 1.0, 0.0).astype(jnp.float32)
+    lane_row = lax.broadcasted_iota(jnp.int32, (1, n), 1)
+    for k in range(n):
+        row = a_ref[k:k + 1, :]
+        root = jnp.sqrt(row[:, k:k + 1])
+        lrow = jnp.where(lane_row >= k, row / root, 0.0)
+        lt_ref[k:k + 1, :] = lrow
+        wrow = w_ref[k:k + 1, :] / root
+        w_ref[k:k + 1, :] = wrow
+        if k + 1 < n:
+            r1 = (k + 1) // 8 * 8
+            blk = a_ref[r1:, :]
+            idx = lax.broadcasted_iota(jnp.int32, (n - r1, 1), 0) + r1
+            m = jnp.where(idx > k, blk[:, k:k + 1] / root, 0.0)
+            a_ref[r1:, :] = blk - m * lrow
+            w_ref[r1:, :] = w_ref[r1:, :] - m * wrow
+
+def chol_inv(g):
+    n = g.shape[0]
+    return pl.pallas_call(
+        _chol_kernel,
+        out_shape=(jax.ShapeDtypeStruct((n, n), jnp.float32), jax.ShapeDtypeStruct((n, n), jnp.float32)),
+        in_specs=[pl.BlockSpec(memory_space=pltpu.VMEM)],
+        out_specs=(pl.BlockSpec(memory_space=pltpu.VMEM), pl.BlockSpec(memory_space=pltpu.VMEM)),
+        scratch_shapes=[pltpu.VMEM((n, n), jnp.float32)],
+    )(g)
+
+
 def cholesky_step(data, row_count, allreduce):
     high = lax.Precision.HIGHEST
-    width = data.shape[1]
     partial_value = lax.dot_general(
         data, data, (((0,), (0,)), ((), ())), precision=high, preferred_element_type=jnp.float32
     )
     gram = allreduce(partial_value) / row_count
-    lower = jnp.linalg.cholesky(gram)
-    inverse = lax.linalg.triangular_solve(
-        lower, jnp.eye(width, dtype=jnp.float32), left_side=True, lower=True
-    )
-    result = jnp.dot(data, inverse.T, precision=high, preferred_element_type=jnp.float32)
-    return (result, lower)
+    gram = (gram + gram.T) / 2
+    upper, inverse = chol_inv(gram)
+    result = lax.dot_general(
+        data, inverse, (((1,), (1,)), ((), ())), precision=high, preferred_element_type=jnp.float32
+    )
+    return (result, upper)
 
 
 def shards(dims, snapshots, jac_blocks, jac_cols):
@@ -180,9 +212,9 @@
     block_rows = jac_cols.shape[0]
     blk = jac_blocks.shape[2]
     row_count = local_rows * lax.axis_size(("bulk", "span"))
-    first, lower1 = cholesky_step(snapshots, row_count, make_allreduce(dims, 0))
-    modes, lower2 = cholesky_step(first, row_count, make_allreduce(dims, 1))
-    factor = jnp.dot(lower2.T, lower1.T, precision=high, preferred_element_type=jnp.float32)
+    first, upper1 = cholesky_step(snapshots, row_count, make_allreduce(dims, 0))
+    modes, upper2 = cholesky_step(first, row_count, make_allreduce(dims, 1))
+    factor = jnp.dot(upper2, upper1, precision=high, preferred_element_type=jnp.float32)
     modes_b = modes.astype(jnp.bfloat16)
     shard_start = (
         lax.axis_index("span") * lax.axis_size("bulk") + lax.axis_index("bulk")

time: 176 us -> 159 us (0.903)
  other arithmetic: 53.1 us -> 6.78 us
  Pallas kernels: 90.1 us -> 118 us
    another operation x10 -> x0, other arithmetic: 45.9 us -> none  [the longest x6 25 us: cholesky_step(): lower = jnp.linalg.cholesky(gram)]
    pallas_call x0 -> x2, Pallas kernels: none -> 28.1 us  [chol_inv(): pl.pallas_call(_chol_kernel, out_shape=(jax.ShapeDtypeStruct((n, n), jnp....]
where the time goes in v3:
time: 159 us
  Pallas kernels  118 us (74%)
  matrix products  17 us (11%)
  other arithmetic  6.78 us (4%)
  starting transfers between devices  5.55 us (3%)
  waiting for transfers between devices  5.25 us (3%)
  local copies, waits for them, and re-layouts  4.95 us (3%)
    pallas_call x3, Pallas kernels, allreduce(): pl.pallas_call(functools.partial(_allreduce_kernel, dims), out_shape=jax....  90.1 us
    pallas_call x2, Pallas kernels, chol_inv(): pl.pallas_call(_chol_kernel, out_shape=(jax.ShapeDtypeStruct((n, n), jnp....  28.1 us
    dot_general x2, matrix products, cholesky_step(): lax.dot_general(data, inverse, (((1,), (1,)), ((), ())), precision=high,...  6.09 us
    dot_general x2, matrix products, cholesky_step(): lax.dot_general(data, data, (((0,), (0,)), ((), ())), precision=high, pre...  5.89 us
    ppermute x1, waiting for transfers between devices, with_halo(): after = lax.ppermute(initial, axis, down)  3.96 us
    gather x1, local copies, waits for them, and re-layouts, shards(): picked = jnp.take(ext_blocks, relative + block_rows, axis=0)  3.55 us
    ppermute x1, starting transfers between devices, with_halo(): before = lax.ppermute(last, axis, up)  3.49 us
  transfers between devices with their start and end apart: 2, of which 2 were waited for; matrix products, arithmetic and copies ran while one was open for 1% of the time, Pallas kernels for 0%

profile of v3, /device:TPU:1, one launch (start us, length us, event | category | flops | bytes accessed | tf_op | source)
XLA Modules:
  0.0 158.5 jit_solution(3892074377327882480)
XLA Ops:
  0.6 0.0 copy-start
  0.6 4.3 %fusion.14.x_ref = f32[128,128]{1,0:T(8,128)} fusion(f32[2048,128]{1,0:T(8,128)} %param.3), kind=kOutput, calls=%fused_computation.20 | convolution fusion | flops 402653184 | bytes 1114112 | tf_op jit(solution)/shard_map/dot_general | solution.py:197
  4.9 35.5 %shard_map.66 = f32[128,128]{1,0:T(8,128)} custom-call(f32[128,128]{1,0:T(8,128)} %fusion.14.x_ref), custom_call_target="tpu_custom_call" | custom-call | tf_op jit(solution)/shard_map/pallas_call | solution.py:142
  40.5 0.9 copy.13
  41.4 0.1 copy.15
  41.5 0.6 fusion.11.g_ref
  42.2 14.0 %shard_map.67 = (f32[128,128]{1,0:T(8,128)}, f32[128,128]{1,0:T(8,128)}) custom-call(f32[128,128]{1,0:T(8,128)} %fusion.11.g_ref), custom_call_target="tpu_custom_call" | custom-call | tf_op jit(solution)/shard_map/pallas_call | solution.py:186
  56.1 2.3 %fusion.15 = f32[128,2048]{1,0:T(8,128)S(1)} fusion(f32[128,128]{1,0:T(8,128)} %get-tuple-element.8, f32[2048,128]{1,0:T(8,128)} %param.3), kind=kOutput, calls=%fused_computation.21 | convolution fusion | flops 402653184 | bytes 2162688 | tf_op jit(solution)/shard_map/dot_general | solution.py:203
  58.4 1.6 %fusion.16.x_ref = f32[128,128]{1,0:T(8,128)} fusion(f32[128,2048]{1,0:T(8,128)S(1)} %fusion.15), kind=kOutput, calls=%fused_computation.22 | convolution fusion | flops 402653184 | bytes 1114112 | tf_op jit(solution)/shard_map/dot_general | solution.py:197
  60.0 24.8 %shard_map.68 = f32[128,128]{1,0:T(8,128)} custom-call(f32[128,128]{1,0:T(8,128)} %fusion.16.x_ref), custom_call_target="tpu_custom_call" | custom-call | tf_op jit(solution)/shard_map/pallas_call | solution.py:142
  84.9 0.8 broadcast_multiply_fusion.1
  85.7 0.1 copy.16
  85.8 1.5 fusion.10.g_ref
  87.3 14.1 %shard_map.69 = (f32[128,128]{1,0:T(8,128)}, f32[128,128]{1,0:T(8,128)}) custom-call(f32[128,128]{1,0:T(8,128)} %fusion.10.g_ref), custom_call_target="tpu_custom_call" | custom-call | tf_op jit(solution)/shard_map/pallas_call | solution.py:186
  101.4 3.8 %fusion.13 = (bf16[2048,128]{1,0:T(8,128)(2,1)}, f32[2048,128]{1,0:T(8,128)}) fusion(f32[128,2048]{1,0:T(8,128)S(1)} %fusion.15, f32[128,128]{1,0:T(8,128)} %get-tuple-element.9), kind=kOutput, calls=%fused_computation.19 | convolution fusion | flops 402915328 | bytes 2686976 | tf_op jit(solution)/shard_map/dot_general | solution.py:203
  105.3 2.1 %collective-permute-start.1 = (bf16[2048,128]{1,0:T(8,128)(2,1)}, bf16[2048,128]{1,0:T(8,128)(2,1)S(1)}, u32[]{:S(2)}, u32[]{:S(2)}) collective-permute-start(bf16[2048,128]{1,0:T(8,128)(2,1)} %get-tuple-element.14), channel_id=1, source_target_pairs={{8,0},{16,8},{24,16},{32,24},{40,32},{48,40},{56,48},{64,56},{72,6... | collective-permute-start | bytes 1572872 | tf_op jit(solution)/shard_map/ppermute | solution.py:21
  107.3 3.5 %collective-permute-start = (bf16[2048,128]{1,0:T(8,128)(2,1)}, bf16[2048,128]{1,0:T(8,128)(2,1)S(1)}, u32[]{:S(2)}, u32[]{:S(2)}) collective-permute-start(bf16[2048,128]{1,0:T(8,128)(2,1)} %get-tuple-element.14), channel_id=1, source_target_pairs={{0,8},{8,16},{16,24},{24,32},{32,40},{40,48},{48,56},{56,64},{64,7... | collective-permute-start | bytes 1572872 | tf_op jit(solution)/shard_map/ppermute | solution.py:20
  110.9 0.1 copy.18
  110.9 0.1 reshape.23
  111.0 0.1 copy.17
  111.1 0.0 copy-done.3
  111.2 0.0 copy-done.4
  111.2 0.8 fusion.17
  112.0 4.0 %collective-permute-done.1 = bf16[2048,128]{1,0:T(8,128)(2,1)S(1)} collective-permute-done((bf16[2048,128]{1,0:T(8,128)(2,1)}, bf16[2048,128]{1,0:T(8,128)(2,1)S(1)}, u32[]{:S(2)}, u32[]{:S(2)}) %collective-permute-start.1) | collective-permute-done | bytes 524320 | tf_op jit(solution)/shard_map/ppermute | solution.py:21
  116.0 1.3 collective-permute-done
  117.2 2.3 %pad_maximum_fusion = bf16[6144,128]{1,0:T(8,128)(2,1)} fusion(bf16[2048,128]{1,0:T(8,128)(2,1)S(1)} %collective-permute-done.1, bf16[2048,128]{1,0:T(8,128)(2,1)} %get-tuple-element.14, bf16[2048,128]{1,0:T(8,128)(2,1)S(1)} %collective-permute-done), kind=kLoop, calls=%fused_computation.4 | loop fusion | flops 4718592 | bytes 3145728 | tf_op jit(solution)/shard_map/concatenate | solution.py:22
  119.6 3.5 %gather_fusion = bf16[64,128,128]{2,1,0:T(8,128)(2,1)} fusion(bf16[48,128,128]{2,1,0:T(8,128)(2,1)} %bitcast.31, s32[1024]{0:T(1024)S(1)} %pad_clamp_fusion), kind=kCustom, calls=%fused_computation | custom fusion | bytes 4194560 | tf_op jit(solution)/shard_map/jit(_take)/gather | solution.py:225
  123.1 2.5 %fusion.6 = bf16[16,128,128]{1,2,0:T(8,128)(2,1)S(1)} fusion(bf16[16,4,128,128]{3,2,1,0:T(8,128)(2,1)S(1)} %copy-done, bf16[16,4,128,128]{3,2,1,0:T(8,128)(2,1)} %bitcast.32, pred[16,4]{1,0:T(8,128)(4,1)S(1)} %copy.17), kind=kOutput, calls=%fused_computation.6 | convolution fusion | flops 269746176 | bytes 4718656 | tf_op jit(solution)/shard_map/rnij,rnjk->rik/dot_general | solution.py:226
  125.6 0.0 copy-start.2
  125.6 1.7 %fusion.18.x_ref = f32[128,128]{1,0:T(8,128)} fusion(f32[2048,128]{1,0:T(8,128)S(1)} %copy-done.1, bf16[2048,128]{1,0:T(8,128)(2,1)S(1)} %bitcast.33), kind=kOutput, calls=%fused_computation.24 | convolution fusion | flops 402653184 | bytes 1638400 | tf_op jit(solution)/shard_map/dot_general | solution.py:228
  127.3 29.8 %shard_map.70 = f32[128,128]{1,0:T(8,128)} custom-call(f32[128,128]{1,0:T(8,128)} %fusion.18.x_ref), custom_call_target="tpu_custom_call" | custom-call | tf_op jit(solution)/shard_map/pallas_call | solution.py:142
  157.1 1.5 broadcast_multiply_fusion.2
  (11 shorter events, 0.0 us)
Async XLA Ops:
  0.6 122.5 %copy-start = (bf16[16,4,128,128]{3,2,1,0:T(8,128)(2,1)S(1)}, bf16[16,4,128,128]{3,2,1,0:T(8,128)(2,1)}, u32[]{:S(2)}) copy-start(bf16[16,4,128,128]{3,2,1,0:T(8,128)(2,1)} %param.4) | copy-start | bytes 6291460
  60.0 50.8 %copy-start.5 = (s32[16,4]{0,1:T(4,128)S(1)}, s32[16,4]{0,1:T(4,128)}, u32[]{:S(2)}) copy-start(s32[16,4]{0,1:T(4,128)} %param.5) | copy-start | bytes 772
  60.0 51.1 %copy-start.3 = (f32[128,128]{1,0:T(8,128)S(1)}, f32[128,128]{1,0:T(8,128)}, u32[]{:S(2)}) copy-start(f32[128,128]{1,0:T(8,128)} %get-tuple-element.11) | copy-start | bytes 196612
  101.4 9.7 %copy-start.4 = (f32[128,128]{1,0:T(8,128)S(1)}, f32[128,128]{1,0:T(8,128)}, u32[]{:S(2)}) copy-start(f32[128,128]{1,0:T(8,128)} %get-tuple-element.10) | copy-start | bytes 196612
  105.3 10.7 %collective-permute-start.1 = (bf16[2048,128]{1,0:T(8,128)(2,1)}, bf16[2048,128]{1,0:T(8,128)(2,1)S(1)}, u32[]{:S(2)}, u32[]{:S(2)}) collective-permute-start(bf16[2048,128]{1,0:T(8,128)(2,1)} %get-tuple-element.14), channel_id=1, source_target_pairs={{8,0},{16,8},{24,16},{32,24},{40,32},{48,40},{56,48},{64,56},{72,6... | collective-permute-start | bytes 1572872 | tf_op jit(solution)/shard_map/ppermute | solution.py:21
  107.3 9.9 %collective-permute-start = (bf16[2048,128]{1,0:T(8,128)(2,1)}, bf16[2048,128]{1,0:T(8,128)(2,1)S(1)}, u32[]{:S(2)}, u32[]{:S(2)}) collective-permute-start(bf16[2048,128]{1,0:T(8,128)(2,1)} %get-tuple-element.14), channel_id=1, source_target_pairs={{0,8},{8,16},{16,24},{24,32},{32,40},{40,48},{48,56},{56,64},{64,7... | collective-permute-start | bytes 1572872 | tf_op jit(solution)/shard_map/ppermute | solution.py:20
  123.1 2.5 %copy-start.1 = (f32[2048,128]{1,0:T(8,128)S(1)}, f32[2048,128]{1,0:T(8,128)}, u32[]{:S(2)}) copy-start(f32[2048,128]{1,0:T(8,128)} %get-tuple-element.15) | copy-start | bytes 3145732
  125.6 33.0 %copy-start.2 = (bf16[16,128,128]{1,2,0:T(8,128)(2,1)}, bf16[16,128,128]{1,2,0:T(8,128)(2,1)S(1)}, u32[]{:S(2)}) copy-start(bf16[16,128,128]{1,2,0:T(8,128)(2,1)S(1)} %fusion.6) | copy-start | bytes 1572868

commit v4 on v3

--- a/solution.py
+++ b/solution.py
@@ -159,27 +159,36 @@
     return allreduce
 
 
-def _chol_kernel(g_ref, lt_ref, w_ref, a_ref):
+def _chol_kernel(g_ref, lt_ref, w_ref):
     n = g_ref.shape[0]
-    a_ref[...] = g_ref[...]
+    a = g_ref[...]
     sub = lax.broadcasted_iota(jnp.int32, (n, n), 0)
     lane = lax.broadcasted_iota(jnp.int32, (n, n), 1)
-    w_ref[...] = jnp.where(sub == lane, 1.0, 0.0).astype(jnp.float32)
+    w = jnp.where(sub == lane, 1.0, 0.0).astype(jnp.float32)
     lane_row = lax.broadcasted_iota(jnp.int32, (1, n), 1)
+    lt_rows = []
+    w_rows = []
     for k in range(n):
-        row = a_ref[k:k + 1, :]
-        root = jnp.sqrt(row[:, k:k + 1])
-        lrow = jnp.where(lane_row >= k, row / root, 0.0)
-        lt_ref[k:k + 1, :] = lrow
-        wrow = w_ref[k:k + 1, :] / root
-        w_ref[k:k + 1, :] = wrow
+        r0 = k // 8 * 8
+        row = a[k - r0:k - r0 + 1, :]
+        recip = 1.0 / jnp.sqrt(row[:, k:k + 1])
+        lrow = jnp.where(lane_row >= k, row * recip, 0.0)
+        wrow = w[k - r0:k - r0 + 1, :] * recip
+        lt_rows.append(lrow)
+        w_rows.append(wrow)
+        if k % 8 == 7:
+            lt_ref[r0:r0 + 8, :] = jnp.concatenate(lt_rows, axis=0)
+            w_ref[r0:r0 + 8, :] = jnp.concatenate(w_rows, axis=0)
+            lt_rows, w_rows = [], []
         if k + 1 < n:
             r1 = (k + 1) // 8 * 8
-            blk = a_ref[r1:, :]
+            if r1 > r0:
+                a = a[r1 - r0:]
+                w = w[r1 - r0:]
             idx = lax.broadcasted_iota(jnp.int32, (n - r1, 1), 0) + r1
-            m = jnp.where(idx > k, blk[:, k:k + 1] / root, 0.0)
-            a_ref[r1:, :] = blk - m * lrow
-            w_ref[r1:, :] = w_ref[r1:, :] - m * wrow
+            m = jnp.where(idx > k, a[:, k:k + 1] * recip, 0.0)
+            a = a - m * lrow
+            w = w - m * wrow
 
 def chol_inv(g):
     n = g.shape[0]
@@ -188,7 +197,6 @@
         out_shape=(jax.ShapeDtypeStruct((n, n), jnp.float32), jax.ShapeDtypeStruct((n, n), jnp.float32)),
         in_specs=[pl.BlockSpec(memory_space=pltpu.VMEM)],
         out_specs=(pl.BlockSpec(memory_space=pltpu.VMEM), pl.BlockSpec(memory_space=pltpu.VMEM)),
-        scratch_shapes=[pltpu.VMEM((n, n), jnp.float32)],
     )(g)
 
 

time: 159 us -> 159 us (level)
  no operation moved by 1% of the time
where the time goes in v4:
time: 159 us
  Pallas kernels  118 us (74%)
  matrix products  17 us (11%)
  other arithmetic  6.78 us (4%)
  starting transfers between devices  5.55 us (3%)
  waiting for transfers between devices  5.25 us (3%)
  local copies, waits for them, and re-layouts  4.95 us (3%)
    pallas_call x3, Pallas kernels, allreduce(): pl.pallas_call(functools.partial(_allreduce_kernel, dims), out_shape=jax....  90.1 us
    pallas_call x2, Pallas kernels, chol_inv(): pl.pallas_call(_chol_kernel, out_shape=(jax.ShapeDtypeStruct((n, n), jnp....  28.2 us
    dot_general x2, matrix products, cholesky_step(): lax.dot_general(data, inverse, (((1,), (1,)), ((), ())), precision=high,...  6.09 us
    dot_general x2, matrix products, cholesky_step(): lax.dot_general(data, data, (((0,), (0,)), ((), ())), precision=high, pre...  5.89 us
    ppermute x1, waiting for transfers between devices, with_halo(): after = lax.ppermute(initial, axis, down)  3.96 us
    gather x1, local copies, waits for them, and re-layouts, shards(): picked = jnp.take(ext_blocks, relative + block_rows, axis=0)  3.55 us
    ppermute x1, starting transfers between devices, with_halo(): before = lax.ppermute(last, axis, up)  3.49 us
  transfers between devices with their start and end apart: 2, of which 2 were waited for; matrix products, arithmetic and copies ran while one was open for 1% of the time, Pallas kernels for 0%

profile of v4, /device:TPU:1, one launch (start us, length us, event | category | flops | bytes accessed | tf_op | source)
XLA Modules:
  0.0 158.6 jit_solution(14362953409721202543)
XLA Ops:
  0.6 0.0 copy-start
  0.6 4.3 %fusion.14.x_ref = f32[128,128]{1,0:T(8,128)} fusion(f32[2048,128]{1,0:T(8,128)} %param.3), kind=kOutput, calls=%fused_computation.20 | convolution fusion | flops 402653184 | bytes 1114112 | tf_op jit(solution)/shard_map/dot_general | solution.py:205
  4.9 35.5 %shard_map.66 = f32[128,128]{1,0:T(8,128)} custom-call(f32[128,128]{1,0:T(8,128)} %fusion.14.x_ref), custom_call_target="tpu_custom_call" | custom-call | tf_op jit(solution)/shard_map/pallas_call | solution.py:142
  40.5 0.9 copy.13
  41.4 0.1 copy.15
  41.5 0.6 fusion.11.g_ref
  42.2 14.0 %shard_map.67 = (f32[128,128]{1,0:T(8,128)}, f32[128,128]{1,0:T(8,128)}) custom-call(f32[128,128]{1,0:T(8,128)} %fusion.11.g_ref), custom_call_target="tpu_custom_call" | custom-call | tf_op jit(solution)/shard_map/pallas_call | solution.py:195
  56.2 2.3 %fusion.15 = f32[128,2048]{1,0:T(8,128)S(1)} fusion(f32[128,128]{1,0:T(8,128)} %get-tuple-element.8, f32[2048,128]{1,0:T(8,128)} %param.3), kind=kOutput, calls=%fused_computation.21 | convolution fusion | flops 402653184 | bytes 2162688 | tf_op jit(solution)/shard_map/dot_general | solution.py:211
  58.5 1.6 %fusion.16.x_ref = f32[128,128]{1,0:T(8,128)} fusion(f32[128,2048]{1,0:T(8,128)S(1)} %fusion.15), kind=kOutput, calls=%fused_computation.22 | convolution fusion | flops 402653184 | bytes 1114112 | tf_op jit(solution)/shard_map/dot_general | solution.py:205
  60.1 24.8 %shard_map.68 = f32[128,128]{1,0:T(8,128)} custom-call(f32[128,128]{1,0:T(8,128)} %fusion.16.x_ref), custom_call_target="tpu_custom_call" | custom-call | tf_op jit(solution)/shard_map/pallas_call | solution.py:142
  84.9 0.8 broadcast_multiply_fusion.1
  85.8 0.1 copy.16
  85.9 1.5 fusion.10.g_ref
  87.3 14.2 %shard_map.69 = (f32[128,128]{1,0:T(8,128)}, f32[128,128]{1,0:T(8,128)}) custom-call(f32[128,128]{1,0:T(8,128)} %fusion.10.g_ref), custom_call_target="tpu_custom_call" | custom-call | tf_op jit(solution)/shard_map/pallas_call | solution.py:195
  101.5 3.8 %fusion.13 = (bf16[2048,128]{1,0:T(8,128)(2,1)}, f32[2048,128]{1,0:T(8,128)}) fusion(f32[128,2048]{1,0:T(8,128)S(1)} %fusion.15, f32[128,128]{1,0:T(8,128)} %get-tuple-element.9), kind=kOutput, calls=%fused_computation.19 | convolution fusion | flops 402915328 | bytes 2686976 | tf_op jit(solution)/shard_map/dot_general | solution.py:211
  105.4 2.1 %collective-permute-start.1 = (bf16[2048,128]{1,0:T(8,128)(2,1)}, bf16[2048,128]{1,0:T(8,128)(2,1)S(1)}, u32[]{:S(2)}, u32[]{:S(2)}) collective-permute-start(bf16[2048,128]{1,0:T(8,128)(2,1)} %get-tuple-element.14), channel_id=1, source_target_pairs={{8,0},{16,8},{24,16},{32,24},{40,32},{48,40},{56,48},{64,56},{72,6... | collective-permute-start | bytes 1572872 | tf_op jit(solution)/shard_map/ppermute | solution.py:21
  107.4 3.5 %collective-permute-start = (bf16[2048,128]{1,0:T(8,128)(2,1)}, bf16[2048,128]{1,0:T(8,128)(2,1)S(1)}, u32[]{:S(2)}, u32[]{:S(2)}) collective-permute-start(bf16[2048,128]{1,0:T(8,128)(2,1)} %get-tuple-element.14), channel_id=1, source_target_pairs={{0,8},{8,16},{16,24},{24,32},{32,40},{40,48},{48,56},{56,64},{64,7... | collective-permute-start | bytes 1572872 | tf_op jit(solution)/shard_map/ppermute | solution.py:20
  111.0 0.1 copy.18
  111.0 0.1 reshape.23
  111.1 0.1 copy.17
  111.3 0.8 fusion.17
  112.1 4.0 %collective-permute-done.1 = bf16[2048,128]{1,0:T(8,128)(2,1)S(1)} collective-permute-done((bf16[2048,128]{1,0:T(8,128)(2,1)}, bf16[2048,128]{1,0:T(8,128)(2,1)S(1)}, u32[]{:S(2)}, u32[]{:S(2)}) %collective-permute-start.1) | collective-permute-done | bytes 524320 | tf_op jit(solution)/shard_map/ppermute | solution.py:21
  116.1 1.3 collective-permute-done
  117.3 2.3 %pad_maximum_fusion = bf16[6144,128]{1,0:T(8,128)(2,1)} fusion(bf16[2048,128]{1,0:T(8,128)(2,1)S(1)} %collective-permute-done.1, bf16[2048,128]{1,0:T(8,128)(2,1)} %get-tuple-element.14, bf16[2048,128]{1,0:T(8,128)(2,1)S(1)} %collective-permute-done), kind=kLoop, calls=%fused_computation.4 | loop fusion | flops 4718592 | bytes 3145728 | tf_op jit(solution)/shard_map/concatenate | solution.py:22
  119.7 3.5 %gather_fusion = bf16[64,128,128]{2,1,0:T(8,128)(2,1)} fusion(bf16[48,128,128]{2,1,0:T(8,128)(2,1)} %bitcast.31, s32[1024]{0:T(1024)S(1)} %pad_clamp_fusion), kind=kCustom, calls=%fused_computation | custom fusion | bytes 4194560 | tf_op jit(solution)/shard_map/jit(_take)/gather | solution.py:233
  123.2 0.0 copy-done
  123.2 2.5 %fusion.6 = bf16[16,128,128]{1,2,0:T(8,128)(2,1)S(1)} fusion(bf16[16,4,128,128]{3,2,1,0:T(8,128)(2,1)S(1)} %copy-done, bf16[16,4,128,128]{3,2,1,0:T(8,128)(2,1)} %bitcast.32, pred[16,4]{1,0:T(8,128)(4,1)S(1)} %copy.17), kind=kOutput, calls=%fused_computation.6 | convolution fusion | flops 269746176 | bytes 4718656 | tf_op jit(solution)/shard_map/rnij,rnjk->rik/dot_general | solution.py:234
  125.7 0.0 copy-start.2
  125.7 0.0 copy-done.1
  125.7 1.7 %fusion.18.x_ref = f32[128,128]{1,0:T(8,128)} fusion(f32[2048,128]{1,0:T(8,128)S(1)} %copy-done.1, bf16[2048,128]{1,0:T(8,128)(2,1)S(1)} %bitcast.33), kind=kOutput, calls=%fused_computation.24 | convolution fusion | flops 402653184 | bytes 1638400 | tf_op jit(solution)/shard_map/dot_general | solution.py:236
  127.4 29.8 %shard_map.70 = f32[128,128]{1,0:T(8,128)} custom-call(f32[128,128]{1,0:T(8,128)} %fusion.18.x_ref), custom_call_target="tpu_custom_call" | custom-call | tf_op jit(solution)/shard_map/pallas_call | solution.py:142
  157.2 1.5 broadcast_multiply_fusion.2
  (11 shorter events, 0.0 us)
Async XLA Ops:
  0.6 122.6 %copy-start = (bf16[16,4,128,128]{3,2,1,0:T(8,128)(2,1)S(1)}, bf16[16,4,128,128]{3,2,1,0:T(8,128)(2,1)}, u32[]{:S(2)}) copy-start(bf16[16,4,128,128]{3,2,1,0:T(8,128)(2,1)} %param.4) | copy-start | bytes 6291460
  60.1 50.9 %copy-start.5 = (s32[16,4]{0,1:T(4,128)S(1)}, s32[16,4]{0,1:T(4,128)}, u32[]{:S(2)}) copy-start(s32[16,4]{0,1:T(4,128)} %param.5) | copy-start | bytes 772
  60.1 51.2 %copy-start.3 = (f32[128,128]{1,0:T(8,128)S(1)}, f32[128,128]{1,0:T(8,128)}, u32[]{:S(2)}) copy-start(f32[128,128]{1,0:T(8,128)} %get-tuple-element.11) | copy-start | bytes 196612
  101.5 9.7 %copy-start.4 = (f32[128,128]{1,0:T(8,128)S(1)}, f32[128,128]{1,0:T(8,128)}, u32[]{:S(2)}) copy-start(f32[128,128]{1,0:T(8,128)} %get-tuple-element.10) | copy-start | bytes 196612
  105.4 10.7 %collective-permute-start.1 = (bf16[2048,128]{1,0:T(8,128)(2,1)}, bf16[2048,128]{1,0:T(8,128)(2,1)S(1)}, u32[]{:S(2)}, u32[]{:S(2)}) collective-permute-start(bf16[2048,128]{1,0:T(8,128)(2,1)} %get-tuple-element.14), channel_id=1, source_target_pairs={{8,0},{16,8},{24,16},{32,24},{40,32},{48,40},{56,48},{64,56},{72,6... | collective-permute-start | bytes 1572872 | tf_op jit(solution)/shard_map/ppermute | solution.py:21
  107.4 9.9 %collective-permute-start = (bf16[2048,128]{1,0:T(8,128)(2,1)}, bf16[2048,128]{1,0:T(8,128)(2,1)S(1)}, u32[]{:S(2)}, u32[]{:S(2)}) collective-permute-start(bf16[2048,128]{1,0:T(8,128)(2,1)} %get-tuple-element.14), channel_id=1, source_target_pairs={{0,8},{8,16},{16,24},{24,32},{32,40},{40,48},{48,56},{56,64},{64,7... | collective-permute-start | bytes 1572872 | tf_op jit(solution)/shard_map/ppermute | solution.py:20
  123.2 2.5 %copy-start.1 = (f32[2048,128]{1,0:T(8,128)S(1)}, f32[2048,128]{1,0:T(8,128)}, u32[]{:S(2)}) copy-start(f32[2048,128]{1,0:T(8,128)} %get-tuple-element.15) | copy-start | bytes 3145732
  125.7 33.0 %copy-start.2 = (bf16[16,128,128]{1,2,0:T(8,128)(2,1)}, bf16[16,128,128]{1,2,0:T(8,128)(2,1)S(1)}, u32[]{:S(2)}) copy-start(bf16[16,128,128]{1,2,0:T(8,128)(2,1)S(1)} %fusion.6) | copy-start | bytes 1572868

commit v5 on v4

--- a/solution.py
+++ b/solution.py
@@ -8,19 +8,6 @@
 from jax.sharding import PartitionSpec as P
 
 MESH = pl.DeviceIdType.MESH
-
-
-def with_halo(array, sides, width):
-    for axis, dim in sides:
-        size, length = (lax.axis_size(axis), array.shape[dim])
-        up = [(i, (i + 1) % size) for i in range(size - 1)]
-        down = [(j, i) for i, j in up]
-        last = lax.slice_in_dim(array, length - width, length, axis=dim)
-        initial = lax.slice_in_dim(array, 0, width, axis=dim)
-        before = lax.ppermute(last, axis, up)
-        after = lax.ppermute(initial, axis, down)
-        array = jnp.concatenate([before, array, after], axis=dim)
-    return array
 
 
 def _coords(nx, nz):
@@ -200,6 +187,93 @@
     )(g)
 
 
+def _jac_kernel(nbulk, cols_ref, modes_ref, jac_ref, out_ref, ext, send_sem, recv_sem):
+    b = lax.axis_index("bulk")
+    s = lax.axis_index("span")
+    rb = modes_ref.shape[0]
+    has_left = b > 0
+    has_right = b < nbulk - 1
+    barrier = pltpu.get_barrier_semaphore()
+
+    @pl.when(has_left)
+    def _():
+        pl.semaphore_signal(barrier, inc=1, device_id=(b - 1, s), device_id_type=MESH)
+
+    @pl.when(has_right)
+    def _():
+        pl.semaphore_signal(barrier, inc=1, device_id=(b + 1, s), device_id_type=MESH)
+
+    pl.semaphore_wait(barrier, has_left.astype(jnp.int32) + has_right.astype(jnp.int32))
+
+    to_left = pltpu.make_async_remote_copy(
+        src_ref=modes_ref, dst_ref=ext.at[pl.ds(2 * rb, rb)], send_sem=send_sem.at[0],
+        recv_sem=recv_sem.at[1], device_id=(b - 1, s), device_id_type=MESH)
+    to_right = pltpu.make_async_remote_copy(
+        src_ref=modes_ref, dst_ref=ext.at[pl.ds(0, rb)], send_sem=send_sem.at[1],
+        recv_sem=recv_sem.at[0], device_id=(b + 1, s), device_id_type=MESH)
+
+    @pl.when(has_left)
+    def _():
+        to_left.start()
+
+    @pl.when(has_right)
+    def _():
+        to_right.start()
+
+    ext[pl.ds(rb, rb)] = modes_ref[...]
+
+    @pl.when(jnp.logical_not(has_left))
+    def _():
+        ext[pl.ds(0, rb)] = jnp.zeros(modes_ref.shape, modes_ref.dtype)
+
+    @pl.when(jnp.logical_not(has_right))
+    def _():
+        ext[pl.ds(2 * rb, rb)] = jnp.zeros(modes_ref.shape, modes_ref.dtype)
+
+    @pl.when(has_left)
+    def _():
+        to_right.wait_recv()
+        to_left.wait_send()
+
+    @pl.when(has_right)
+    def _():
+        to_left.wait_recv()
+        to_right.wait_send()
+
+    start = (s * nbulk + b) * rb - rb
+
+    def row(r, carry):
+        acc = None
+        for n in range(jac_ref.shape[1]):
+            idx = jnp.clip(cols_ref[r, n] - start, 0, 3 * rb - 1)
+            term = jnp.dot(jac_ref[r, n], ext[idx], preferred_element_type=jnp.float32)
+            acc = term if acc is None else acc + term
+        out_ref[r] = acc.astype(out_ref.dtype)
+        return carry
+
+    lax.fori_loop(0, rb, row, 0)
+
+
+def jac_apply(nbulk, cid, jac_cols, modes_b, jac_blocks):
+    rb, nb, blk, width = jac_blocks.shape[0], jac_blocks.shape[1], jac_blocks.shape[2], modes_b.shape[1]
+    modes_blocks = modes_b.reshape(rb, blk, width)
+    out = pl.pallas_call(
+        functools.partial(_jac_kernel, nbulk),
+        out_shape=jax.ShapeDtypeStruct((rb, blk, width), jnp.bfloat16),
+        in_specs=[pl.BlockSpec(memory_space=pltpu.SMEM),
+                  pl.BlockSpec(memory_space=pltpu.VMEM),
+                  pl.BlockSpec(memory_space=pltpu.VMEM)],
+        out_specs=pl.BlockSpec(memory_space=pltpu.VMEM),
+        scratch_shapes=[
+            pltpu.VMEM((3 * rb, blk, width), jnp.bfloat16),
+            pltpu.SemaphoreType.DMA((2,)),
+            pltpu.SemaphoreType.DMA((2,)),
+        ],
+        compiler_params=pltpu.CompilerParams(collective_id=cid, has_side_effects=True),
+    )(jac_cols, modes_blocks, jac_blocks)
+    return out.reshape(rb * blk, width)
+
+
 def cholesky_step(data, row_count, allreduce):
     high = lax.Precision.HIGHEST
     partial_value = lax.dot_general(
@@ -224,15 +298,7 @@
     modes, upper2 = cholesky_step(first, row_count, make_allreduce(dims, 1))
     factor = jnp.dot(upper2, upper1, precision=high, preferred_element_type=jnp.float32)
     modes_b = modes.astype(jnp.bfloat16)
-    shard_start = (
-        lax.axis_index("span") * lax.axis_size("bulk") + lax.axis_index("bulk")
-    ) * block_rows
-    relative = jac_cols - shard_start
-    extended = with_halo(modes_b, (("bulk", 0),), local_rows)
-    ext_blocks = extended.reshape(3 * block_rows, blk, width)
-    picked = jnp.take(ext_blocks, relative + block_rows, axis=0)
-    product = jnp.einsum("rnij,rnjk->rik", jac_blocks, picked, preferred_element_type=jnp.float32)
-    jac_modes = product.astype(jnp.bfloat16).reshape(local_rows, width)
+    jac_modes = jac_apply(lax.axis_size("bulk"), 3, jac_cols, modes_b, jac_blocks)
     partial_value = lax.dot_general(
         modes,
         jac_modes.astype(jnp.float32),

time: 159 us -> 152 us (0.956)
  Pallas kernels: 118 us -> 129 us
  starting transfers between devices: 5.55 us -> 0 us
  waiting for transfers between devices: 5.25 us -> 0 us
  matrix products: 17 us -> 13.8 us
  other arithmetic: 6.78 us -> 4.46 us
  local copies, waits for them, and re-layouts: 4.95 us -> 3.36 us
    pallas_call x0 -> x1, Pallas kernels: none -> 14.9 us  [jac_apply(): pl.pallas_call(functools.partial(_jac_kernel, nbulk), out_shape=jax.Shape...]
    ppermute x2 -> x0, starting transfers between devices: 5.55 us -> none  [the longest x1 3.49 us: with_halo(): before = lax.ppermute(last, axis, up)]
    ppermute x2 -> x0, waiting for transfers between devices: 5.25 us -> none  [the longest x1 3.96 us: with_halo(): after = lax.ppermute(initial, axis, down)]
    pallas_call x3, Pallas kernels: 90.1 us -> 85.8 us  [allreduce(): pl.pallas_call(functools.partial(_allreduce_kernel, dims), out_shape=jax....]
    gather x1 -> x0, local copies, waits for them, and re-layouts: 3.55 us -> none  [shards(): picked = jnp.take(ext_blocks, relative + block_rows, axis=0)]
    dot_general x1 -> x0, matrix products: 2.47 us -> none  [shards(): jnp.einsum('rnij,rnjk->rik', jac_blocks, picked, preferred_element_type=j...]
    concatenate x1 -> x0, other arithmetic: 2.31 us -> none  [with_halo(): array = jnp.concatenate([before, array, after], axis=dim)]
    unnamed x12 -> x10, local copies, waits for them, and re-layouts: 0.03 us -> 2.25 us
  transfers between devices with their start and end apart: 2 -> 0, of which waited for: 2 -> 0; matrix products, arithmetic and copies ran while one was open for 1% -> 0% of each run, Pallas kernels for 0% -> 0%
where the time goes in v5:
time: 152 us; the launch traced here: 151 us
  Pallas kernels  129 us (85%)
  matrix products  13.8 us (9%)
  other arithmetic  4.46 us (3%)
  local copies, waits for them, and re-layouts  3.36 us (2%)
    pallas_call x3, Pallas kernels, allreduce(): pl.pallas_call(functools.partial(_allreduce_kernel, dims), out_shape=jax....  85.8 us
    pallas_call x2, Pallas kernels, chol_inv(): pl.pallas_call(_chol_kernel, out_shape=(jax.ShapeDtypeStruct((n, n), jnp....  28.2 us
    pallas_call x1, Pallas kernels, jac_apply(): pl.pallas_call(functools.partial(_jac_kernel, nbulk), out_shape=jax.Shape...  14.9 us
    dot_general x2, matrix products, cholesky_step(): lax.dot_general(data, inverse, (((1,), (1,)), ((), ())), precision=high,...  5.33 us
    dot_general x2, matrix products, cholesky_step(): lax.dot_general(data, data, (((0,), (0,)), ((), ())), precision=high, pre...  4.07 us

profile of v5, /device:TPU:1, one launch (start us, length us, event | category | flops | bytes accessed | tf_op | source)
XLA Modules:
  0.0 151.2 jit_solution(17489450307305639695)
XLA Ops:
  0.6 0.0 copy-start
  0.6 1.4 copy.11.cols_ref
  2.1 0.0 copy-done
  2.1 2.5 %fusion.3.x_ref = f32[128,128]{1,0:T(8,128)} fusion(f32[2048,128]{1,0:T(8,128)S(1)} %copy-done), kind=kOutput, calls=%fused_computation.8 | convolution fusion | flops 402653184 | bytes 1114112 | tf_op jit(solution)/shard_map/dot_general | solution.py:279
  4.5 35.5 %shard_map.66 = f32[128,128]{1,0:T(8,128)} custom-call(f32[128,128]{1,0:T(8,128)} %fusion.3.x_ref), custom_call_target="tpu_custom_call" | custom-call | tf_op jit(solution)/shard_map/pallas_call | solution.py:129
  40.1 0.9 copy.7
  41.0 0.1 copy.9
  41.1 0.6 fusion.1.g_ref
  41.8 14.0 %shard_map.67 = (f32[128,128]{1,0:T(8,128)}, f32[128,128]{1,0:T(8,128)}) custom-call(f32[128,128]{1,0:T(8,128)} %fusion.1.g_ref), custom_call_target="tpu_custom_call" | custom-call | tf_op jit(solution)/shard_map/pallas_call | solution.py:182
  55.8 0.0 copy-start.3
  55.8 1.9 %fusion.4 = f32[128,2048]{1,0:T(8,128)S(1)} fusion(f32[128,128]{1,0:T(8,128)} %get-tuple-element.8, f32[2048,128]{1,0:T(8,128)S(1)} %copy-done), kind=kOutput, calls=%fused_computation.9 | convolution fusion | flops 402653184 | bytes 2162688 | tf_op jit(solution)/shard_map/dot_general | solution.py:285
  57.7 1.6 %fusion.5.x_ref = f32[128,128]{1,0:T(8,128)} fusion(f32[128,2048]{1,0:T(8,128)S(1)} %fusion.4), kind=kOutput, calls=%fused_computation.10 | convolution fusion | flops 402653184 | bytes 1114112 | tf_op jit(solution)/shard_map/dot_general | solution.py:279
  59.3 24.7 %shard_map.68 = f32[128,128]{1,0:T(8,128)} custom-call(f32[128,128]{1,0:T(8,128)} %fusion.5.x_ref), custom_call_target="tpu_custom_call" | custom-call | tf_op jit(solution)/shard_map/pallas_call | solution.py:129
  84.1 0.8 broadcast_multiply_fusion.1
  84.9 0.1 copy.10
  85.0 1.5 fusion.g_ref
  86.5 14.2 %shard_map.69 = (f32[128,128]{1,0:T(8,128)}, f32[128,128]{1,0:T(8,128)}) custom-call(f32[128,128]{1,0:T(8,128)} %fusion.g_ref), custom_call_target="tpu_custom_call" | custom-call | tf_op jit(solution)/shard_map/pallas_call | solution.py:182
  100.7 0.0 copy-done.3
  100.7 1.7 %fusion.6 = f32[128,128]{1,0:T(8,128)} fusion(f32[128,128]{1,0:T(8,128)} %get-tuple-element.10, f32[128,128]{1,0:T(8,128)S(1)} %copy-done.3), kind=kOutput, calls=%fused_computation.11 | convolution fusion | flops 25165824 | bytes 196608 | tf_op jit(solution)/shard_map/dot_general | solution.py:299
  102.4 3.4 %fusion.2 = (bf16[2048,128]{1,0:T(8,128)(2,1)}, f32[2048,128]{1,0:T(8,128)S(1)}) fusion(f32[128,2048]{1,0:T(8,128)S(1)} %fusion.4, f32[128,128]{1,0:T(8,128)} %get-tuple-element.9), kind=kOutput, calls=%fused_computation.7 | convolution fusion | flops 402915328 | bytes 2686976 | tf_op jit(solution)/shard_map/dot_general | solution.py:285
  105.8 0.0 copy-start.2
  105.8 14.9 %shard_map.70 = bf16[16,128,128]{2,1,0:T(8,128)(2,1)} custom-call(s32[16,4]{1,0:T(8,128)} %copy.11.cols_ref, bf16[16,128,128]{2,1,0:T(8,128)(2,1)} %bitcast.24, bf16[16,4,128,128]{3,2,1,0:T(8,128)(2,1)} %jac_ref.1), custom_call_target="tpu_custom_call" | custom-call | tf_op jit(solution)/shard_map/pallas_call | solution.py:260
  120.7 0.0 copy-start.1
  120.7 2.7 %fusion.7.x_ref = f32[128,128]{1,0:T(8,128)} fusion(f32[2048,128]{1,0:T(8,128)S(1)} %get-tuple-element.18, bf16[2048,128]{1,0:T(8,128)(2,1)} %bitcast.22), kind=kOutput, calls=%fused_computation.12 | convolution fusion | flops 402653184 | bytes 1638400 | tf_op jit(solution)/shard_map/dot_general | solution.py:302
  123.4 0.0 copy-done.2
  123.4 25.6 %shard_map.71 = f32[128,128]{1,0:T(8,128)} custom-call(f32[128,128]{1,0:T(8,128)} %fusion.7.x_ref), custom_call_target="tpu_custom_call" | custom-call | tf_op jit(solution)/shard_map/pallas_call | solution.py:129
  149.0 1.5 broadcast_multiply_fusion.2
  150.4 0.0 copy-done.1
  150.4 0.8 copy.13
  (1 shorter events, 0.0 us)
Async XLA Ops:
  0.6 1.5 copy-start
  55.8 44.9 %copy-start.3 = (f32[128,128]{1,0:T(8,128)S(1)}, f32[128,128]{1,0:T(8,128)}, u32[]{:S(2)}) copy-start(f32[128,128]{1,0:T(8,128)} %get-tuple-element.11) | copy-start | bytes 196612
  105.8 17.6 %copy-start.2 = (f32[2048,128]{1,0:T(8,128)}, f32[2048,128]{1,0:T(8,128)S(1)}, u32[]{:S(2)}) copy-start(f32[2048,128]{1,0:T(8,128)S(1)} %get-tuple-element.18) | copy-start | bytes 3145732
  120.7 29.8 %copy-start.1 = (bf16[16,128,128]{2,1,0:T(8,128)(2,1)S(1)}, bf16[16,128,128]{2,1,0:T(8,128)(2,1)}, u32[]{:S(2)}) copy-start(bf16[16,128,128]{2,1,0:T(8,128)(2,1)} %shard_map.70) | copy-start | bytes 1572868

commit v6 on v5

--- a/solution.py
+++ b/solution.py
@@ -146,9 +146,10 @@
     return allreduce
 
 
-def _chol_kernel(g_ref, lt_ref, w_ref):
+def _chol_kernel(count, g_ref, lt_ref, w_ref):
     n = g_ref.shape[0]
-    a = g_ref[...]
+    g = g_ref[...] / count
+    a = (g + g.T) / 2
     sub = lax.broadcasted_iota(jnp.int32, (n, n), 0)
     lane = lax.broadcasted_iota(jnp.int32, (n, n), 1)
     w = jnp.where(sub == lane, 1.0, 0.0).astype(jnp.float32)
@@ -158,7 +159,7 @@
     for k in range(n):
         r0 = k // 8 * 8
         row = a[k - r0:k - r0 + 1, :]
-        recip = 1.0 / jnp.sqrt(row[:, k:k + 1])
+        recip = lax.rsqrt(row[:, k:k + 1])
         lrow = jnp.where(lane_row >= k, row * recip, 0.0)
         wrow = w[k - r0:k - r0 + 1, :] * recip
         lt_rows.append(lrow)
@@ -177,10 +178,10 @@
             a = a - m * lrow
             w = w - m * wrow
 
-def chol_inv(g):
+def chol_inv(g, count):
     n = g.shape[0]
     return pl.pallas_call(
-        _chol_kernel,
+        functools.partial(_chol_kernel, float(count)),
         out_shape=(jax.ShapeDtypeStruct((n, n), jnp.float32), jax.ShapeDtypeStruct((n, n), jnp.float32)),
         in_specs=[pl.BlockSpec(memory_space=pltpu.VMEM)],
         out_specs=(pl.BlockSpec(memory_space=pltpu.VMEM), pl.BlockSpec(memory_space=pltpu.VMEM)),
@@ -279,9 +280,7 @@
     partial_value = lax.dot_general(
         data, data, (((0,), (0,)), ((), ())), precision=high, preferred_element_type=jnp.float32
     )
-    gram = allreduce(partial_value) / row_count
-    gram = (gram + gram.T) / 2
-    upper, inverse = chol_inv(gram)
+    upper, inverse = chol_inv(allreduce(partial_value), row_count)
     result = lax.dot_general(
         data, inverse, (((1,), (1,)), ((), ())), precision=high, preferred_element_type=jnp.float32
     )

time: 152 us -> 144 us (0.947)
  Pallas kernels: 129 us -> 125 us
  other arithmetic: 4.46 us -> 1.48 us
    pallas_call x2, Pallas kernels: 28.2 us -> 24.7 us  [chol_inv(): pl.pallas_call(functools.partial(_chol_kernel, float(count)), out_shape=(...]
    div x4 -> x0, other arithmetic: 2.98 us -> none  [the longest x2 2.13 us: cholesky_step(): gram = (gram + gram.T) / 2]
where the time goes in v6:
time: 144 us
  Pallas kernels  125 us (87%)
  matrix products  13.8 us (10%)
  local copies, waits for them, and re-layouts  2.25 us (2%)
  other arithmetic  1.48 us (1%)
    pallas_call x3, Pallas kernels, allreduce(): pl.pallas_call(functools.partial(_allreduce_kernel, dims), out_shape=jax....  85.7 us
    pallas_call x2, Pallas kernels, chol_inv(): pl.pallas_call(functools.partial(_chol_kernel, float(count)), out_shape=(...  24.7 us
    pallas_call x1, Pallas kernels, jac_apply(): pl.pallas_call(functools.partial(_jac_kernel, nbulk), out_shape=jax.Shape...  14.9 us
    dot_general x2, matrix products, cholesky_step(): lax.dot_general(data, inverse, (((1,), (1,)), ((), ())), precision=high,...  5.33 us
    dot_general x2, matrix products, cholesky_step(): lax.dot_general(data, data, (((0,), (0,)), ((), ())), precision=high, pre...  4.07 us

profile of v6, /device:TPU:1, one launch (start us, length us, event | category | flops | bytes accessed | tf_op | source)
XLA Modules:
  0.0 143.5 jit_solution(7458283943017879879)
XLA Ops:
  0.6 0.0 copy-start
  0.6 1.4 %copy.7.cols_ref = s32[16,4]{1,0:T(8,128)} copy(s32[16,4]{0,1:T(4,128)} %param.5) | data formatting | bytes 512 | tf_op args[2]
  2.1 0.0 copy-done
  2.1 2.5 %fusion.1.x_ref = f32[128,128]{1,0:T(8,128)} fusion(f32[2048,128]{1,0:T(8,128)S(1)} %copy-done), kind=kOutput, calls=%fused_computation.2 | convolution fusion | flops 402653184 | bytes 1114112 | tf_op jit(solution)/shard_map/dot_general | solution.py:280
  4.5 35.5 %shard_map.66.g_ref = f32[128,128]{1,0:T(8,128)} custom-call(f32[128,128]{1,0:T(8,128)} %fusion.1.x_ref), custom_call_target="tpu_custom_call" | custom-call | tf_op jit(solution)/shard_map/pallas_call | solution.py:129
  40.1 12.3 %shard_map.67 = (f32[128,128]{1,0:T(8,128)}, f32[128,128]{1,0:T(8,128)}) custom-call(f32[128,128]{1,0:T(8,128)} %shard_map.66.g_ref), custom_call_target="tpu_custom_call" | custom-call | tf_op jit(solution)/shard_map/pallas_call | solution.py:183
  52.4 0.0 copy-start.3
  52.4 1.9 %fusion.2 = f32[128,2048]{1,0:T(8,128)S(1)} fusion(f32[128,128]{1,0:T(8,128)} %get-tuple-element.8, f32[2048,128]{1,0:T(8,128)S(1)} %copy-done), kind=kOutput, calls=%fused_computation.3 | convolution fusion | flops 402653184 | bytes 2162688 | tf_op jit(solution)/shard_map/dot_general | solution.py:284
  54.3 1.6 %fusion.3.x_ref = f32[128,128]{1,0:T(8,128)} fusion(f32[128,2048]{1,0:T(8,128)S(1)} %fusion.2), kind=kOutput, calls=%fused_computation.4 | convolution fusion | flops 402653184 | bytes 1114112 | tf_op jit(solution)/shard_map/dot_general | solution.py:280
  55.9 24.7 %shard_map.68.g_ref = f32[128,128]{1,0:T(8,128)} custom-call(f32[128,128]{1,0:T(8,128)} %fusion.3.x_ref), custom_call_target="tpu_custom_call" | custom-call | tf_op jit(solution)/shard_map/pallas_call | solution.py:129
  80.6 12.4 %shard_map.69 = (f32[128,128]{1,0:T(8,128)}, f32[128,128]{1,0:T(8,128)}) custom-call(f32[128,128]{1,0:T(8,128)} %shard_map.68.g_ref), custom_call_target="tpu_custom_call" | custom-call | tf_op jit(solution)/shard_map/pallas_call | solution.py:183
  93.1 0.0 copy-done.3
  93.1 1.7 %fusion.4 = f32[128,128]{1,0:T(8,128)} fusion(f32[128,128]{1,0:T(8,128)} %get-tuple-element.10, f32[128,128]{1,0:T(8,128)S(1)} %copy-done.3), kind=kOutput, calls=%fused_computation.5 | convolution fusion | flops 25165824 | bytes 196608 | tf_op jit(solution)/shard_map/dot_general | solution.py:298
  94.7 3.4 %fusion = (bf16[2048,128]{1,0:T(8,128)(2,1)}, f32[2048,128]{1,0:T(8,128)S(1)}) fusion(f32[128,2048]{1,0:T(8,128)S(1)} %fusion.2, f32[128,128]{1,0:T(8,128)} %get-tuple-element.9), kind=kOutput, calls=%fused_computation.1 | convolution fusion | flops 402915328 | bytes 2686976 | tf_op jit(solution)/shard_map/dot_general | solution.py:284
  98.2 0.0 copy-start.2
  98.2 14.9 %shard_map.70 = bf16[16,128,128]{2,1,0:T(8,128)(2,1)} custom-call(s32[16,4]{1,0:T(8,128)} %copy.7.cols_ref, bf16[16,128,128]{2,1,0:T(8,128)(2,1)} %bitcast.16, bf16[16,4,128,128]{3,2,1,0:T(8,128)(2,1)} %jac_ref.1), custom_call_target="tpu_custom_call" | custom-call | tf_op jit(solution)/shard_map/pallas_call | solution.py:261
  113.0 0.0 copy-start.1
  113.0 2.7 %fusion.5.x_ref = f32[128,128]{1,0:T(8,128)} fusion(f32[2048,128]{1,0:T(8,128)S(1)} %get-tuple-element.18, bf16[2048,128]{1,0:T(8,128)(2,1)} %bitcast.14), kind=kOutput, calls=%fused_computation.6 | convolution fusion | flops 402653184 | bytes 1638400 | tf_op jit(solution)/shard_map/dot_general | solution.py:301
  115.8 0.0 copy-done.2
  115.8 25.5 %shard_map.71 = f32[128,128]{1,0:T(8,128)} custom-call(f32[128,128]{1,0:T(8,128)} %fusion.5.x_ref), custom_call_target="tpu_custom_call" | custom-call | tf_op jit(solution)/shard_map/pallas_call | solution.py:129
  141.3 1.5 %broadcast_multiply_fusion = f32[128,128]{1,0:T(8,128)} fusion(f32[128,128]{1,0:T(8,128)} %shard_map.71), kind=kLoop, calls=%fused_computation | loop fusion | flops 16384 | bytes 131072 | tf_op jit(solution)/shard_map/div | solution.py:308
  142.7 0.0 copy-done.1
  142.7 0.8 copy.9
Async XLA Ops:
  0.6 1.5 %copy-start = (f32[2048,128]{1,0:T(8,128)S(1)}, f32[2048,128]{1,0:T(8,128)}, u32[]{:S(2)}) copy-start(f32[2048,128]{1,0:T(8,128)} %param.3) | copy-start | bytes 3145732
  52.4 40.7 %copy-start.3 = (f32[128,128]{1,0:T(8,128)S(1)}, f32[128,128]{1,0:T(8,128)}, u32[]{:S(2)}) copy-start(f32[128,128]{1,0:T(8,128)} %get-tuple-element.11) | copy-start | bytes 196612
  98.2 17.6 %copy-start.2 = (f32[2048,128]{1,0:T(8,128)}, f32[2048,128]{1,0:T(8,128)S(1)}, u32[]{:S(2)}) copy-start(f32[2048,128]{1,0:T(8,128)S(1)} %get-tuple-element.18) | copy-start | bytes 3145732
  113.0 29.7 %copy-start.1 = (bf16[16,128,128]{2,1,0:T(8,128)(2,1)S(1)}, bf16[16,128,128]{2,1,0:T(8,128)(2,1)}, u32[]{:S(2)}) copy-start(bf16[16,128,128]{2,1,0:T(8,128)(2,1)} %shard_map.70) | copy-start | bytes 1572868

commit v7 on v6

--- a/solution.py
+++ b/solution.py
@@ -26,7 +26,7 @@
     )
 
 
-def _allreduce_kernel(dims, x_ref, o_ref, s_core, s_x, s_z, s_y, res, send_sem, recv_sem):
+def _allreduce_kernel(dims, scale, x_ref, o_ref, s_core, s_x, s_z, s_y, res, send_sem, recv_sem):
     nx, nz, ny = dims
     b, s, core, x, z = _coords(nx, nz)
     rows = x_ref.shape[0]
@@ -115,10 +115,10 @@
     _remote(res.at[pl.ds(theirs, half)], res.at[pl.ds(theirs, half)],
             send_sem.at[o_gc], recv_sem.at[o_gc + 1 - core], partner).wait_recv()
     cp.wait_send()
-    o_ref[...] = res[...]
-
-
-def make_allreduce(dims, cid):
+    o_ref[...] = res[...] if scale == 1.0 else res[...] * scale
+
+
+def make_allreduce(dims, cid, scale=1.0):
     nx, nz, ny = dims
     total = 2 + nx + nz + ny + nx + 2
 
@@ -127,7 +127,7 @@
         half = rows // 2
         chunk = half // nx
         return pl.pallas_call(
-            functools.partial(_allreduce_kernel, dims),
+            functools.partial(_allreduce_kernel, dims, scale),
             out_shape=jax.ShapeDtypeStruct(partial_value.shape, jnp.float32),
             in_specs=[pl.BlockSpec(memory_space=pltpu.VMEM)],
             out_specs=pl.BlockSpec(memory_space=pltpu.VMEM),
@@ -188,7 +188,9 @@
     )(g)
 
 
-def _jac_kernel(nbulk, cols_ref, modes_ref, jac_ref, out_ref, ext, send_sem, recv_sem):
+def _jac_kernel(nbulk, cols_hbm, modes_ref, jac_ref, out_ref, ext, cols_ref, cols_sem, send_sem, recv_sem):
+    cols_copy = pltpu.make_async_copy(cols_hbm, cols_ref, cols_sem)
+    cols_copy.start()
     b = lax.axis_index("bulk")
     s = lax.axis_index("span")
     rb = modes_ref.shape[0]
@@ -241,12 +243,13 @@
         to_left.wait_recv()
         to_right.wait_send()
 
+    cols_copy.wait()
     start = (s * nbulk + b) * rb - rb
 
     def row(r, carry):
         acc = None
         for n in range(jac_ref.shape[1]):
-            idx = jnp.clip(cols_ref[r, n] - start, 0, 3 * rb - 1)
+            idx = jnp.clip(cols_ref[n, r] - start, 0, 3 * rb - 1)
             term = jnp.dot(jac_ref[r, n], ext[idx], preferred_element_type=jnp.float32)
             acc = term if acc is None else acc + term
         out_ref[r] = acc.astype(out_ref.dtype)
@@ -261,17 +264,19 @@
     out = pl.pallas_call(
         functools.partial(_jac_kernel, nbulk),
         out_shape=jax.ShapeDtypeStruct((rb, blk, width), jnp.bfloat16),
-        in_specs=[pl.BlockSpec(memory_space=pltpu.SMEM),
+        in_specs=[pl.BlockSpec(memory_space=pl.ANY),
                   pl.BlockSpec(memory_space=pltpu.VMEM),
                   pl.BlockSpec(memory_space=pltpu.VMEM)],
         out_specs=pl.BlockSpec(memory_space=pltpu.VMEM),
         scratch_shapes=[
             pltpu.VMEM((3 * rb, blk, width), jnp.bfloat16),
+            pltpu.SMEM(jac_cols.shape[::-1], jnp.int32),
+            pltpu.SemaphoreType.DMA(()),
             pltpu.SemaphoreType.DMA((2,)),
             pltpu.SemaphoreType.DMA((2,)),
         ],
         compiler_params=pltpu.CompilerParams(collective_id=cid, has_side_effects=True),
-    )(jac_cols, modes_blocks, jac_blocks)
+    )(jac_cols.T, modes_blocks, jac_blocks)
     return out.reshape(rb * blk, width)
 
 
@@ -305,7 +310,7 @@
         precision=high,
         preferred_element_type=jnp.float32,
     )
-    reduced = make_allreduce(dims, 2)(partial_value) / row_count
+    reduced = make_allreduce(dims, 2, 1.0 / row_count)(partial_value)
     return (modes, factor, jac_modes, reduced)
 
 

time: 144 us -> 144 us (level)
  other arithmetic: 1.48 us -> 0 us
    div x1 -> x0, other arithmetic: 1.48 us -> none  [shards(): reduced = make_allreduce(dims, 2)(partial_value) / row_count]
where the time goes in v7:
time: 144 us; the launch traced here: 143 us
  Pallas kernels  125 us (87%)
  matrix products  13.8 us (10%)
  local copies, waits for them, and re-layouts  3.5 us (2%)
    pallas_call x3, Pallas kernels, allreduce(): pl.pallas_call(functools.partial(_allreduce_kernel, dims, scale), out_sha...  85.7 us
    pallas_call x2, Pallas kernels, chol_inv(): pl.pallas_call(functools.partial(_chol_kernel, float(count)), out_shape=(...  24.7 us
    pallas_call x1, Pallas kernels, jac_apply(): pl.pallas_call(functools.partial(_jac_kernel, nbulk), out_shape=jax.Shape...  14.8 us
    dot_general x2, matrix products, cholesky_step(): lax.dot_general(data, inverse, (((1,), (1,)), ((), ())), precision=high,...  5.33 us
    dot_general x2, matrix products, cholesky_step(): lax.dot_general(data, data, (((0,), (0,)), ((), ())), precision=high, pre...  4.07 us
    unnamed x10, local copies, waits for them, and re-layouts  3.5 us

profile of v7, /device:TPU:1, one launch (start us, length us, event | category | flops | bytes accessed | tf_op | source)
XLA Modules:
  0.0 143.3 jit_solution(5783535927373794026)
XLA Ops:
  0.6 0.0 copy-start
  0.6 1.2 copy-done
  1.9 2.5 %fusion.1.x_ref = f32[128,128]{1,0:T(8,128)} fusion(f32[2048,128]{1,0:T(8,128)S(1)} %copy-done), kind=kOutput, calls=%fused_computation.1 | convolution fusion | flops 402653184 | bytes 1114112 | tf_op jit(solution)/shard_map/dot_general | solution.py:285
  4.3 35.5 %shard_map.66.g_ref = f32[128,128]{1,0:T(8,128)} custom-call(f32[128,128]{1,0:T(8,128)} %fusion.1.x_ref), custom_call_target="tpu_custom_call" | custom-call | tf_op jit(solution)/shard_map/pallas_call | solution.py:129
  39.9 12.3 %shard_map.67 = (f32[128,128]{1,0:T(8,128)}, f32[128,128]{1,0:T(8,128)}) custom-call(f32[128,128]{1,0:T(8,128)} %shard_map.66.g_ref), custom_call_target="tpu_custom_call" | custom-call | tf_op jit(solution)/shard_map/pallas_call | solution.py:183
  52.1 0.0 copy-start.3
  52.1 1.9 %fusion.2 = f32[128,2048]{1,0:T(8,128)S(1)} fusion(f32[128,128]{1,0:T(8,128)} %get-tuple-element.8, f32[2048,128]{1,0:T(8,128)S(1)} %copy-done), kind=kOutput, calls=%fused_computation.2 | convolution fusion | flops 402653184 | bytes 2162688 | tf_op jit(solution)/shard_map/dot_general | solution.py:289
  54.0 1.6 %fusion.3.x_ref = f32[128,128]{1,0:T(8,128)} fusion(f32[128,2048]{1,0:T(8,128)S(1)} %fusion.2), kind=kOutput, calls=%fused_computation.3 | convolution fusion | flops 402653184 | bytes 1114112 | tf_op jit(solution)/shard_map/dot_general | solution.py:285
  55.7 24.7 %shard_map.68.g_ref = f32[128,128]{1,0:T(8,128)} custom-call(f32[128,128]{1,0:T(8,128)} %fusion.3.x_ref), custom_call_target="tpu_custom_call" | custom-call | tf_op jit(solution)/shard_map/pallas_call | solution.py:129
  80.4 12.4 %shard_map.69 = (f32[128,128]{1,0:T(8,128)}, f32[128,128]{1,0:T(8,128)}) custom-call(f32[128,128]{1,0:T(8,128)} %shard_map.68.g_ref), custom_call_target="tpu_custom_call" | custom-call | tf_op jit(solution)/shard_map/pallas_call | solution.py:183
  92.8 0.0 copy-done.3
  92.8 1.7 %fusion.4 = f32[128,128]{1,0:T(8,128)} fusion(f32[128,128]{1,0:T(8,128)} %get-tuple-element.10, f32[128,128]{1,0:T(8,128)S(1)} %copy-done.3), kind=kOutput, calls=%fused_computation.4 | convolution fusion | flops 25165824 | bytes 196608 | tf_op jit(solution)/shard_map/dot_general | solution.py:303
  94.5 3.4 %fusion = (bf16[2048,128]{1,0:T(8,128)(2,1)}, f32[2048,128]{1,0:T(8,128)S(1)}) fusion(f32[128,2048]{1,0:T(8,128)S(1)} %fusion.2, f32[128,128]{1,0:T(8,128)} %get-tuple-element.9), kind=kOutput, calls=%fused_computation | convolution fusion | flops 402915328 | bytes 2686976 | tf_op jit(solution)/shard_map/dot_general | solution.py:289
  97.9 0.0 copy-start.2
  97.9 14.8 %shard_map.70 = bf16[16,128,128]{2,1,0:T(8,128)(2,1)} custom-call(s32[4,16]{1,0:T(4,128)} %bitcast.18, bf16[16,128,128]{2,1,0:T(8,128)(2,1)} %bitcast.17, bf16[16,4,128,128]{3,2,1,0:T(8,128)(2,1)} %jac_ref.1), custom_call_target="tpu_custom_call" | custom-call | tf_op jit(solution)/shard_map/pallas_call | solution.py:264
  112.8 0.0 copy-start.1
  112.8 2.7 %fusion.5.x_ref = f32[128,128]{1,0:T(8,128)} fusion(f32[2048,128]{1,0:T(8,128)S(1)} %get-tuple-element.18, bf16[2048,128]{1,0:T(8,128)(2,1)} %bitcast.15), kind=kOutput, calls=%fused_computation.5 | convolution fusion | flops 402653184 | bytes 1638400 | tf_op jit(solution)/shard_map/dot_general | solution.py:306
  115.5 0.0 copy-done.2
  115.5 25.5 %shard_map.71 = f32[128,128]{1,0:T(8,128)} custom-call(f32[128,128]{1,0:T(8,128)} %fusion.5.x_ref), custom_call_target="tpu_custom_call" | custom-call | tf_op jit(solution)/shard_map/pallas_call | solution.py:129
  141.0 0.0 copy-done.1
  141.0 0.8 copy.9
  141.8 1.5 %copy.10 = f32[128,128]{1,0:T(8,128)} copy(f32[128,128]{1,0:T(8,128)} %shard_map.71) | data formatting | bytes 131072
Async XLA Ops:
  0.6 1.2 copy-start
  52.1 40.7 %copy-start.3 = (f32[128,128]{1,0:T(8,128)S(1)}, f32[128,128]{1,0:T(8,128)}, u32[]{:S(2)}) copy-start(f32[128,128]{1,0:T(8,128)} %get-tuple-element.11) | copy-start | bytes 196612
  97.9 17.6 %copy-start.2 = (f32[2048,128]{1,0:T(8,128)}, f32[2048,128]{1,0:T(8,128)S(1)}, u32[]{:S(2)}) copy-start(f32[2048,128]{1,0:T(8,128)S(1)} %get-tuple-element.18) | copy-start | bytes 3145732
  112.8 28.2 %copy-start.1 = (bf16[16,128,128]{2,1,0:T(8,128)(2,1)S(1)}, bf16[16,128,128]{2,1,0:T(8,128)(2,1)}, u32[]{:S(2)}) copy-start(bf16[16,128,128]{2,1,0:T(8,128)(2,1)} %shard_map.70) | copy-start | bytes 1572868

commit v8 on v7

--- a/solution.py
+++ b/solution.py
@@ -159,7 +159,8 @@
     for k in range(n):
         r0 = k // 8 * 8
         row = a[k - r0:k - r0 + 1, :]
-        recip = lax.rsqrt(row[:, k:k + 1])
+        colb = jnp.broadcast_to(a[:, k:k + 1], a.shape)
+        recip = lax.rsqrt(colb[k - r0:k - r0 + 1, :])
         lrow = jnp.where(lane_row >= k, row * recip, 0.0)
         wrow = w[k - r0:k - r0 + 1, :] * recip
         lt_rows.append(lrow)
@@ -173,10 +174,12 @@
             if r1 > r0:
                 a = a[r1 - r0:]
                 w = w[r1 - r0:]
+                colb = colb[r1 - r0:]
             idx = lax.broadcasted_iota(jnp.int32, (n - r1, 1), 0) + r1
-            m = jnp.where(idx > k, a[:, k:k + 1] * recip, 0.0)
+            m = jnp.where(idx > k, colb * recip, 0.0)
             a = a - m * lrow
             w = w - m * wrow
+
 
 def chol_inv(g, count):
     n = g.shape[0]

time: 144 us -> 144 us (level)
  no operation moved by 1% of the time
where the time goes in v8:
time: 144 us; the launch traced here: 143 us
  Pallas kernels  125 us (87%)
  matrix products  14 us (10%)
  local copies, waits for them, and re-layouts  3.5 us (2%)
    pallas_call x3, Pallas kernels, allreduce(): pl.pallas_call(functools.partial(_allreduce_kernel, dims, scale), out_sha...  85.8 us
    pallas_call x2, Pallas kernels, chol_inv(): pl.pallas_call(functools.partial(_chol_kernel, float(count)), out_shape=(...  24.5 us
    pallas_call x1, Pallas kernels, jac_apply(): pl.pallas_call(functools.partial(_jac_kernel, nbulk), out_shape=jax.Shape...  14.8 us
    dot_general x2, matrix products, cholesky_step(): lax.dot_general(data, inverse, (((1,), (1,)), ((), ())), precision=high,...  5.5 us
    dot_general x2, matrix products, cholesky_step(): lax.dot_general(data, data, (((0,), (0,)), ((), ())), precision=high, pre...  4.07 us
    unnamed x10, local copies, waits for them, and re-layouts  3.5 us

profile of v8, /device:TPU:1, one launch (start us, length us, event | category | flops | bytes accessed | tf_op | source)
XLA Modules:
  0.0 143.4 jit_solution(5192059325713921003)
XLA Ops:
  0.6 0.0 copy-start
  0.6 1.2 copy-done
  1.9 2.5 %fusion.1.x_ref = f32[128,128]{1,0:T(8,128)} fusion(f32[2048,128]{1,0:T(8,128)S(1)} %copy-done), kind=kOutput, calls=%fused_computation.1 | convolution fusion | flops 402653184 | bytes 1114112 | tf_op jit(solution)/shard_map/dot_general | solution.py:288
  4.3 35.5 %shard_map.66.g_ref = f32[128,128]{1,0:T(8,128)} custom-call(f32[128,128]{1,0:T(8,128)} %fusion.1.x_ref), custom_call_target="tpu_custom_call" | custom-call | tf_op jit(solution)/shard_map/pallas_call | solution.py:129
  39.9 12.3 %shard_map.67 = (f32[128,128]{1,0:T(8,128)}, f32[128,128]{1,0:T(8,128)}) custom-call(f32[128,128]{1,0:T(8,128)} %shard_map.66.g_ref), custom_call_target="tpu_custom_call" | custom-call | tf_op jit(solution)/shard_map/pallas_call | solution.py:186
  52.1 0.0 copy-start.3
  52.1 1.9 %fusion.2 = f32[128,2048]{1,0:T(8,128)S(1)} fusion(f32[128,128]{1,0:T(8,128)} %get-tuple-element.8, f32[2048,128]{1,0:T(8,128)S(1)} %copy-done), kind=kOutput, calls=%fused_computation.2 | convolution fusion | flops 402653184 | bytes 2162688 | tf_op jit(solution)/shard_map/dot_general | solution.py:292
  54.0 1.6 %fusion.3.x_ref = f32[128,128]{1,0:T(8,128)} fusion(f32[128,2048]{1,0:T(8,128)S(1)} %fusion.2), kind=kOutput, calls=%fused_computation.3 | convolution fusion | flops 402653184 | bytes 1114112 | tf_op jit(solution)/shard_map/dot_general | solution.py:288
  55.6 24.7 %shard_map.68.g_ref = f32[128,128]{1,0:T(8,128)} custom-call(f32[128,128]{1,0:T(8,128)} %fusion.3.x_ref), custom_call_target="tpu_custom_call" | custom-call | tf_op jit(solution)/shard_map/pallas_call | solution.py:129
  80.4 12.3 %shard_map.69 = (f32[128,128]{1,0:T(8,128)}, f32[128,128]{1,0:T(8,128)}) custom-call(f32[128,128]{1,0:T(8,128)} %shard_map.68.g_ref), custom_call_target="tpu_custom_call" | custom-call | tf_op jit(solution)/shard_map/pallas_call | solution.py:186
  92.6 0.0 copy-done.3
  92.6 1.7 %fusion.4 = f32[128,128]{1,0:T(8,128)} fusion(f32[128,128]{1,0:T(8,128)} %get-tuple-element.10, f32[128,128]{1,0:T(8,128)S(1)} %copy-done.3), kind=kOutput, calls=%fused_computation.4 | convolution fusion | flops 25165824 | bytes 196608 | tf_op jit(solution)/shard_map/dot_general | solution.py:306
  94.3 3.6 %fusion = (bf16[2048,128]{1,0:T(8,128)(2,1)}, f32[2048,128]{1,0:T(8,128)S(1)}) fusion(f32[128,2048]{1,0:T(8,128)S(1)} %fusion.2, f32[128,128]{1,0:T(8,128)} %get-tuple-element.9), kind=kOutput, calls=%fused_computation | convolution fusion | flops 402915328 | bytes 2686976 | tf_op jit(solution)/shard_map/dot_general | solution.py:292
  97.9 0.0 copy-start.2
  97.9 14.8 %shard_map.70 = bf16[16,128,128]{2,1,0:T(8,128)(2,1)} custom-call(s32[4,16]{1,0:T(4,128)} %bitcast.18, bf16[16,128,128]{2,1,0:T(8,128)(2,1)} %bitcast.17, bf16[16,4,128,128]{3,2,1,0:T(8,128)(2,1)} %jac_ref.1), custom_call_target="tpu_custom_call" | custom-call | tf_op jit(solution)/shard_map/pallas_call | solution.py:267
  112.8 0.0 copy-start.1
  112.8 2.7 %fusion.5.x_ref = f32[128,128]{1,0:T(8,128)} fusion(f32[2048,128]{1,0:T(8,128)S(1)} %get-tuple-element.18, bf16[2048,128]{1,0:T(8,128)(2,1)} %bitcast.15), kind=kOutput, calls=%fused_computation.5 | convolution fusion | flops 402653184 | bytes 1638400 | tf_op jit(solution)/shard_map/dot_general | solution.py:309
  115.5 0.0 copy-done.2
  115.5 25.6 %shard_map.71 = f32[128,128]{1,0:T(8,128)} custom-call(f32[128,128]{1,0:T(8,128)} %fusion.5.x_ref), custom_call_target="tpu_custom_call" | custom-call | tf_op jit(solution)/shard_map/pallas_call | solution.py:129
  141.1 0.0 copy-done.1
  141.1 0.8 copy.9
  141.9 1.5 %copy.10 = f32[128,128]{1,0:T(8,128)} copy(f32[128,128]{1,0:T(8,128)} %shard_map.71) | data formatting | bytes 131072
Async XLA Ops:
  0.6 1.2 copy-start
  52.1 40.5 %copy-start.3 = (f32[128,128]{1,0:T(8,128)S(1)}, f32[128,128]{1,0:T(8,128)}, u32[]{:S(2)}) copy-start(f32[128,128]{1,0:T(8,128)} %get-tuple-element.11) | copy-start | bytes 196612
  97.9 17.6 %copy-start.2 = (f32[2048,128]{1,0:T(8,128)}, f32[2048,128]{1,0:T(8,128)S(1)}, u32[]{:S(2)}) copy-start(f32[2048,128]{1,0:T(8,128)S(1)} %get-tuple-element.18) | copy-start | bytes 3145732
  112.8 28.3 %copy-start.1 = (bf16[16,128,128]{2,1,0:T(8,128)(2,1)S(1)}, bf16[16,128,128]{2,1,0:T(8,128)(2,1)}, u32[]{:S(2)}) copy-start(bf16[16,128,128]{2,1,0:T(8,128)(2,1)} %shard_map.70) | copy-start | bytes 1572868

commit v9 on v8

--- a/solution.py
+++ b/solution.py
@@ -146,7 +146,12 @@
     return allreduce
 
 
-def _chol_kernel(count, g_ref, lt_ref, w_ref):
+def _chol_kernel(count, g_ref, *refs):
+    if len(refs) == 4:
+        prev_ref, lt_ref, w_ref, f_ref = refs
+    else:
+        prev_ref, f_ref = None, None
+        lt_ref, w_ref = refs
     n = g_ref.shape[0]
     g = g_ref[...] / count
     a = (g + g.T) / 2
@@ -179,16 +184,22 @@
             m = jnp.where(idx > k, colb * recip, 0.0)
             a = a - m * lrow
             w = w - m * wrow
-
-
-def chol_inv(g, count):
+    if f_ref is not None:
+        f_ref[...] = jnp.dot(lt_ref[...], prev_ref[...], precision=lax.Precision.HIGHEST,
+                             preferred_element_type=jnp.float32)
+
+
+def chol_inv(g, count, prev=None):
     n = g.shape[0]
+    square = jax.ShapeDtypeStruct((n, n), jnp.float32)
+    vmem = pl.BlockSpec(memory_space=pltpu.VMEM)
+    outs = 2 if prev is None else 3
     return pl.pallas_call(
         functools.partial(_chol_kernel, float(count)),
-        out_shape=(jax.ShapeDtypeStruct((n, n), jnp.float32), jax.ShapeDtypeStruct((n, n), jnp.float32)),
-        in_specs=[pl.BlockSpec(memory_space=pltpu.VMEM)],
-        out_specs=(pl.BlockSpec(memory_space=pltpu.VMEM), pl.BlockSpec(memory_space=pltpu.VMEM)),
-    )(g)
+        out_shape=(square,) * outs,
+        in_specs=[vmem] * (1 if prev is None else 2),
+        out_specs=(vmem,) * outs,
+    )(g, *(() if prev is None else (prev,)))
 
 
 def _jac_kernel(nbulk, cols_hbm, modes_ref, jac_ref, out_ref, ext, cols_ref, cols_sem, send_sem, recv_sem):
@@ -283,16 +294,16 @@
     return out.reshape(rb * blk, width)
 
 
-def cholesky_step(data, row_count, allreduce):
+def cholesky_step(data, row_count, allreduce, prev=None):
     high = lax.Precision.HIGHEST
     partial_value = lax.dot_general(
         data, data, (((0,), (0,)), ((), ())), precision=high, preferred_element_type=jnp.float32
     )
-    upper, inverse = chol_inv(allreduce(partial_value), row_count)
+    outs = chol_inv(allreduce(partial_value), row_count, prev)
     result = lax.dot_general(
-        data, inverse, (((1,), (1,)), ((), ())), precision=high, preferred_element_type=jnp.float32
-    )
-    return (result, upper)
+        data, outs[1], (((1,), (1,)), ((), ())), precision=high, preferred_element_type=jnp.float32
+    )
+    return (result, outs[0] if prev is None else outs[2])
 
 
 def shards(dims, snapshots, jac_blocks, jac_cols):
@@ -302,8 +313,7 @@
     blk = jac_blocks.shape[2]
     row_count = local_rows * lax.axis_size(("bulk", "span"))
     first, upper1 = cholesky_step(snapshots, row_count, make_allreduce(dims, 0))
-    modes, upper2 = cholesky_step(first, row_count, make_allreduce(dims, 1))
-    factor = jnp.dot(upper2, upper1, precision=high, preferred_element_type=jnp.float32)
+    modes, factor = cholesky_step(first, row_count, make_allreduce(dims, 1), upper1)
     modes_b = modes.astype(jnp.bfloat16)
     jac_modes = jac_apply(lax.axis_size("bulk"), 3, jac_cols, modes_b, jac_blocks)
     partial_value = lax.dot_general(

time: 144 us -> 142 us (0.986)
  matrix products: 14 us -> 12.3 us
    dot_general x3 -> x2, matrix products: 7.18 us -> 5.47 us  [cholesky_step(): lax.dot_general(data, outs[1], (((1,), (1,)), ((), ())), precision=high,...]
    unnamed x10 -> x8, local copies, waits for them, and re-layouts: 3.5 us -> 3.5 us
where the time goes in v9:
time: 142 us
  Pallas kernels  125 us (88%)
  matrix products  12.3 us (9%)
  local copies, waits for them, and re-layouts  3.5 us (2%)
    pallas_call x3, Pallas kernels, allreduce(): pl.pallas_call(functools.partial(_allreduce_kernel, dims, scale), out_sha...  85.8 us
    pallas_call x2, Pallas kernels, chol_inv(): pl.pallas_call(functools.partial(_chol_kernel, float(count)), out_shape=(...  24.7 us
    pallas_call x1, Pallas kernels, jac_apply(): pl.pallas_call(functools.partial(_jac_kernel, nbulk), out_shape=jax.Shape...  14.8 us
    dot_general x2, matrix products, cholesky_step(): lax.dot_general(data, outs[1], (((1,), (1,)), ((), ())), precision=high,...  5.47 us
    dot_general x2, matrix products, cholesky_step(): lax.dot_general(data, data, (((0,), (0,)), ((), ())), precision=high, pre...  4.07 us
    unnamed x8, local copies, waits for them, and re-layouts  3.5 us

profile of v9, /device:TPU:1, one launch (start us, length us, event | category | flops | bytes accessed | tf_op | source)
XLA Modules:
  0.0 141.8 jit_solution(4161781907507724587)
XLA Ops:
  0.6 0.0 copy-start
  0.6 1.2 copy-done
  1.9 2.5 %fusion.1.x_ref = f32[128,128]{1,0:T(8,128)} fusion(f32[2048,128]{1,0:T(8,128)S(1)} %copy-done), kind=kOutput, calls=%fused_computation.1 | convolution fusion | flops 402653184 | bytes 1114112 | tf_op jit(solution)/shard_map/dot_general | solution.py:299
  4.3 35.5 %shard_map.66.g_ref = f32[128,128]{1,0:T(8,128)} custom-call(f32[128,128]{1,0:T(8,128)} %fusion.1.x_ref), custom_call_target="tpu_custom_call" | custom-call | tf_op jit(solution)/shard_map/pallas_call | solution.py:129
  39.9 12.3 %shard_map.67 = (f32[128,128]{1,0:T(8,128)}, f32[128,128]{1,0:T(8,128)}) custom-call(f32[128,128]{1,0:T(8,128)} %shard_map.66.g_ref), custom_call_target="tpu_custom_call" | custom-call | tf_op jit(solution)/shard_map/pallas_call | solution.py:197
  52.1 1.9 %fusion.2 = f32[128,2048]{1,0:T(8,128)S(1)} fusion(f32[128,128]{1,0:T(8,128)} %get-tuple-element.8, f32[2048,128]{1,0:T(8,128)S(1)} %copy-done), kind=kOutput, calls=%fused_computation.2 | convolution fusion | flops 402653184 | bytes 2162688 | tf_op jit(solution)/shard_map/dot_general | solution.py:303
  54.0 1.6 %fusion.3.x_ref = f32[128,128]{1,0:T(8,128)} fusion(f32[128,2048]{1,0:T(8,128)S(1)} %fusion.2), kind=kOutput, calls=%fused_computation.3 | convolution fusion | flops 402653184 | bytes 1114112 | tf_op jit(solution)/shard_map/dot_general | solution.py:299
  55.6 24.7 %shard_map.68.g_ref = f32[128,128]{1,0:T(8,128)} custom-call(f32[128,128]{1,0:T(8,128)} %fusion.3.x_ref), custom_call_target="tpu_custom_call" | custom-call | tf_op jit(solution)/shard_map/pallas_call | solution.py:129
  80.3 12.4 %shard_map.69 = (f32[128,128]{1,0:T(8,128)}, f32[128,128]{1,0:T(8,128)}, f32[128,128]{1,0:T(8,128)}) custom-call(f32[128,128]{1,0:T(8,128)} %shard_map.68.g_ref, f32[128,128]{1,0:T(8,128)} %get-tuple-element.9.refs_0_), custom_call_target="tpu_custom_call" | custom-call | tf_op jit(solution)/shard_map/pallas_call | solution.py:197
  92.7 3.6 %fusion = (bf16[2048,128]{1,0:T(8,128)(2,1)}, f32[2048,128]{1,0:T(8,128)S(1)}) fusion(f32[128,2048]{1,0:T(8,128)S(1)} %fusion.2, f32[128,128]{1,0:T(8,128)} %get-tuple-element.10), kind=kOutput, calls=%fused_computation | convolution fusion | flops 402915328 | bytes 2686976 | tf_op jit(solution)/shard_map/dot_general | solution.py:303
  96.4 0.0 copy-start.2
  96.4 14.8 %shard_map.70 = bf16[16,128,128]{2,1,0:T(8,128)(2,1)} custom-call(s32[4,16]{1,0:T(4,128)} %bitcast.16, bf16[16,128,128]{2,1,0:T(8,128)(2,1)} %bitcast.15, bf16[16,4,128,128]{3,2,1,0:T(8,128)(2,1)} %jac_ref.1), custom_call_target="tpu_custom_call" | custom-call | tf_op jit(solution)/shard_map/pallas_call | solution.py:278
  111.2 0.0 copy-start.1
  111.2 2.7 %fusion.4.x_ref = f32[128,128]{1,0:T(8,128)} fusion(f32[2048,128]{1,0:T(8,128)S(1)} %get-tuple-element.18, bf16[2048,128]{1,0:T(8,128)(2,1)} %bitcast.13), kind=kOutput, calls=%fused_computation.4 | convolution fusion | flops 402653184 | bytes 1638400 | tf_op jit(solution)/shard_map/dot_general | solution.py:319
  114.0 0.0 copy-done.2
  114.0 25.6 %shard_map.71 = f32[128,128]{1,0:T(8,128)} custom-call(f32[128,128]{1,0:T(8,128)} %fusion.4.x_ref), custom_call_target="tpu_custom_call" | custom-call | tf_op jit(solution)/shard_map/pallas_call | solution.py:129
  139.5 0.0 copy-done.1
  139.5 0.8 copy.9
  140.3 1.5 %copy.10 = f32[128,128]{1,0:T(8,128)} copy(f32[128,128]{1,0:T(8,128)} %shard_map.71) | data formatting | bytes 131072
Async XLA Ops:
  0.6 1.2 copy-start
  96.4 17.6 %copy-start.2 = (f32[2048,128]{1,0:T(8,128)}, f32[2048,128]{1,0:T(8,128)S(1)}, u32[]{:S(2)}) copy-start(f32[2048,128]{1,0:T(8,128)S(1)} %get-tuple-element.18) | copy-start | bytes 3145732
  111.2 28.3 %copy-start.1 = (bf16[16,128,128]{2,1,0:T(8,128)(2,1)S(1)}, bf16[16,128,128]{2,1,0:T(8,128)(2,1)}, u32[]{:S(2)}) copy-start(bf16[16,128,128]{2,1,0:T(8,128)(2,1)} %shard_map.70) | copy-start | bytes 1572868

commit v10 on v9

--- a/solution.py
+++ b/solution.py
@@ -316,13 +316,17 @@
     modes, factor = cholesky_step(first, row_count, make_allreduce(dims, 1), upper1)
     modes_b = modes.astype(jnp.bfloat16)
     jac_modes = jac_apply(lax.axis_size("bulk"), 3, jac_cols, modes_b, jac_blocks)
-    partial_value = lax.dot_general(
-        modes,
-        jac_modes.astype(jnp.float32),
-        (((0,), (0,)), ((), ())),
-        precision=high,
-        preferred_element_type=jnp.float32,
-    )
+    pieces = [modes_b]
+    rest = modes - lax.reduce_precision(modes, exponent_bits=8, mantissa_bits=7)
+    for _ in range(2):
+        pieces.append(rest.astype(jnp.bfloat16))
+        rest = rest - lax.reduce_precision(rest, exponent_bits=8, mantissa_bits=7)
+    partial_value = None
+    for piece in pieces:
+        term = lax.dot_general(
+            piece, jac_modes, (((0,), (0,)), ((), ())), preferred_element_type=jnp.float32
+        )
+        partial_value = term if partial_value is None else partial_value + term
     reduced = make_allreduce(dims, 2, 1.0 / row_count)(partial_value)
     return (modes, factor, jac_modes, reduced)
 

time: 142 us -> 144 us (1.014)
    dot_general x1 -> x3, matrix products: 2.73 us -> 3.81 us  [shards(): lax.dot_general(piece, jac_modes, (((0,), (0,)), ((), ())), preferred_ele...]
    unnamed x8 -> x10, local copies, waits for them, and re-layouts: 3.5 us -> 3.5 us
where the time goes in v10:
time: 144 us; the launch traced here: 143 us
  Pallas kernels  125 us (87%)
  matrix products  13.3 us (9%)
  local copies, waits for them, and re-layouts  3.5 us (2%)
    pallas_call x3, Pallas kernels, allreduce(): pl.pallas_call(functools.partial(_allreduce_kernel, dims, scale), out_sha...  85.7 us
    pallas_call x2, Pallas kernels, chol_inv(): pl.pallas_call(functools.partial(_chol_kernel, float(count)), out_shape=(...  24.7 us
    pallas_call x1, Pallas kernels, jac_apply(): pl.pallas_call(functools.partial(_jac_kernel, nbulk), out_shape=jax.Shape...  15 us
    dot_general x2, matrix products, cholesky_step(): lax.dot_general(data, outs[1], (((1,), (1,)), ((), ())), precision=high,...  5.47 us
    dot_general x2, matrix products, cholesky_step(): lax.dot_general(data, data, (((0,), (0,)), ((), ())), precision=high, pre...  4.07 us
    dot_general x3, matrix products, shards(): lax.dot_general(piece, jac_modes, (((0,), (0,)), ((), ())), preferred_ele...  3.81 us
    unnamed x10, local copies, waits for them, and re-layouts  3.5 us

profile of v10, /device:TPU:1, one launch (start us, length us, event | category | flops | bytes accessed | tf_op | source)
XLA Modules:
  0.0 143.0 jit_solution(9121334580695024500)
XLA Ops:
  0.6 0.0 copy-start
  0.6 1.2 copy-done
  1.9 2.5 %fusion.5.x_ref = f32[128,128]{1,0:T(8,128)} fusion(f32[2048,128]{1,0:T(8,128)S(1)} %copy-done), kind=kOutput, calls=%fused_computation.7 | convolution fusion | flops 402653184 | bytes 1114112 | tf_op jit(solution)/shard_map/dot_general | solution.py:299
  4.3 35.5 %shard_map.66.g_ref = f32[128,128]{1,0:T(8,128)} custom-call(f32[128,128]{1,0:T(8,128)} %fusion.5.x_ref), custom_call_target="tpu_custom_call" | custom-call | tf_op jit(solution)/shard_map/pallas_call | solution.py:129
  39.9 12.3 %shard_map.67 = (f32[128,128]{1,0:T(8,128)}, f32[128,128]{1,0:T(8,128)}) custom-call(f32[128,128]{1,0:T(8,128)} %shard_map.66.g_ref), custom_call_target="tpu_custom_call" | custom-call | tf_op jit(solution)/shard_map/pallas_call | solution.py:197
  52.1 1.9 %fusion.6 = f32[128,2048]{1,0:T(8,128)S(1)} fusion(f32[128,128]{1,0:T(8,128)} %get-tuple-element.8, f32[2048,128]{1,0:T(8,128)S(1)} %copy-done), kind=kOutput, calls=%fused_computation.8 | convolution fusion | flops 402653184 | bytes 2162688 | tf_op jit(solution)/shard_map/dot_general | solution.py:303
  54.0 1.6 %fusion.7.x_ref = f32[128,128]{1,0:T(8,128)} fusion(f32[128,2048]{1,0:T(8,128)S(1)} %fusion.6), kind=kOutput, calls=%fused_computation.9 | convolution fusion | flops 402653184 | bytes 1114112 | tf_op jit(solution)/shard_map/dot_general | solution.py:299
  55.6 24.7 %shard_map.68.g_ref = f32[128,128]{1,0:T(8,128)} custom-call(f32[128,128]{1,0:T(8,128)} %fusion.7.x_ref), custom_call_target="tpu_custom_call" | custom-call | tf_op jit(solution)/shard_map/pallas_call | solution.py:129
  80.3 12.4 %shard_map.69 = (f32[128,128]{1,0:T(8,128)}, f32[128,128]{1,0:T(8,128)}, f32[128,128]{1,0:T(8,128)}) custom-call(f32[128,128]{1,0:T(8,128)} %shard_map.68.g_ref, f32[128,128]{1,0:T(8,128)} %get-tuple-element.9.refs_0_), custom_call_target="tpu_custom_call" | custom-call | tf_op jit(solution)/shard_map/pallas_call | solution.py:197
  92.8 3.6 %fusion.4 = (bf16[2048,128]{1,0:T(8,128)(2,1)}, f32[2048,128]{1,0:T(8,128)S(1)}) fusion(f32[128,2048]{1,0:T(8,128)S(1)} %fusion.6, f32[128,128]{1,0:T(8,128)} %get-tuple-element.10), kind=kOutput, calls=%fused_computation.6 | convolution fusion | flops 402915328 | bytes 2686976 | tf_op jit(solution)/shard_map/dot_general | solution.py:303
  96.4 0.0 copy-start.2
  96.4 0.0 copy-start.3
  96.4 15.0 %shard_map.70 = bf16[16,128,128]{2,1,0:T(8,128)(2,1)} custom-call(s32[4,16]{1,0:T(4,128)} %bitcast.20, bf16[16,128,128]{2,1,0:T(8,128)(2,1)} %bitcast.19, bf16[16,4,128,128]{3,2,1,0:T(8,128)(2,1)} %jac_ref.1), custom_call_target="tpu_custom_call" | custom-call | tf_op jit(solution)/shard_map/pallas_call | solution.py:278
  111.4 0.0 copy-start.1
  111.4 0.0 copy-done.3
  111.4 1.4 %fusion.8 = f32[128,128]{1,0:T(8,128)S(1)} fusion(bf16[2048,128]{1,0:T(8,128)(2,1)S(1)} %copy-done.3, bf16[2048,128]{1,0:T(8,128)(2,1)} %bitcast.15), kind=kOutput, calls=%fused_computation.10 | convolution fusion | flops 67108864 | bytes 1114112 | tf_op jit(solution)/shard_map/dot_general | solution.py:326
  112.8 1.4 convolution_add_fusion.1
  114.2 0.0 copy-done.2
  114.2 0.0 copy-done.1
  114.3 1.0 convolution_add_fusion.x_ref
  115.2 25.5 %shard_map.71 = f32[128,128]{1,0:T(8,128)} custom-call(f32[128,128]{1,0:T(8,128)} %convolution_add_fusion.x_ref), custom_call_target="tpu_custom_call" | custom-call | tf_op jit(solution)/shard_map/pallas_call | solution.py:129
  140.7 0.8 copy.9
  141.5 1.5 %copy.10 = f32[128,128]{1,0:T(8,128)} copy(f32[128,128]{1,0:T(8,128)} %shard_map.71) | data formatting | bytes 131072
Async XLA Ops:
  0.6 1.2 copy-start
  96.4 17.8 %copy-start.2 = (f32[2048,128]{1,0:T(8,128)}, f32[2048,128]{1,0:T(8,128)S(1)}, u32[]{:S(2)}) copy-start(f32[2048,128]{1,0:T(8,128)S(1)} %get-tuple-element.18) | copy-start | bytes 3145732
  96.4 15.0 %copy-start.3 = (bf16[2048,128]{1,0:T(8,128)(2,1)S(1)}, bf16[2048,128]{1,0:T(8,128)(2,1)}, u32[]{:S(2)}) copy-start(bf16[2048,128]{1,0:T(8,128)(2,1)} %get-tuple-element.12) | copy-start | bytes 1572868
  111.4 2.9 %copy-start.1 = (bf16[16,128,128]{2,1,0:T(8,128)(2,1)S(1)}, bf16[16,128,128]{2,1,0:T(8,128)(2,1)}, u32[]{:S(2)}) copy-start(bf16[16,128,128]{2,1,0:T(8,128)(2,1)} %shard_map.70) | copy-start | bytes 1572868

commit v11 on v9

--- a/solution.py
+++ b/solution.py
@@ -301,7 +301,8 @@
     )
     outs = chol_inv(allreduce(partial_value), row_count, prev)
     result = lax.dot_general(
-        data, outs[1], (((1,), (1,)), ((), ())), precision=high, preferred_element_type=jnp.float32
+        data, outs[1], (((1,), (1,)), ((), ())), precision=lax.Precision.HIGH,
+        preferred_element_type=jnp.float32,
     )
     return (result, outs[0] if prev is None else outs[2])
 
@@ -320,7 +321,7 @@
         modes,
         jac_modes.astype(jnp.float32),
         (((0,), (0,)), ((), ())),
-        precision=high,
+        precision=lax.Precision.HIGH,
         preferred_element_type=jnp.float32,
     )
     reduced = make_allreduce(dims, 2, 1.0 / row_count)(partial_value)

time: 142 us -> 141 us (level)
  matrix products: 12.3 us -> 10.6 us
    dot_general x2, matrix products: 5.47 us -> 4.05 us  [cholesky_step(): lax.dot_general(data, outs[1], (((1,), (1,)), ((), ())), precision=lax.Pr...]
where the time goes in v11:
time: 141 us; the launch traced here: 140 us
  Pallas kernels  125 us (89%)
  matrix products  10.6 us (8%)
  local copies, waits for them, and re-layouts  3.5 us (2%)
    pallas_call x3, Pallas kernels, allreduce(): pl.pallas_call(functools.partial(_allreduce_kernel, dims, scale), out_sha...  85.9 us
    pallas_call x2, Pallas kernels, chol_inv(): pl.pallas_call(functools.partial(_chol_kernel, float(count)), out_shape=(...  24.7 us
    pallas_call x1, Pallas kernels, jac_apply(): pl.pallas_call(functools.partial(_jac_kernel, nbulk), out_shape=jax.Shape...  14.8 us
    dot_general x2, matrix products, cholesky_step(): lax.dot_general(data, data, (((0,), (0,)), ((), ())), precision=high, pre...  4.07 us
    dot_general x2, matrix products, cholesky_step(): lax.dot_general(data, outs[1], (((1,), (1,)), ((), ())), precision=lax.Pr...  4.05 us
    unnamed x8, local copies, waits for them, and re-layouts  3.5 us

profile of v11, /device:TPU:1, one launch (start us, length us, event | category | flops | bytes accessed | tf_op | source)
XLA Modules:
  0.0 140.2 jit_solution(186235940019140379)
XLA Ops:
  0.6 0.0 copy-start
  0.6 1.2 copy-done
  1.9 2.5 %fusion.1.x_ref = f32[128,128]{1,0:T(8,128)} fusion(f32[2048,128]{1,0:T(8,128)S(1)} %copy-done), kind=kOutput, calls=%fused_computation.1 | convolution fusion | flops 402653184 | bytes 1114112 | tf_op jit(solution)/shard_map/dot_general | solution.py:299
  4.3 35.5 %shard_map.66.g_ref = f32[128,128]{1,0:T(8,128)} custom-call(f32[128,128]{1,0:T(8,128)} %fusion.1.x_ref), custom_call_target="tpu_custom_call" | custom-call | tf_op jit(solution)/shard_map/pallas_call | solution.py:129
  39.9 12.3 %shard_map.67 = (f32[128,128]{1,0:T(8,128)}, f32[128,128]{1,0:T(8,128)}) custom-call(f32[128,128]{1,0:T(8,128)} %shard_map.66.g_ref), custom_call_target="tpu_custom_call" | custom-call | tf_op jit(solution)/shard_map/pallas_call | solution.py:197
  52.1 1.4 %fusion.2 = f32[128,2048]{1,0:T(8,128)S(1)} fusion(f32[128,128]{1,0:T(8,128)} %get-tuple-element.8, f32[2048,128]{1,0:T(8,128)S(1)} %copy-done), kind=kOutput, calls=%fused_computation.2 | convolution fusion | flops 201326592 | bytes 2162688 | tf_op jit(solution)/shard_map/dot_general | solution.py:303
  53.5 1.6 %fusion.3.x_ref = f32[128,128]{1,0:T(8,128)} fusion(f32[128,2048]{1,0:T(8,128)S(1)} %fusion.2), kind=kOutput, calls=%fused_computation.3 | convolution fusion | flops 402653184 | bytes 1114112 | tf_op jit(solution)/shard_map/dot_general | solution.py:299
  55.2 24.7 %shard_map.68.g_ref = f32[128,128]{1,0:T(8,128)} custom-call(f32[128,128]{1,0:T(8,128)} %fusion.3.x_ref), custom_call_target="tpu_custom_call" | custom-call | tf_op jit(solution)/shard_map/pallas_call | solution.py:129
  79.9 12.4 %shard_map.69 = (f32[128,128]{1,0:T(8,128)}, f32[128,128]{1,0:T(8,128)}, f32[128,128]{1,0:T(8,128)}) custom-call(f32[128,128]{1,0:T(8,128)} %shard_map.68.g_ref, f32[128,128]{1,0:T(8,128)} %get-tuple-element.9.refs_0_), custom_call_target="tpu_custom_call" | custom-call | tf_op jit(solution)/shard_map/pallas_call | solution.py:197
  92.3 2.6 %fusion = (bf16[2048,128]{1,0:T(8,128)(2,1)}, f32[2048,128]{1,0:T(8,128)S(1)}) fusion(f32[128,2048]{1,0:T(8,128)S(1)} %fusion.2, f32[128,128]{1,0:T(8,128)} %get-tuple-element.10), kind=kOutput, calls=%fused_computation | convolution fusion | flops 201588736 | bytes 2686976 | tf_op jit(solution)/shard_map/dot_general | solution.py:303
  94.9 0.0 copy-start.2
  94.9 14.8 %shard_map.70 = bf16[16,128,128]{2,1,0:T(8,128)(2,1)} custom-call(s32[4,16]{1,0:T(4,128)} %bitcast.16, bf16[16,128,128]{2,1,0:T(8,128)(2,1)} %bitcast.15, bf16[16,4,128,128]{3,2,1,0:T(8,128)(2,1)} %jac_ref.1), custom_call_target="tpu_custom_call" | custom-call | tf_op jit(solution)/shard_map/pallas_call | solution.py:278
  109.8 0.0 copy-start.1
  109.8 2.5 %fusion.4.x_ref = f32[128,128]{1,0:T(8,128)} fusion(f32[2048,128]{1,0:T(8,128)S(1)} %get-tuple-element.18, bf16[2048,128]{1,0:T(8,128)(2,1)} %bitcast.13), kind=kOutput, calls=%fused_computation.4 | convolution fusion | flops 201326592 | bytes 1638400 | tf_op jit(solution)/shard_map/dot_general | solution.py:320
  112.3 0.0 copy-done.2
  112.3 25.6 %shard_map.71 = f32[128,128]{1,0:T(8,128)} custom-call(f32[128,128]{1,0:T(8,128)} %fusion.4.x_ref), custom_call_target="tpu_custom_call" | custom-call | tf_op jit(solution)/shard_map/pallas_call | solution.py:129
  137.9 0.0 copy-done.1
  137.9 0.8 copy.9
  138.7 1.5 %copy.10 = f32[128,128]{1,0:T(8,128)} copy(f32[128,128]{1,0:T(8,128)} %shard_map.71) | data formatting | bytes 131072
Async XLA Ops:
  0.6 1.2 copy-start
  94.9 17.3 %copy-start.2 = (f32[2048,128]{1,0:T(8,128)}, f32[2048,128]{1,0:T(8,128)S(1)}, u32[]{:S(2)}) copy-start(f32[2048,128]{1,0:T(8,128)S(1)} %get-tuple-element.18) | copy-start | bytes 3145732
  109.8 28.1 %copy-start.1 = (bf16[16,128,128]{2,1,0:T(8,128)(2,1)S(1)}, bf16[16,128,128]{2,1,0:T(8,128)(2,1)}, u32[]{:S(2)}) copy-start(bf16[16,128,128]{2,1,0:T(8,128)(2,1)} %shard_map.70) | copy-start | bytes 1572868

commit v12 on v11

--- a/solution.py
+++ b/solution.py
@@ -294,14 +294,14 @@
     return out.reshape(rb * blk, width)
 
 
-def cholesky_step(data, row_count, allreduce, prev=None):
+def cholesky_step(data, row_count, allreduce, prev=None, precision=lax.Precision.HIGHEST):
     high = lax.Precision.HIGHEST
     partial_value = lax.dot_general(
         data, data, (((0,), (0,)), ((), ())), precision=high, preferred_element_type=jnp.float32
     )
     outs = chol_inv(allreduce(partial_value), row_count, prev)
     result = lax.dot_general(
-        data, outs[1], (((1,), (1,)), ((), ())), precision=lax.Precision.HIGH,
+        data, outs[1], (((1,), (1,)), ((), ())), precision=precision,
         preferred_element_type=jnp.float32,
     )
     return (result, outs[0] if prev is None else outs[2])
@@ -314,7 +314,7 @@
     blk = jac_blocks.shape[2]
     row_count = local_rows * lax.axis_size(("bulk", "span"))
     first, upper1 = cholesky_step(snapshots, row_count, make_allreduce(dims, 0))
-    modes, factor = cholesky_step(first, row_count, make_allreduce(dims, 1), upper1)
+    modes, factor = cholesky_step(first, row_count, make_allreduce(dims, 1), upper1, lax.Precision.HIGH)
     modes_b = modes.astype(jnp.bfloat16)
     jac_modes = jac_apply(lax.axis_size("bulk"), 3, jac_cols, modes_b, jac_blocks)
     partial_value = lax.dot_general(

time: 141 us -> 141 us (level)
  no operation moved by 1% of the time
where the time goes in v12:
time: 141 us
  Pallas kernels  125 us (89%)
  matrix products  11.2 us (8%)
  local copies, waits for them, and re-layouts  3.5 us (2%)
    pallas_call x3, Pallas kernels, allreduce(): pl.pallas_call(functools.partial(_allreduce_kernel, dims, scale), out_sha...  85.8 us
    pallas_call x2, Pallas kernels, chol_inv(): pl.pallas_call(functools.partial(_chol_kernel, float(count)), out_shape=(...  24.7 us
    pallas_call x1, Pallas kernels, jac_apply(): pl.pallas_call(functools.partial(_jac_kernel, nbulk), out_shape=jax.Shape...  14.8 us
    dot_general x2, matrix products, cholesky_step(): lax.dot_general(data, outs[1], (((1,), (1,)), ((), ())), precision=precis...  4.66 us
    dot_general x2, matrix products, cholesky_step(): lax.dot_general(data, data, (((0,), (0,)), ((), ())), precision=high, pre...  4.07 us
    unnamed x8, local copies, waits for them, and re-layouts  3.5 us

profile of v12, /device:TPU:1, one launch (start us, length us, event | category | flops | bytes accessed | tf_op | source)
XLA Modules:
  0.0 140.7 jit_solution(4363837488322485508)
XLA Ops:
  0.6 0.0 copy-start
  0.6 1.2 copy-done
  1.9 2.5 %fusion.1.x_ref = f32[128,128]{1,0:T(8,128)} fusion(f32[2048,128]{1,0:T(8,128)S(1)} %copy-done), kind=kOutput, calls=%fused_computation.1 | convolution fusion | flops 402653184 | bytes 1114112 | tf_op jit(solution)/shard_map/dot_general | solution.py:299
  4.3 35.5 %shard_map.66.g_ref = f32[128,128]{1,0:T(8,128)} custom-call(f32[128,128]{1,0:T(8,128)} %fusion.1.x_ref), custom_call_target="tpu_custom_call" | custom-call | tf_op jit(solution)/shard_map/pallas_call | solution.py:129
  39.9 12.3 %shard_map.67 = (f32[128,128]{1,0:T(8,128)}, f32[128,128]{1,0:T(8,128)}) custom-call(f32[128,128]{1,0:T(8,128)} %shard_map.66.g_ref), custom_call_target="tpu_custom_call" | custom-call | tf_op jit(solution)/shard_map/pallas_call | solution.py:197
  52.1 1.9 %fusion.2 = f32[128,2048]{1,0:T(8,128)S(1)} fusion(f32[128,128]{1,0:T(8,128)} %get-tuple-element.8, f32[2048,128]{1,0:T(8,128)S(1)} %copy-done), kind=kOutput, calls=%fused_computation.2 | convolution fusion | flops 402653184 | bytes 2162688 | tf_op jit(solution)/shard_map/dot_general | solution.py:303
  54.0 1.6 %fusion.3.x_ref = f32[128,128]{1,0:T(8,128)} fusion(f32[128,2048]{1,0:T(8,128)S(1)} %fusion.2), kind=kOutput, calls=%fused_computation.3 | convolution fusion | flops 402653184 | bytes 1114112 | tf_op jit(solution)/shard_map/dot_general | solution.py:299
  55.6 24.7 %shard_map.68.g_ref = f32[128,128]{1,0:T(8,128)} custom-call(f32[128,128]{1,0:T(8,128)} %fusion.3.x_ref), custom_call_target="tpu_custom_call" | custom-call | tf_op jit(solution)/shard_map/pallas_call | solution.py:129
  80.3 12.4 %shard_map.69 = (f32[128,128]{1,0:T(8,128)}, f32[128,128]{1,0:T(8,128)}, f32[128,128]{1,0:T(8,128)}) custom-call(f32[128,128]{1,0:T(8,128)} %shard_map.68.g_ref, f32[128,128]{1,0:T(8,128)} %get-tuple-element.9.refs_0_), custom_call_target="tpu_custom_call" | custom-call | tf_op jit(solution)/shard_map/pallas_call | solution.py:197
  92.7 2.8 %fusion = (bf16[2048,128]{1,0:T(8,128)(2,1)}, f32[2048,128]{1,0:T(8,128)S(1)}) fusion(f32[128,2048]{1,0:T(8,128)S(1)} %fusion.2, f32[128,128]{1,0:T(8,128)} %get-tuple-element.10), kind=kOutput, calls=%fused_computation | convolution fusion | flops 201588736 | bytes 2686976 | tf_op jit(solution)/shard_map/dot_general | solution.py:303
  95.6 0.0 copy-start.2
  95.6 14.8 %shard_map.70 = bf16[16,128,128]{2,1,0:T(8,128)(2,1)} custom-call(s32[4,16]{1,0:T(4,128)} %bitcast.16, bf16[16,128,128]{2,1,0:T(8,128)(2,1)} %bitcast.15, bf16[16,4,128,128]{3,2,1,0:T(8,128)(2,1)} %jac_ref.1), custom_call_target="tpu_custom_call" | custom-call | tf_op jit(solution)/shard_map/pallas_call | solution.py:278
  110.4 0.0 copy-start.1
  110.4 2.5 %fusion.4.x_ref = f32[128,128]{1,0:T(8,128)} fusion(f32[2048,128]{1,0:T(8,128)S(1)} %get-tuple-element.18, bf16[2048,128]{1,0:T(8,128)(2,1)} %bitcast.13), kind=kOutput, calls=%fused_computation.4 | convolution fusion | flops 201326592 | bytes 1638400 | tf_op jit(solution)/shard_map/dot_general | solution.py:320
  112.9 0.0 copy-done.2
  112.9 25.6 %shard_map.71 = f32[128,128]{1,0:T(8,128)} custom-call(f32[128,128]{1,0:T(8,128)} %fusion.4.x_ref), custom_call_target="tpu_custom_call" | custom-call | tf_op jit(solution)/shard_map/pallas_call | solution.py:129
  138.4 0.0 copy-done.1
  138.5 0.8 copy.9
  139.2 1.5 %copy.10 = f32[128,128]{1,0:T(8,128)} copy(f32[128,128]{1,0:T(8,128)} %shard_map.71) | data formatting | bytes 131072
Async XLA Ops:
  0.6 1.2 copy-start
  95.6 17.3 %copy-start.2 = (f32[2048,128]{1,0:T(8,128)}, f32[2048,128]{1,0:T(8,128)S(1)}, u32[]{:S(2)}) copy-start(f32[2048,128]{1,0:T(8,128)S(1)} %get-tuple-element.18) | copy-start | bytes 3145732
  110.4 28.0 %copy-start.1 = (bf16[16,128,128]{2,1,0:T(8,128)(2,1)S(1)}, bf16[16,128,128]{2,1,0:T(8,128)(2,1)}, u32[]{:S(2)}) copy-start(bf16[16,128,128]{2,1,0:T(8,128)(2,1)} %shard_map.70) | copy-start | bytes 1572868

commit v13 on v12

--- a/solution.py
+++ b/solution.py
@@ -38,12 +38,12 @@
     y_dev = lambda p: (b, p)
     o_core, o_x, o_z, o_y = 0, 2, 2 + nx, 2 + nx + nz
     o_gx = o_y + ny
-    o_gc = o_gx + nx
 
     barrier = pltpu.get_barrier_semaphore()
     peers = [partner]
     for n, pos, dev in ((nx, x, x_dev), (nz, z, z_dev), (ny, s, y_dev)):
         peers += [dev((pos + d) % n) for d in range(1, n)]
+    peers += [((((x + d) % nx) * nz + z) * 2 + 1 - core, s) for d in range(1, nx)]
     for peer in peers:
         pl.semaphore_signal(barrier, inc=1, device_id=peer, device_id_type=MESH)
     pl.semaphore_wait(barrier, len(peers))
@@ -93,34 +93,31 @@
         for k in range(1, n):
             acc = acc + slots[k]
 
-    row = lambda p: pl.multiple_of(core * half + p * chunk, chunk)
-    res[pl.ds(row(x), chunk), :] = acc
+    row = lambda c, p: pl.multiple_of(c * half + p * chunk, chunk)
+    both = lambda c, p: ((p * nz + z) * 2 + c, s)
+    res[pl.ds(row(core, x), chunk), :] = acc
     copies = []
-    for d in range(1, nx):
-        p = (x + d) % nx
-        cp = _remote(res.at[pl.ds(row(x), chunk)], res.at[pl.ds(row(x), chunk)],
-                     send_sem.at[o_gx + p], recv_sem.at[o_gx + x], x_dev(p))
-        cp.start()
-        copies.append(cp)
-    for d in range(1, nx):
-        j = (x + d) % nx
-        _remote(res.at[pl.ds(row(j), chunk)], res.at[pl.ds(row(j), chunk)],
-                send_sem.at[o_gx + j], recv_sem.at[o_gx + j], x_dev(j)).wait_recv()
-    for cp in copies:
-        cp.wait_send()
-
-    cp = _remote(res.at[pl.ds(mine, half)], res.at[pl.ds(mine, half)],
-                 send_sem.at[o_gc], recv_sem.at[o_gc + core], partner)
-    cp.start()
-    _remote(res.at[pl.ds(theirs, half)], res.at[pl.ds(theirs, half)],
-            send_sem.at[o_gc], recv_sem.at[o_gc + 1 - core], partner).wait_recv()
-    cp.wait_send()
+    for c2 in range(2):
+        for p in range(nx):
+            skip = jnp.logical_and(c2 == core, p == x)
+            cp = _remote(res.at[pl.ds(row(core, x), chunk)], res.at[pl.ds(row(core, x), chunk)],
+                         send_sem.at[o_gx + c2 * nx + p], recv_sem.at[o_gx + core * nx + x], both(c2, p))
+            pl.when(jnp.logical_not(skip))(cp.start)
+            copies.append((skip, cp))
+    for c2 in range(2):
+        for p in range(nx):
+            skip = jnp.logical_and(c2 == core, p == x)
+            cp = _remote(res.at[pl.ds(row(c2, p), chunk)], res.at[pl.ds(row(c2, p), chunk)],
+                         send_sem.at[o_gx + c2 * nx + p], recv_sem.at[o_gx + c2 * nx + p], both(c2, p))
+            pl.when(jnp.logical_not(skip))(cp.wait_recv)
+    for skip, cp in copies:
+        pl.when(jnp.logical_not(skip))(cp.wait_send)
     o_ref[...] = res[...] if scale == 1.0 else res[...] * scale
 
 
 def make_allreduce(dims, cid, scale=1.0):
     nx, nz, ny = dims
-    total = 2 + nx + nz + ny + nx + 2
+    total = 2 + nx + nz + ny + 2 * nx
 
     def allreduce(partial_value):
         rows, cols = partial_value.shape

time: 141 us -> 139 us (0.986)
  Pallas kernels: 125 us -> 123 us
    pallas_call x3, Pallas kernels: 85.8 us -> 83.1 us  [allreduce(): pl.pallas_call(functools.partial(_allreduce_kernel, dims, scale), out_sha...]
where the time goes in v13:
time: 139 us; the launch traced here: 138 us
  Pallas kernels  123 us (88%)
  matrix products  11 us (8%)
  local copies, waits for them, and re-layouts  3.5 us (3%)
    pallas_call x3, Pallas kernels, allreduce(): pl.pallas_call(functools.partial(_allreduce_kernel, dims, scale), out_sha...  83.1 us
    pallas_call x2, Pallas kernels, chol_inv(): pl.pallas_call(functools.partial(_chol_kernel, float(count)), out_shape=(...  24.8 us
    pallas_call x1, Pallas kernels, jac_apply(): pl.pallas_call(functools.partial(_jac_kernel, nbulk), out_shape=jax.Shape...  14.8 us
    dot_general x2, matrix products, cholesky_step(): lax.dot_general(data, outs[1], (((1,), (1,)), ((), ())), precision=precis...  4.49 us
    dot_general x2, matrix products, cholesky_step(): lax.dot_general(data, data, (((0,), (0,)), ((), ())), precision=high, pre...  4.07 us
    unnamed x8, local copies, waits for them, and re-layouts  3.5 us

profile of v13, /device:TPU:1, one launch (start us, length us, event | category | flops | bytes accessed | tf_op | source)
XLA Modules:
  0.0 138.0 jit_solution(4253396094464656854)
XLA Ops:
  0.6 0.0 copy-start
  0.6 1.2 copy-done
  1.9 2.5 %fusion.1.x_ref = f32[128,128]{1,0:T(8,128)} fusion(f32[2048,128]{1,0:T(8,128)S(1)} %copy-done), kind=kOutput, calls=%fused_computation.1 | convolution fusion | flops 402653184 | bytes 1114112 | tf_op jit(solution)/shard_map/dot_general | solution.py:296
  4.3 34.4 %shard_map.66.g_ref = f32[128,128]{1,0:T(8,128)} custom-call(f32[128,128]{1,0:T(8,128)} %fusion.1.x_ref), custom_call_target="tpu_custom_call" | custom-call | tf_op jit(solution)/shard_map/pallas_call | solution.py:126
  38.7 12.3 %shard_map.67 = (f32[128,128]{1,0:T(8,128)}, f32[128,128]{1,0:T(8,128)}) custom-call(f32[128,128]{1,0:T(8,128)} %shard_map.66.g_ref), custom_call_target="tpu_custom_call" | custom-call | tf_op jit(solution)/shard_map/pallas_call | solution.py:194
  51.0 1.9 %fusion.2 = f32[128,2048]{1,0:T(8,128)S(1)} fusion(f32[128,128]{1,0:T(8,128)} %get-tuple-element.8, f32[2048,128]{1,0:T(8,128)S(1)} %copy-done), kind=kOutput, calls=%fused_computation.2 | convolution fusion | flops 402653184 | bytes 2162688 | tf_op jit(solution)/shard_map/dot_general | solution.py:300
  52.9 1.6 %fusion.3.x_ref = f32[128,128]{1,0:T(8,128)} fusion(f32[128,2048]{1,0:T(8,128)S(1)} %fusion.2), kind=kOutput, calls=%fused_computation.3 | convolution fusion | flops 402653184 | bytes 1114112 | tf_op jit(solution)/shard_map/dot_general | solution.py:296
  54.5 23.9 %shard_map.68.g_ref = f32[128,128]{1,0:T(8,128)} custom-call(f32[128,128]{1,0:T(8,128)} %fusion.3.x_ref), custom_call_target="tpu_custom_call" | custom-call | tf_op jit(solution)/shard_map/pallas_call | solution.py:126
  78.4 12.6 %shard_map.69 = (f32[128,128]{1,0:T(8,128)}, f32[128,128]{1,0:T(8,128)}, f32[128,128]{1,0:T(8,128)}) custom-call(f32[128,128]{1,0:T(8,128)} %shard_map.68.g_ref, f32[128,128]{1,0:T(8,128)} %get-tuple-element.9.refs_0_), custom_call_target="tpu_custom_call" | custom-call | tf_op jit(solution)/shard_map/pallas_call | solution.py:194
  91.0 2.6 %fusion = (bf16[2048,128]{1,0:T(8,128)(2,1)}, f32[2048,128]{1,0:T(8,128)S(1)}) fusion(f32[128,2048]{1,0:T(8,128)S(1)} %fusion.2, f32[128,128]{1,0:T(8,128)} %get-tuple-element.10), kind=kOutput, calls=%fused_computation | convolution fusion | flops 201588736 | bytes 2686976 | tf_op jit(solution)/shard_map/dot_general | solution.py:300
  93.6 0.0 copy-start.2
  93.6 14.8 %shard_map.70 = bf16[16,128,128]{2,1,0:T(8,128)(2,1)} custom-call(s32[4,16]{1,0:T(4,128)} %bitcast.16, bf16[16,128,128]{2,1,0:T(8,128)(2,1)} %bitcast.15, bf16[16,4,128,128]{3,2,1,0:T(8,128)(2,1)} %jac_ref.1), custom_call_target="tpu_custom_call" | custom-call | tf_op jit(solution)/shard_map/pallas_call | solution.py:275
  108.4 0.0 copy-start.1
  108.4 2.5 %fusion.4.x_ref = f32[128,128]{1,0:T(8,128)} fusion(f32[2048,128]{1,0:T(8,128)S(1)} %get-tuple-element.18, bf16[2048,128]{1,0:T(8,128)(2,1)} %bitcast.13), kind=kOutput, calls=%fused_computation.4 | convolution fusion | flops 201326592 | bytes 1638400 | tf_op jit(solution)/shard_map/dot_general | solution.py:317
  110.9 0.0 copy-done.2
  110.9 24.8 %shard_map.71 = f32[128,128]{1,0:T(8,128)} custom-call(f32[128,128]{1,0:T(8,128)} %fusion.4.x_ref), custom_call_target="tpu_custom_call" | custom-call | tf_op jit(solution)/shard_map/pallas_call | solution.py:126
  135.7 0.0 copy-done.1
  135.8 0.8 copy.9
  136.6 1.5 %copy.10 = f32[128,128]{1,0:T(8,128)} copy(f32[128,128]{1,0:T(8,128)} %shard_map.71) | data formatting | bytes 131072
Async XLA Ops:
  0.6 1.2 copy-start
  93.6 17.3 %copy-start.2 = (f32[2048,128]{1,0:T(8,128)}, f32[2048,128]{1,0:T(8,128)S(1)}, u32[]{:S(2)}) copy-start(f32[2048,128]{1,0:T(8,128)S(1)} %get-tuple-element.18) | copy-start | bytes 3145732
  108.4 27.3 %copy-start.1 = (bf16[16,128,128]{2,1,0:T(8,128)(2,1)S(1)}, bf16[16,128,128]{2,1,0:T(8,128)(2,1)}, u32[]{:S(2)}) copy-start(bf16[16,128,128]{2,1,0:T(8,128)(2,1)} %shard_map.70) | copy-start | bytes 1572868

commit v14 on v13

--- a/solution.py
+++ b/solution.py
@@ -26,7 +26,7 @@
     )
 
 
-def _allreduce_kernel(dims, scale, x_ref, o_ref, s_core, s_x, s_z, s_y, res, send_sem, recv_sem):
+def _allreduce_kernel(dims, scale, x_ref, o_ref, s_x, s_z, s_y, res, send_sem, recv_sem):
     nx, nz, ny = dims
     b, s, core, x, z = _coords(nx, nz)
     rows = x_ref.shape[0]
@@ -36,7 +36,7 @@
     x_dev = lambda p: ((p * nz + z) * 2 + core, s)
     z_dev = lambda p: ((x * nz + p) * 2 + core, s)
     y_dev = lambda p: (b, p)
-    o_core, o_x, o_z, o_y = 0, 2, 2 + nx, 2 + nx + nz
+    o_x, o_z, o_y = 0, 2 * nx, 2 * nx + nz
     o_gx = o_y + ny
 
     barrier = pltpu.get_barrier_semaphore()
@@ -48,32 +48,28 @@
         pl.semaphore_signal(barrier, inc=1, device_id=peer, device_id_type=MESH)
     pl.semaphore_wait(barrier, len(peers))
 
-    mine = pl.multiple_of(core * half, half)
-    theirs = pl.multiple_of((1 - core) * half, half)
-    c_copy = _remote(x_ref.at[pl.ds(theirs, half)], s_core.at[core],
-                     send_sem.at[o_core], recv_sem.at[o_core + core], partner)
-    c_copy.start()
-    s_core[core] = x_ref[pl.ds(mine, half), :]
-    _remote(s_core.at[1 - core], s_core.at[1 - core], send_sem.at[o_core],
-            recv_sem.at[o_core + 1 - core], partner).wait_recv()
-    c_copy.wait_send()
-    s_core[core] = s_core[0] + s_core[1]
-
+    row = lambda c, p: pl.multiple_of(c * half + p * chunk, chunk)
+    both = lambda c, p: ((p * nz + z) * 2 + c, s)
+    me = core * nx + x
     copies = []
-    for d in range(1, nx):
-        p = (x + d) % nx
-        cp = _remote(s_core.at[core, pl.ds(pl.multiple_of(p * chunk, chunk), chunk)], s_x.at[x],
-                     send_sem.at[o_x + p], recv_sem.at[o_x + x], x_dev(p))
-        cp.start()
-        copies.append(cp)
-    s_x[x] = s_core[core, pl.ds(pl.multiple_of(x * chunk, chunk), chunk), :]
-    for d in range(1, nx):
-        j = (x + d) % nx
-        _remote(s_x.at[j], s_x.at[j], send_sem.at[o_x + j], recv_sem.at[o_x + j], x_dev(j)).wait_recv()
-    for cp in copies:
-        cp.wait_send()
+    for c2 in range(2):
+        for p in range(nx):
+            skip = jnp.logical_and(c2 == core, p == x)
+            cp = _remote(x_ref.at[pl.ds(row(c2, p), chunk)], s_x.at[me],
+                         send_sem.at[o_x + c2 * nx + p], recv_sem.at[o_x + me], both(c2, p))
+            pl.when(jnp.logical_not(skip))(cp.start)
+            copies.append((skip, cp))
+    s_x[me] = x_ref[pl.ds(row(core, x), chunk), :]
+    for c2 in range(2):
+        for p in range(nx):
+            skip = jnp.logical_and(c2 == core, p == x)
+            j = c2 * nx + p
+            cp = _remote(s_x.at[j], s_x.at[j], send_sem.at[o_x + j], recv_sem.at[o_x + j], both(c2, p))
+            pl.when(jnp.logical_not(skip))(cp.wait_recv)
+    for skip, cp in copies:
+        pl.when(jnp.logical_not(skip))(cp.wait_send)
     acc = s_x[0]
-    for k in range(1, nx):
+    for k in range(1, 2 * nx):
         acc = acc + s_x[k]
 
     for n, pos, dev, slots, off in ((nz, z, z_dev, s_z, o_z), (ny, s, y_dev, s_y, o_y)):
@@ -117,7 +113,7 @@
 
 def make_allreduce(dims, cid, scale=1.0):
     nx, nz, ny = dims
-    total = 2 + nx + nz + ny + 2 * nx
+    total = 2 * nx + nz + ny + 2 * nx
 
     def allreduce(partial_value):
         rows, cols = partial_value.shape
@@ -129,8 +125,7 @@
             in_specs=[pl.BlockSpec(memory_space=pltpu.VMEM)],
             out_specs=pl.BlockSpec(memory_space=pltpu.VMEM),
             scratch_shapes=[
-                pltpu.VMEM((2, half, cols), jnp.float32),
-                pltpu.VMEM((nx, chunk, cols), jnp.float32),
+                pltpu.VMEM((2 * nx, chunk, cols), jnp.float32),
                 pltpu.VMEM((nz, chunk, cols), jnp.float32),
                 pltpu.VMEM((ny, chunk, cols), jnp.float32),
                 pltpu.VMEM((rows, cols), jnp.float32),

time: 139 us -> 137 us (0.986)
  Pallas kernels: 123 us -> 121 us
    pallas_call x3, Pallas kernels: 83.1 us -> 81.3 us  [allreduce(): pl.pallas_call(functools.partial(_allreduce_kernel, dims, scale), out_sha...]
where the time goes in v14:
time: 137 us; the launch traced here: 136 us
  Pallas kernels  121 us (88%)
  matrix products  11 us (8%)
  local copies, waits for them, and re-layouts  3.5 us (3%)
    pallas_call x3, Pallas kernels, allreduce(): pl.pallas_call(functools.partial(_allreduce_kernel, dims, scale), out_sha...  81.3 us
    pallas_call x2, Pallas kernels, chol_inv(): pl.pallas_call(functools.partial(_chol_kernel, float(count)), out_shape=(...  24.8 us
    pallas_call x1, Pallas kernels, jac_apply(): pl.pallas_call(functools.partial(_jac_kernel, nbulk), out_shape=jax.Shape...  14.9 us
    dot_general x2, matrix products, cholesky_step(): lax.dot_general(data, outs[1], (((1,), (1,)), ((), ())), precision=precis...  4.49 us
    dot_general x2, matrix products, cholesky_step(): lax.dot_general(data, data, (((0,), (0,)), ((), ())), precision=high, pre...  4.07 us
    unnamed x8, local copies, waits for them, and re-layouts  3.5 us

profile of v14, /device:TPU:1, one launch (start us, length us, event | category | flops | bytes accessed | tf_op | source)
XLA Modules:
  0.0 136.3 jit_solution(9251634428499022714)
XLA Ops:
  0.6 0.0 copy-start
  0.6 1.2 copy-done
  1.9 2.5 %fusion.1.x_ref = f32[128,128]{1,0:T(8,128)} fusion(f32[2048,128]{1,0:T(8,128)S(1)} %copy-done), kind=kOutput, calls=%fused_computation.1 | convolution fusion | flops 402653184 | bytes 1114112 | tf_op jit(solution)/shard_map/dot_general | solution.py:291
  4.3 33.7 %shard_map.66.g_ref = f32[128,128]{1,0:T(8,128)} custom-call(f32[128,128]{1,0:T(8,128)} %fusion.1.x_ref), custom_call_target="tpu_custom_call" | custom-call | tf_op jit(solution)/shard_map/pallas_call | solution.py:122
  38.0 12.3 %shard_map.67 = (f32[128,128]{1,0:T(8,128)}, f32[128,128]{1,0:T(8,128)}) custom-call(f32[128,128]{1,0:T(8,128)} %shard_map.66.g_ref), custom_call_target="tpu_custom_call" | custom-call | tf_op jit(solution)/shard_map/pallas_call | solution.py:189
  50.3 1.9 %fusion.2 = f32[128,2048]{1,0:T(8,128)S(1)} fusion(f32[128,128]{1,0:T(8,128)} %get-tuple-element.8, f32[2048,128]{1,0:T(8,128)S(1)} %copy-done), kind=kOutput, calls=%fused_computation.2 | convolution fusion | flops 402653184 | bytes 2162688 | tf_op jit(solution)/shard_map/dot_general | solution.py:295
  52.2 1.6 %fusion.3.x_ref = f32[128,128]{1,0:T(8,128)} fusion(f32[128,2048]{1,0:T(8,128)S(1)} %fusion.2), kind=kOutput, calls=%fused_computation.3 | convolution fusion | flops 402653184 | bytes 1114112 | tf_op jit(solution)/shard_map/dot_general | solution.py:291
  53.8 23.2 %shard_map.68.g_ref = f32[128,128]{1,0:T(8,128)} custom-call(f32[128,128]{1,0:T(8,128)} %fusion.3.x_ref), custom_call_target="tpu_custom_call" | custom-call | tf_op jit(solution)/shard_map/pallas_call | solution.py:122
  77.0 12.6 %shard_map.69 = (f32[128,128]{1,0:T(8,128)}, f32[128,128]{1,0:T(8,128)}, f32[128,128]{1,0:T(8,128)}) custom-call(f32[128,128]{1,0:T(8,128)} %shard_map.68.g_ref, f32[128,128]{1,0:T(8,128)} %get-tuple-element.9.refs_0_), custom_call_target="tpu_custom_call" | custom-call | tf_op jit(solution)/shard_map/pallas_call | solution.py:189
  89.5 2.6 %fusion = (bf16[2048,128]{1,0:T(8,128)(2,1)}, f32[2048,128]{1,0:T(8,128)S(1)}) fusion(f32[128,2048]{1,0:T(8,128)S(1)} %fusion.2, f32[128,128]{1,0:T(8,128)} %get-tuple-element.10), kind=kOutput, calls=%fused_computation | convolution fusion | flops 201588736 | bytes 2686976 | tf_op jit(solution)/shard_map/dot_general | solution.py:295
  92.1 0.0 copy-start.2
  92.2 14.9 %shard_map.70 = bf16[16,128,128]{2,1,0:T(8,128)(2,1)} custom-call(s32[4,16]{1,0:T(4,128)} %bitcast.16, bf16[16,128,128]{2,1,0:T(8,128)(2,1)} %bitcast.15, bf16[16,4,128,128]{3,2,1,0:T(8,128)(2,1)} %jac_ref.1), custom_call_target="tpu_custom_call" | custom-call | tf_op jit(solution)/shard_map/pallas_call | solution.py:270
  107.1 0.0 copy-start.1
  107.1 2.5 %fusion.4.x_ref = f32[128,128]{1,0:T(8,128)} fusion(f32[2048,128]{1,0:T(8,128)S(1)} %get-tuple-element.18, bf16[2048,128]{1,0:T(8,128)(2,1)} %bitcast.13), kind=kOutput, calls=%fused_computation.4 | convolution fusion | flops 201326592 | bytes 1638400 | tf_op jit(solution)/shard_map/dot_general | solution.py:312
  109.6 0.0 copy-done.2
  109.6 24.4 %shard_map.71 = f32[128,128]{1,0:T(8,128)} custom-call(f32[128,128]{1,0:T(8,128)} %fusion.4.x_ref), custom_call_target="tpu_custom_call" | custom-call | tf_op jit(solution)/shard_map/pallas_call | solution.py:122
  134.0 0.0 copy-done.1
  134.0 0.8 copy.9
  134.8 1.5 %copy.10 = f32[128,128]{1,0:T(8,128)} copy(f32[128,128]{1,0:T(8,128)} %shard_map.71) | data formatting | bytes 131072
Async XLA Ops:
  0.6 1.2 copy-start
  92.1 17.4 %copy-start.2 = (f32[2048,128]{1,0:T(8,128)}, f32[2048,128]{1,0:T(8,128)S(1)}, u32[]{:S(2)}) copy-start(f32[2048,128]{1,0:T(8,128)S(1)} %get-tuple-element.18) | copy-start | bytes 3145732
  107.1 26.9 %copy-start.1 = (bf16[16,128,128]{2,1,0:T(8,128)(2,1)S(1)}, bf16[16,128,128]{2,1,0:T(8,128)(2,1)}, u32[]{:S(2)}) copy-start(bf16[16,128,128]{2,1,0:T(8,128)(2,1)} %shard_map.70) | copy-start | bytes 1572868

commit v15 on v14

--- a/solution.py
+++ b/solution.py
@@ -288,8 +288,10 @@
 
 def cholesky_step(data, row_count, allreduce, prev=None, precision=lax.Precision.HIGHEST):
     high = lax.Precision.HIGHEST
+    gram_precision = high if prev is None else precision
     partial_value = lax.dot_general(
-        data, data, (((0,), (0,)), ((), ())), precision=high, preferred_element_type=jnp.float32
+        data, data, (((0,), (0,)), ((), ())), precision=gram_precision,
+        preferred_element_type=jnp.float32,
     )
     outs = chol_inv(allreduce(partial_value), row_count, prev)
     result = lax.dot_general(

time: 137 us -> 136 us (level)
  no operation moved by 1% of the time
where the time goes in v15:
time: 136 us
  Pallas kernels  121 us (89%)
  matrix products  10.6 us (8%)
  local copies, waits for them, and re-layouts  3.5 us (3%)
    pallas_call x3, Pallas kernels, allreduce(): pl.pallas_call(functools.partial(_allreduce_kernel, dims, scale), out_sha...  81.3 us
    pallas_call x2, Pallas kernels, chol_inv(): pl.pallas_call(functools.partial(_chol_kernel, float(count)), out_shape=(...  24.7 us
    pallas_call x1, Pallas kernels, jac_apply(): pl.pallas_call(functools.partial(_jac_kernel, nbulk), out_shape=jax.Shape...  14.9 us
    dot_general x2, matrix products, cholesky_step(): lax.dot_general(data, outs[1], (((1,), (1,)), ((), ())), precision=precis...  4.49 us
    dot_general x2, matrix products, cholesky_step(): lax.dot_general(data, data, (((0,), (0,)), ((), ())), precision=gram_prec...  3.68 us
    unnamed x8, local copies, waits for them, and re-layouts  3.5 us

profile of v15, /device:TPU:1, one launch (start us, length us, event | category | flops | bytes accessed | tf_op | source)
XLA Modules:
  0.0 135.8 jit_solution(9175440517201546926)
XLA Ops:
  0.6 0.0 copy-start
  0.6 1.2 copy-done
  1.9 2.5 %fusion.1.x_ref = f32[128,128]{1,0:T(8,128)} fusion(f32[2048,128]{1,0:T(8,128)S(1)} %copy-done), kind=kOutput, calls=%fused_computation.1 | convolution fusion | flops 402653184 | bytes 1114112 | tf_op jit(solution)/shard_map/dot_general | solution.py:292
  4.3 33.7 %shard_map.66.g_ref = f32[128,128]{1,0:T(8,128)} custom-call(f32[128,128]{1,0:T(8,128)} %fusion.1.x_ref), custom_call_target="tpu_custom_call" | custom-call | tf_op jit(solution)/shard_map/pallas_call | solution.py:122
  38.0 12.3 %shard_map.67 = (f32[128,128]{1,0:T(8,128)}, f32[128,128]{1,0:T(8,128)}) custom-call(f32[128,128]{1,0:T(8,128)} %shard_map.66.g_ref), custom_call_target="tpu_custom_call" | custom-call | tf_op jit(solution)/shard_map/pallas_call | solution.py:189
  50.3 1.9 %fusion.2 = f32[128,2048]{1,0:T(8,128)S(1)} fusion(f32[128,128]{1,0:T(8,128)} %get-tuple-element.8, f32[2048,128]{1,0:T(8,128)S(1)} %copy-done), kind=kOutput, calls=%fused_computation.2 | convolution fusion | flops 402653184 | bytes 2162688 | tf_op jit(solution)/shard_map/dot_general | solution.py:297
  52.2 1.2 fusion.3.x_ref
  53.4 23.2 %shard_map.68.g_ref = f32[128,128]{1,0:T(8,128)} custom-call(f32[128,128]{1,0:T(8,128)} %fusion.3.x_ref), custom_call_target="tpu_custom_call" | custom-call | tf_op jit(solution)/shard_map/pallas_call | solution.py:122
  76.6 12.4 %shard_map.69 = (f32[128,128]{1,0:T(8,128)}, f32[128,128]{1,0:T(8,128)}, f32[128,128]{1,0:T(8,128)}) custom-call(f32[128,128]{1,0:T(8,128)} %shard_map.68.g_ref, f32[128,128]{1,0:T(8,128)} %get-tuple-element.9.refs_0_), custom_call_target="tpu_custom_call" | custom-call | tf_op jit(solution)/shard_map/pallas_call | solution.py:189
  89.0 2.6 %fusion = (bf16[2048,128]{1,0:T(8,128)(2,1)}, f32[2048,128]{1,0:T(8,128)S(1)}) fusion(f32[128,2048]{1,0:T(8,128)S(1)} %fusion.2, f32[128,128]{1,0:T(8,128)} %get-tuple-element.10), kind=kOutput, calls=%fused_computation | convolution fusion | flops 201588736 | bytes 2686976 | tf_op jit(solution)/shard_map/dot_general | solution.py:297
  91.7 0.0 copy-start.2
  91.7 14.9 %shard_map.70 = bf16[16,128,128]{2,1,0:T(8,128)(2,1)} custom-call(s32[4,16]{1,0:T(4,128)} %bitcast.16, bf16[16,128,128]{2,1,0:T(8,128)(2,1)} %bitcast.15, bf16[16,4,128,128]{3,2,1,0:T(8,128)(2,1)} %jac_ref.1), custom_call_target="tpu_custom_call" | custom-call | tf_op jit(solution)/shard_map/pallas_call | solution.py:270
  106.6 0.0 copy-start.1
  106.6 2.5 %fusion.4.x_ref = f32[128,128]{1,0:T(8,128)} fusion(f32[2048,128]{1,0:T(8,128)S(1)} %get-tuple-element.18, bf16[2048,128]{1,0:T(8,128)(2,1)} %bitcast.13), kind=kOutput, calls=%fused_computation.4 | convolution fusion | flops 201326592 | bytes 1638400 | tf_op jit(solution)/shard_map/dot_general | solution.py:314
  109.1 0.0 copy-done.2
  109.1 24.4 %shard_map.71 = f32[128,128]{1,0:T(8,128)} custom-call(f32[128,128]{1,0:T(8,128)} %fusion.4.x_ref), custom_call_target="tpu_custom_call" | custom-call | tf_op jit(solution)/shard_map/pallas_call | solution.py:122
  133.5 0.0 copy-done.1
  133.5 0.8 copy.9
  134.3 1.5 %copy.10 = f32[128,128]{1,0:T(8,128)} copy(f32[128,128]{1,0:T(8,128)} %shard_map.71) | data formatting | bytes 131072
Async XLA Ops:
  0.6 1.2 copy-start
  91.7 17.4 %copy-start.2 = (f32[2048,128]{1,0:T(8,128)}, f32[2048,128]{1,0:T(8,128)S(1)}, u32[]{:S(2)}) copy-start(f32[2048,128]{1,0:T(8,128)S(1)} %get-tuple-element.18) | copy-start | bytes 3145732
  106.6 26.9 %copy-start.1 = (bf16[16,128,128]{2,1,0:T(8,128)(2,1)S(1)}, bf16[16,128,128]{2,1,0:T(8,128)(2,1)}, u32[]{:S(2)}) copy-start(bf16[16,128,128]{2,1,0:T(8,128)(2,1)} %shard_map.70) | copy-start | bytes 1572868

commit v16 on v15

--- a/solution.py
+++ b/solution.py
@@ -194,7 +194,7 @@
     )(g, *(() if prev is None else (prev,)))
 
 
-def _jac_kernel(nbulk, cols_hbm, modes_ref, jac_ref, out_ref, ext, cols_ref, cols_sem, send_sem, recv_sem):
+def _jac_kernel(nbulk, cols_hbm, modes_ref, jac_ref, out_ref, ext, acc_ref, cols_ref, cols_sem, send_sem, recv_sem):
     cols_copy = pltpu.make_async_copy(cols_hbm, cols_ref, cols_sem)
     cols_copy.start()
     b = lax.axis_index("bulk")
@@ -239,6 +239,12 @@
     def _():
         ext[pl.ds(2 * rb, rb)] = jnp.zeros(modes_ref.shape, modes_ref.dtype)
 
+    def own(r, carry):
+        acc_ref[r] = jnp.dot(jac_ref[r, 0], modes_ref[r], preferred_element_type=jnp.float32)
+        return carry
+
+    lax.fori_loop(0, rb, own, 0)
+
     @pl.when(has_left)
     def _():
         to_right.wait_recv()
@@ -253,11 +259,11 @@
     start = (s * nbulk + b) * rb - rb
 
     def row(r, carry):
-        acc = None
-        for n in range(jac_ref.shape[1]):
+        acc = acc_ref[r]
+        for n in range(1, jac_ref.shape[1]):
             idx = jnp.clip(cols_ref[n, r] - start, 0, 3 * rb - 1)
             term = jnp.dot(jac_ref[r, n], ext[idx], preferred_element_type=jnp.float32)
-            acc = term if acc is None else acc + term
+            acc = acc + term
         out_ref[r] = acc.astype(out_ref.dtype)
         return carry
 
@@ -276,6 +282,7 @@
         out_specs=pl.BlockSpec(memory_space=pltpu.VMEM),
         scratch_shapes=[
             pltpu.VMEM((3 * rb, blk, width), jnp.bfloat16),
+            pltpu.VMEM((rb, blk, width), jnp.float32),
             pltpu.SMEM(jac_cols.shape[::-1], jnp.int32),
             pltpu.SemaphoreType.DMA(()),
             pltpu.SemaphoreType.DMA((2,)),

time: 136 us -> 136 us (level)
  no operation moved by 1% of the time
where the time goes in v16:
time: 136 us
  Pallas kernels  121 us (89%)
  matrix products  10.8 us (8%)
  local copies, waits for them, and re-layouts  3.5 us (3%)
    pallas_call x3, Pallas kernels, allreduce(): pl.pallas_call(functools.partial(_allreduce_kernel, dims, scale), out_sha...  81.3 us
    pallas_call x2, Pallas kernels, chol_inv(): pl.pallas_call(functools.partial(_chol_kernel, float(count)), out_shape=(...  24.7 us
    pallas_call x1, Pallas kernels, jac_apply(): pl.pallas_call(functools.partial(_jac_kernel, nbulk), out_shape=jax.Shape...  14.8 us
    dot_general x2, matrix products, cholesky_step(): lax.dot_general(data, outs[1], (((1,), (1,)), ((), ())), precision=precis...  4.66 us
    dot_general x2, matrix products, cholesky_step(): lax.dot_general(data, data, (((0,), (0,)), ((), ())), precision=gram_prec...  3.68 us
    unnamed x8, local copies, waits for them, and re-layouts  3.5 us

profile of v16, /device:TPU:1, one launch (start us, length us, event | category | flops | bytes accessed | tf_op | source)
XLA Modules:
  0.0 135.8 jit_solution(3438615116038917375)
XLA Ops:
  0.6 0.0 copy-start
  0.6 1.2 copy-done
  1.9 2.5 %fusion.1.x_ref = f32[128,128]{1,0:T(8,128)} fusion(f32[2048,128]{1,0:T(8,128)S(1)} %copy-done), kind=kOutput, calls=%fused_computation.1 | convolution fusion | flops 402653184 | bytes 1114112 | tf_op jit(solution)/shard_map/dot_general | solution.py:299
  4.3 33.7 %shard_map.66.g_ref = f32[128,128]{1,0:T(8,128)} custom-call(f32[128,128]{1,0:T(8,128)} %fusion.1.x_ref), custom_call_target="tpu_custom_call" | custom-call | tf_op jit(solution)/shard_map/pallas_call | solution.py:122
  38.0 12.3 %shard_map.67 = (f32[128,128]{1,0:T(8,128)}, f32[128,128]{1,0:T(8,128)}) custom-call(f32[128,128]{1,0:T(8,128)} %shard_map.66.g_ref), custom_call_target="tpu_custom_call" | custom-call | tf_op jit(solution)/shard_map/pallas_call | solution.py:189
  50.3 1.9 %fusion.2 = f32[128,2048]{1,0:T(8,128)S(1)} fusion(f32[128,128]{1,0:T(8,128)} %get-tuple-element.8, f32[2048,128]{1,0:T(8,128)S(1)} %copy-done), kind=kOutput, calls=%fused_computation.2 | convolution fusion | flops 402653184 | bytes 2162688 | tf_op jit(solution)/shard_map/dot_general | solution.py:304
  52.2 1.2 fusion.3.x_ref
  53.4 23.2 %shard_map.68.g_ref = f32[128,128]{1,0:T(8,128)} custom-call(f32[128,128]{1,0:T(8,128)} %fusion.3.x_ref), custom_call_target="tpu_custom_call" | custom-call | tf_op jit(solution)/shard_map/pallas_call | solution.py:122
  76.6 12.4 %shard_map.69 = (f32[128,128]{1,0:T(8,128)}, f32[128,128]{1,0:T(8,128)}, f32[128,128]{1,0:T(8,128)}) custom-call(f32[128,128]{1,0:T(8,128)} %shard_map.68.g_ref, f32[128,128]{1,0:T(8,128)} %get-tuple-element.9.refs_0_), custom_call_target="tpu_custom_call" | custom-call | tf_op jit(solution)/shard_map/pallas_call | solution.py:189
  89.0 2.8 %fusion = (bf16[2048,128]{1,0:T(8,128)(2,1)}, f32[2048,128]{1,0:T(8,128)S(1)}) fusion(f32[128,2048]{1,0:T(8,128)S(1)} %fusion.2, f32[128,128]{1,0:T(8,128)} %get-tuple-element.10), kind=kOutput, calls=%fused_computation | convolution fusion | flops 201588736 | bytes 2686976 | tf_op jit(solution)/shard_map/dot_general | solution.py:304
  91.8 0.0 copy-start.2
  91.8 14.8 %shard_map.70 = bf16[16,128,128]{2,1,0:T(8,128)(2,1)} custom-call(s32[4,16]{1,0:T(4,128)} %bitcast.16, bf16[16,128,128]{2,1,0:T(8,128)(2,1)} %bitcast.15, bf16[16,4,128,128]{3,2,1,0:T(8,128)(2,1)} %jac_ref.1), custom_call_target="tpu_custom_call" | custom-call | tf_op jit(solution)/shard_map/pallas_call | solution.py:276
  106.6 0.0 copy-start.1
  106.6 2.5 %fusion.4.x_ref = f32[128,128]{1,0:T(8,128)} fusion(f32[2048,128]{1,0:T(8,128)S(1)} %get-tuple-element.18, bf16[2048,128]{1,0:T(8,128)(2,1)} %bitcast.13), kind=kOutput, calls=%fused_computation.4 | convolution fusion | flops 201326592 | bytes 1638400 | tf_op jit(solution)/shard_map/dot_general | solution.py:321
  109.1 0.0 copy-done.2
  109.1 24.4 %shard_map.71 = f32[128,128]{1,0:T(8,128)} custom-call(f32[128,128]{1,0:T(8,128)} %fusion.4.x_ref), custom_call_target="tpu_custom_call" | custom-call | tf_op jit(solution)/shard_map/pallas_call | solution.py:122
  133.5 0.0 copy-done.1
  133.5 0.8 copy.9
  134.3 1.5 %copy.10 = f32[128,128]{1,0:T(8,128)} copy(f32[128,128]{1,0:T(8,128)} %shard_map.71) | data formatting | bytes 131072
Async XLA Ops:
  0.6 1.2 copy-start
  91.8 17.3 %copy-start.2 = (f32[2048,128]{1,0:T(8,128)}, f32[2048,128]{1,0:T(8,128)S(1)}, u32[]{:S(2)}) copy-start(f32[2048,128]{1,0:T(8,128)S(1)} %get-tuple-element.18) | copy-start | bytes 3145732
  106.6 26.9 %copy-start.1 = (bf16[16,128,128]{2,1,0:T(8,128)(2,1)S(1)}, bf16[16,128,128]{2,1,0:T(8,128)(2,1)}, u32[]{:S(2)}) copy-start(bf16[16,128,128]{2,1,0:T(8,128)(2,1)} %shard_map.70) | copy-start | bytes 1572868

commit v17 on v15

--- a/solution.py
+++ b/solution.py
@@ -66,8 +66,7 @@
             j = c2 * nx + p
             cp = _remote(s_x.at[j], s_x.at[j], send_sem.at[o_x + j], recv_sem.at[o_x + j], both(c2, p))
             pl.when(jnp.logical_not(skip))(cp.wait_recv)
-    for skip, cp in copies:
-        pl.when(jnp.logical_not(skip))(cp.wait_send)
+    pending = list(copies)
     acc = s_x[0]
     for k in range(1, 2 * nx):
         acc = acc + s_x[k]
@@ -83,8 +82,7 @@
         for d in range(1, n):
             j = (pos + d) % n
             _remote(slots.at[j], slots.at[j], send_sem.at[off + j], recv_sem.at[off + j], dev(j)).wait_recv()
-        for cp in copies:
-            cp.wait_send()
+        pending += [(False, cp) for cp in copies]
         acc = slots[0]
         for k in range(1, n):
             acc = acc + slots[k]
@@ -106,7 +104,7 @@
             cp = _remote(res.at[pl.ds(row(c2, p), chunk)], res.at[pl.ds(row(c2, p), chunk)],
                          send_sem.at[o_gx + c2 * nx + p], recv_sem.at[o_gx + c2 * nx + p], both(c2, p))
             pl.when(jnp.logical_not(skip))(cp.wait_recv)
-    for skip, cp in copies:
+    for skip, cp in pending + copies:
         pl.when(jnp.logical_not(skip))(cp.wait_send)
     o_ref[...] = res[...] if scale == 1.0 else res[...] * scale
 

time: 136 us -> 137 us (level)
  no operation moved by 1% of the time
where the time goes in v17:
time: 137 us; the launch traced here: 136 us
  Pallas kernels  121 us (88%)
  matrix products  10.8 us (8%)
  local copies, waits for them, and re-layouts  3.5 us (3%)
    pallas_call x3, Pallas kernels, allreduce(): pl.pallas_call(functools.partial(_allreduce_kernel, dims, scale), out_sha...  81.3 us
    pallas_call x2, Pallas kernels, chol_inv(): pl.pallas_call(functools.partial(_chol_kernel, float(count)), out_shape=(...  24.7 us
    pallas_call x1, Pallas kernels, jac_apply(): pl.pallas_call(functools.partial(_jac_kernel, nbulk), out_shape=jax.Shape...  14.9 us
    dot_general x2, matrix products, cholesky_step(): lax.dot_general(data, outs[1], (((1,), (1,)), ((), ())), precision=precis...  4.66 us
    dot_general x2, matrix products, cholesky_step(): lax.dot_general(data, data, (((0,), (0,)), ((), ())), precision=gram_prec...  3.68 us
    unnamed x8, local copies, waits for them, and re-layouts  3.5 us

profile of v17, /device:TPU:1, one launch (start us, length us, event | category | flops | bytes accessed | tf_op | source)
XLA Modules:
  0.0 135.9 jit_solution(12790564027733050313)
XLA Ops:
  0.6 0.0 copy-start
  0.6 1.2 copy-done
  1.9 2.5 %fusion.1.x_ref = f32[128,128]{1,0:T(8,128)} fusion(f32[2048,128]{1,0:T(8,128)S(1)} %copy-done), kind=kOutput, calls=%fused_computation.1 | convolution fusion | flops 402653184 | bytes 1114112 | tf_op jit(solution)/shard_map/dot_general | solution.py:290
  4.3 33.7 %shard_map.66.g_ref = f32[128,128]{1,0:T(8,128)} custom-call(f32[128,128]{1,0:T(8,128)} %fusion.1.x_ref), custom_call_target="tpu_custom_call" | custom-call | tf_op jit(solution)/shard_map/pallas_call | solution.py:120
  38.0 12.3 %shard_map.67 = (f32[128,128]{1,0:T(8,128)}, f32[128,128]{1,0:T(8,128)}) custom-call(f32[128,128]{1,0:T(8,128)} %shard_map.66.g_ref), custom_call_target="tpu_custom_call" | custom-call | tf_op jit(solution)/shard_map/pallas_call | solution.py:187
  50.3 1.9 %fusion.2 = f32[128,2048]{1,0:T(8,128)S(1)} fusion(f32[128,128]{1,0:T(8,128)} %get-tuple-element.8, f32[2048,128]{1,0:T(8,128)S(1)} %copy-done), kind=kOutput, calls=%fused_computation.2 | convolution fusion | flops 402653184 | bytes 2162688 | tf_op jit(solution)/shard_map/dot_general | solution.py:295
  52.2 1.2 fusion.3.x_ref
  53.4 23.2 %shard_map.68.g_ref = f32[128,128]{1,0:T(8,128)} custom-call(f32[128,128]{1,0:T(8,128)} %fusion.3.x_ref), custom_call_target="tpu_custom_call" | custom-call | tf_op jit(solution)/shard_map/pallas_call | solution.py:120
  76.6 12.4 %shard_map.69 = (f32[128,128]{1,0:T(8,128)}, f32[128,128]{1,0:T(8,128)}, f32[128,128]{1,0:T(8,128)}) custom-call(f32[128,128]{1,0:T(8,128)} %shard_map.68.g_ref, f32[128,128]{1,0:T(8,128)} %get-tuple-element.9.refs_0_), custom_call_target="tpu_custom_call" | custom-call | tf_op jit(solution)/shard_map/pallas_call | solution.py:187
  89.0 2.8 %fusion = (bf16[2048,128]{1,0:T(8,128)(2,1)}, f32[2048,128]{1,0:T(8,128)S(1)}) fusion(f32[128,2048]{1,0:T(8,128)S(1)} %fusion.2, f32[128,128]{1,0:T(8,128)} %get-tuple-element.10), kind=kOutput, calls=%fused_computation | convolution fusion | flops 201588736 | bytes 2686976 | tf_op jit(solution)/shard_map/dot_general | solution.py:295
  91.8 0.0 copy-start.2
  91.8 14.9 %shard_map.70 = bf16[16,128,128]{2,1,0:T(8,128)(2,1)} custom-call(s32[4,16]{1,0:T(4,128)} %bitcast.16, bf16[16,128,128]{2,1,0:T(8,128)(2,1)} %bitcast.15, bf16[16,4,128,128]{3,2,1,0:T(8,128)(2,1)} %jac_ref.1), custom_call_target="tpu_custom_call" | custom-call | tf_op jit(solution)/shard_map/pallas_call | solution.py:268
  106.8 0.0 copy-start.1
  106.8 2.5 %fusion.4.x_ref = f32[128,128]{1,0:T(8,128)} fusion(f32[2048,128]{1,0:T(8,128)S(1)} %get-tuple-element.18, bf16[2048,128]{1,0:T(8,128)(2,1)} %bitcast.13), kind=kOutput, calls=%fused_computation.4 | convolution fusion | flops 201326592 | bytes 1638400 | tf_op jit(solution)/shard_map/dot_general | solution.py:312
  109.2 0.0 copy-done.2
  109.2 24.4 %shard_map.71 = f32[128,128]{1,0:T(8,128)} custom-call(f32[128,128]{1,0:T(8,128)} %fusion.4.x_ref), custom_call_target="tpu_custom_call" | custom-call | tf_op jit(solution)/shard_map/pallas_call | solution.py:120
  133.6 0.0 copy-done.1
  133.6 0.8 copy.9
  134.4 1.5 %copy.10 = f32[128,128]{1,0:T(8,128)} copy(f32[128,128]{1,0:T(8,128)} %shard_map.71) | data formatting | bytes 131072
Async XLA Ops:
  0.6 1.2 copy-start
  91.8 17.4 %copy-start.2 = (f32[2048,128]{1,0:T(8,128)}, f32[2048,128]{1,0:T(8,128)S(1)}, u32[]{:S(2)}) copy-start(f32[2048,128]{1,0:T(8,128)S(1)} %get-tuple-element.18) | copy-start | bytes 3145732
  106.8 26.8 %copy-start.1 = (bf16[16,128,128]{2,1,0:T(8,128)(2,1)S(1)}, bf16[16,128,128]{2,1,0:T(8,128)(2,1)}, u32[]{:S(2)}) copy-start(bf16[16,128,128]{2,1,0:T(8,128)(2,1)} %shard_map.70) | copy-start | bytes 1572868

commit v18 on v16

--- a/solution.py
+++ b/solution.py
@@ -66,8 +66,7 @@
             j = c2 * nx + p
             cp = _remote(s_x.at[j], s_x.at[j], send_sem.at[o_x + j], recv_sem.at[o_x + j], both(c2, p))
             pl.when(jnp.logical_not(skip))(cp.wait_recv)
-    for skip, cp in copies:
-        pl.when(jnp.logical_not(skip))(cp.wait_send)
+    pending = list(copies)
     acc = s_x[0]
     for k in range(1, 2 * nx):
         acc = acc + s_x[k]
@@ -83,8 +82,7 @@
         for d in range(1, n):
             j = (pos + d) % n
             _remote(slots.at[j], slots.at[j], send_sem.at[off + j], recv_sem.at[off + j], dev(j)).wait_recv()
-        for cp in copies:
-            cp.wait_send()
+        pending += [(False, cp) for cp in copies]
         acc = slots[0]
         for k in range(1, n):
             acc = acc + slots[k]
@@ -106,7 +104,7 @@
             cp = _remote(res.at[pl.ds(row(c2, p), chunk)], res.at[pl.ds(row(c2, p), chunk)],
                          send_sem.at[o_gx + c2 * nx + p], recv_sem.at[o_gx + c2 * nx + p], both(c2, p))
             pl.when(jnp.logical_not(skip))(cp.wait_recv)
-    for skip, cp in copies:
+    for skip, cp in pending + copies:
         pl.when(jnp.logical_not(skip))(cp.wait_send)
     o_ref[...] = res[...] if scale == 1.0 else res[...] * scale
 

time: 136 us -> 136 us (level)
  no operation moved by 1% of the time
where the time goes in v18:
time: 136 us
  Pallas kernels  121 us (89%)
  matrix products  10.8 us (8%)
  local copies, waits for them, and re-layouts  3.5 us (3%)
    pallas_call x3, Pallas kernels, allreduce(): pl.pallas_call(functools.partial(_allreduce_kernel, dims, scale), out_sha...  81.3 us
    pallas_call x2, Pallas kernels, chol_inv(): pl.pallas_call(functools.partial(_chol_kernel, float(count)), out_shape=(...  24.7 us
    pallas_call x1, Pallas kernels, jac_apply(): pl.pallas_call(functools.partial(_jac_kernel, nbulk), out_shape=jax.Shape...  14.8 us
    dot_general x2, matrix products, cholesky_step(): lax.dot_general(data, outs[1], (((1,), (1,)), ((), ())), precision=precis...  4.66 us
    dot_general x2, matrix products, cholesky_step(): lax.dot_general(data, data, (((0,), (0,)), ((), ())), precision=gram_prec...  3.68 us
    unnamed x8, local copies, waits for them, and re-layouts  3.5 us

profile of v18, /device:TPU:1, one launch (start us, length us, event | category | flops | bytes accessed | tf_op | source)
XLA Modules:
  0.0 135.8 jit_solution(6196855470989120875)
XLA Ops:
  0.6 0.0 copy-start
  0.6 1.2 copy-done
  1.9 2.5 %fusion.1.x_ref = f32[128,128]{1,0:T(8,128)} fusion(f32[2048,128]{1,0:T(8,128)S(1)} %copy-done), kind=kOutput, calls=%fused_computation.1 | convolution fusion | flops 402653184 | bytes 1114112 | tf_op jit(solution)/shard_map/dot_general | solution.py:297
  4.3 33.7 %shard_map.66.g_ref = f32[128,128]{1,0:T(8,128)} custom-call(f32[128,128]{1,0:T(8,128)} %fusion.1.x_ref), custom_call_target="tpu_custom_call" | custom-call | tf_op jit(solution)/shard_map/pallas_call | solution.py:120
  38.0 12.3 %shard_map.67 = (f32[128,128]{1,0:T(8,128)}, f32[128,128]{1,0:T(8,128)}) custom-call(f32[128,128]{1,0:T(8,128)} %shard_map.66.g_ref), custom_call_target="tpu_custom_call" | custom-call | tf_op jit(solution)/shard_map/pallas_call | solution.py:187
  50.3 1.9 %fusion.2 = f32[128,2048]{1,0:T(8,128)S(1)} fusion(f32[128,128]{1,0:T(8,128)} %get-tuple-element.8, f32[2048,128]{1,0:T(8,128)S(1)} %copy-done), kind=kOutput, calls=%fused_computation.2 | convolution fusion | flops 402653184 | bytes 2162688 | tf_op jit(solution)/shard_map/dot_general | solution.py:302
  52.2 1.2 fusion.3.x_ref
  53.4 23.2 %shard_map.68.g_ref = f32[128,128]{1,0:T(8,128)} custom-call(f32[128,128]{1,0:T(8,128)} %fusion.3.x_ref), custom_call_target="tpu_custom_call" | custom-call | tf_op jit(solution)/shard_map/pallas_call | solution.py:120
  76.6 12.4 %shard_map.69 = (f32[128,128]{1,0:T(8,128)}, f32[128,128]{1,0:T(8,128)}, f32[128,128]{1,0:T(8,128)}) custom-call(f32[128,128]{1,0:T(8,128)} %shard_map.68.g_ref, f32[128,128]{1,0:T(8,128)} %get-tuple-element.9.refs_0_), custom_call_target="tpu_custom_call" | custom-call | tf_op jit(solution)/shard_map/pallas_call | solution.py:187
  89.0 2.8 %fusion = (bf16[2048,128]{1,0:T(8,128)(2,1)}, f32[2048,128]{1,0:T(8,128)S(1)}) fusion(f32[128,2048]{1,0:T(8,128)S(1)} %fusion.2, f32[128,128]{1,0:T(8,128)} %get-tuple-element.10), kind=kOutput, calls=%fused_computation | convolution fusion | flops 201588736 | bytes 2686976 | tf_op jit(solution)/shard_map/dot_general | solution.py:302
  91.8 0.0 copy-start.2
  91.8 14.8 %shard_map.70 = bf16[16,128,128]{2,1,0:T(8,128)(2,1)} custom-call(s32[4,16]{1,0:T(4,128)} %bitcast.16, bf16[16,128,128]{2,1,0:T(8,128)(2,1)} %bitcast.15, bf16[16,4,128,128]{3,2,1,0:T(8,128)(2,1)} %jac_ref.1), custom_call_target="tpu_custom_call" | custom-call | tf_op jit(solution)/shard_map/pallas_call | solution.py:274
  106.6 0.0 copy-start.1
  106.6 2.5 %fusion.4.x_ref = f32[128,128]{1,0:T(8,128)} fusion(f32[2048,128]{1,0:T(8,128)S(1)} %get-tuple-element.18, bf16[2048,128]{1,0:T(8,128)(2,1)} %bitcast.13), kind=kOutput, calls=%fused_computation.4 | convolution fusion | flops 201326592 | bytes 1638400 | tf_op jit(solution)/shard_map/dot_general | solution.py:319
  109.1 0.0 copy-done.2
  109.1 24.4 %shard_map.71 = f32[128,128]{1,0:T(8,128)} custom-call(f32[128,128]{1,0:T(8,128)} %fusion.4.x_ref), custom_call_target="tpu_custom_call" | custom-call | tf_op jit(solution)/shard_map/pallas_call | solution.py:120
  133.5 0.0 copy-done.1
  133.5 0.8 copy.9
  134.3 1.5 %copy.10 = f32[128,128]{1,0:T(8,128)} copy(f32[128,128]{1,0:T(8,128)} %shard_map.71) | data formatting | bytes 131072
Async XLA Ops:
  0.6 1.2 copy-start
  91.8 17.3 %copy-start.2 = (f32[2048,128]{1,0:T(8,128)}, f32[2048,128]{1,0:T(8,128)S(1)}, u32[]{:S(2)}) copy-start(f32[2048,128]{1,0:T(8,128)S(1)} %get-tuple-element.18) | copy-start | bytes 3145732
  106.6 26.8 %copy-start.1 = (bf16[16,128,128]{2,1,0:T(8,128)(2,1)S(1)}, bf16[16,128,128]{2,1,0:T(8,128)(2,1)}, u32[]{:S(2)}) copy-start(bf16[16,128,128]{2,1,0:T(8,128)(2,1)} %shard_map.70) | copy-start | bytes 1572868
